TPU v7x, 32 devices: a whole 2x2x4 slice. The times are simulated.
32 devices in a mesh: slab: 16 (over z, x, core), cross: 2 (over y).
Axes of the slice: x: 2, y: 2, z: 4, core: 2. Of those that a mesh axis runs over, the one named last changes fastest.
Arguments:
- sim_field: float32 [4, 1536, 4096], P(None, 'slab', 'cross'), may hold values from -6 to 6
- brick_edges: int32 [16, 2], P('slab'), may hold values from 0 to 1025, as said below
- cell_width: float32 [1024], P('slab'), may hold values from 0.5 to 2
Outputs:
- tile_detail: float32 [4, 960, 4096], P(None, 'slab', 'cross')
- tree_detail: float32 [4, 64, 4096], P(None, 'slab', 'cross')
- coarse_final: float32 [4, 5, 4096], P(None, None, 'cross')
Inputs may be any that keep to these rules, and one draw needn't show every extreme that they name: Brick 0 starts at node 0; for s >= 1, brick_edges[s, 0] - 64 s lies between 1 and 16; each brick ends where the next starts and the last ends at 1025; some brick starts exactly 16 after its tile and another exactly 1 after.
All inputs are finite; a program needn't handle non-finite values.
Results may differ from a plain program's by a relative error of at most 0.00022.
Values sent between devices are 32-bit elements; how exact they have to be, the bound alone decides.
No kernel may reach another device: no remote copies, remote signals or barrier semaphores. Data moves between devices by JAX's collectives and lax.ppermute only.
A program may use at most 128 MiB of HBM per device.

v0:
```python
import jax
import jax.numpy as jnp
from jax import lax
from jax.sharding import PartitionSpec as P

TILE = 64
HALO = 16
LEVELS = 4


def passed_along(x, axis, by):
    count = lax.axis_size(axis)
    pairs = [(i, i + by) for i in range(count) if 0 <= i + by < count]
    return lax.ppermute(x, axis, pairs)


def from_partner(block, axis, bit):
    count = lax.axis_size(axis)
    route = []
    for low in range(count):
        high = low | 1 << bit
        if high != low and high < count:
            route += [(low, high), (high, low)]
    return lax.ppermute(block, axis, route)


def one_level(values, widths):
    left_width = widths[0::2]
    right_width = widths[1::2]
    coarse_width = left_width + right_width
    even_nodes = values[:, 0::2, :]
    odd_nodes = values[:, 1::2, :]
    details = (
        odd_nodes
        - (
            right_width[:, None] * even_nodes[:, :-1, :]
            + left_width[:, None] * even_nodes[:, 1:, :]
        )
        / coarse_width[:, None]
    )
    weight_after = left_width / 6.0 + right_width / 3.0
    before = right_width / 6.0 + left_width / 3.0
    zero_row = jnp.zeros_like(details[:, :1, :])
    load_vec = jnp.concatenate(
        [weight_after[:, None] * details, zero_row], axis=1
    ) + jnp.concatenate([zero_row, before[:, None] * details], axis=1)
    zero_width = jnp.zeros_like(coarse_width[:1])
    padded_width = jnp.concatenate([zero_width, coarse_width, zero_width])
    main_diag = (padded_width[:-1] + padded_width[1:]) / 3.0
    lower_diag = padded_width[:-1] / 6.0
    upper_diag = padded_width[1:] / 6.0
    identity = jnp.eye(main_diag.shape[0], dtype=values.dtype)
    inverse = lax.linalg.tridiagonal_solve(lower_diag, main_diag, upper_diag, identity)
    correction = jnp.einsum("kj,sjl->skl", inverse, load_vec, precision=lax.Precision.HIGHEST)
    return (even_nodes + correction, details, coarse_width)


def merge_sets(lower_values, lower_widths, upper_values, upper_widths):
    shared = 0.5 * (lower_values[:, -1:, :] + upper_values[:, :1, :])
    values = jnp.concatenate([lower_values[:, :-1, :], shared, upper_values[:, 1:, :]], axis=1)
    widths = jnp.concatenate([lower_widths, upper_widths])
    return one_level(values, widths)


def assemble(bricks, edges, slab_index):
    first_node = edges[0, 0]
    finish = edges[0, 1]
    length = finish - first_node
    tail_cells = lax.dynamic_slice_in_dim(bricks, length - HALO, HALO, 1)
    from_left = passed_along(tail_cells, "slab", 1)
    joined = jnp.concatenate([from_left, bricks], axis=1)
    node_ids = slab_index * TILE + jnp.arange(TILE + 1, dtype=jnp.int32)
    positions = node_ids - first_node + HALO
    return jnp.take(joined, positions, axis=1)


def on_device(sim_field, brick_edges, cell_width):
    slab_index = lax.axis_index("slab")
    cross_count = lax.axis_size("cross")
    species, rows_count, line_count = sim_field.shape
    blocks = sim_field.reshape(species, rows_count, cross_count, line_count // cross_count)
    arrived = lax.all_to_all(blocks, "cross", split_axis=2, concat_axis=2, tiled=True)
    relaid = arrived.reshape(species, rows_count, line_count)
    tile_values = assemble(relaid, brick_edges, slab_index)
    values = tile_values
    widths = cell_width
    collected = []
    for level_index in range(LEVELS):
        values, details, widths = one_level(values, widths)
        collected.append(details)
    tile_detail = jnp.concatenate(collected, axis=1)
    tree_depth = lax.axis_size("slab").bit_length() - 1
    stored = jnp.zeros((values.shape[0], values.shape[1] - 1, values.shape[2]), values.dtype)
    for level_index in range(tree_depth):
        other_values, other_widths = from_partner((values, widths), "slab", level_index)
        upper_side = slab_index >> level_index & 1 == 1
        lower_values = jnp.where(upper_side, other_values, values)
        lower_widths = jnp.where(upper_side, other_widths, widths)
        upper_values = jnp.where(upper_side, values, other_values)
        upper_widths = jnp.where(upper_side, widths, other_widths)
        values, details, widths = merge_sets(lower_values, lower_widths, upper_values, upper_widths)
        keep_here = upper_side & (slab_index & 2**level_index - 1 == 0)
        if level_index == tree_depth - 1:
            keep_here = keep_here | (slab_index == 0)
        stored = jnp.where(keep_here, details, stored)
    return (tile_detail, stored, values)


def solution(mesh):
    placed = (P(None, "slab", "cross"), P("slab", None), P("slab"))
    return jax.shard_map(
        on_device,
        mesh=mesh,
        in_specs=placed,
        out_specs=(P(None, "slab", "cross"), P(None, "slab", "cross"), P(None, None, "cross")),
        check_vma=False,
    )
```

profile of v0, /device:TPU:0, one launch (start us, length us, event | category | flops | bytes accessed | tf_op | source)
XLA Modules:
  0.0 333.3 jit_solution(6127420235838031505)
XLA Ops:
  0.6 4.2 %reshape.79 = f32[4,96,2,1024]{3,2,1,0:T(2,128)S(1)} reshape(f32[4,96,2048]{2,1,0:T(8,128)} %param.3) | data formatting | bytes 6291456 | tf_op jit(solution)/shard_map/reshape | solution.py:81
  4.9 3.7 %copy.16 = f32[4,96,2,1024]{3,0,1,2:T(4,128)} copy(f32[4,96,2,1024]{3,2,1,0:T(2,128)S(1)} %reshape.79) | data formatting | bytes 6291456 | tf_op jit(solution)/shard_map/reshape | solution.py:81
  8.6 4.4 %all-to-all-start = ((f32[4,96,2,1024]{3,0,1,2:T(4,128)}), f32[4,96,2,1024]{3,0,1,2:T(4,128)S(1)}, u32[]{:S(2)}, u32[]{:S(2)}) async-start(f32[4,96,2,1024]{3,0,1,2:T(4,128)} %copy.16), calls=%async_computation | async-start | bytes 6291456 | tf_op jit(solution)/shard_map/all_to_all | solution.py:82
  16.3 1.2 compare_and_fusion
  17.6 0.7 fusion.206
  18.3 0.7 fusion.208
  19.0 0.7 fusion.205
  19.8 0.7 fusion.210
  20.5 0.7 fusion.207
  21.2 0.7 fusion.209
  82.3 19.9 %fusion.89 = (f32[1,33]{1,0:T(1,128)S(1)}, f32[1,33]{1,0:T(1,128)S(1)}, f32[1,33]{1,0:T(1,128)S(1)}, f32[1,33]{1,0:T(1,128)S(1)}, f32[1,33]{1,0:T(1,128)S(1)}, /...) fusion(f32[33,33]{1,0:T(8,128)S(1)} %fusion.52, ...), kind=kLoop, calls=%fused_computation.209 | loop fusion | flops 3102 | bytes 8700 | tf_op jit(solution)/shard_map/eval_jaxpr/div | solution.py:53
  102.9 0.7 fusion.203
  103.6 0.7 fusion.202
  104.3 0.7 fusion.204
  133.7 10.0 %fusion.73 = (f32[1,17]{1,0:T(1,128)S(1)}, f32[1,17]{1,0:T(1,128)S(1)}, f32[1,17]{1,0:T(1,128)S(1)}, f32[1,17]{1,0:T(1,128)S(1)}, f32[1,17]{1,0:T(1,128)S(1)}, /...) fusion(f32[17,17]{1,0:T(8,128)S(1)} %fusion.54, ...), kind=kLoop, calls=%fused_computation.176 | loop fusion | flops 782 | bytes 2300 | tf_op jit(solution)/shard_map/eval_jaxpr/div | solution.py:53
  144.4 0.7 fusion.201
  145.1 0.7 fusion.199
  159.5 5.1 %fusion.65 = (f32[1,9]{1,0:T(1,128)S(1)}, f32[1,9]{1,0:T(1,128)S(1)}, f32[1,9]{1,0:T(1,128)S(1)}, f32[1,9]{1,0:T(1,128)S(1)}, f32[1,9]{1,0:T(1,128)S(1)}, /*inde...) fusion(f32[9,9]{1,0:T(8,128)S(1)} %fusion.56, f32[]{:T(128)S(6)} %sub.3217, f32[]{:T(128)} %bitcast.174, ...), kind=kLoop, calls=%fused_computation.159 | loop fusion | flops 198 | bytes 636 | tf_op jit(solution)/shard_map/eval_jaxpr/div | solution.py:53
  165.9 0.7 fusion.196
  173.0 2.5 subtract_divide_fusion.17
  181.8 0.7 multiply_subtract_fusion.20
  182.6 0.7 multiply_subtract_fusion.28
  183.3 0.8 multiply_subtract_fusion.44
  185.1 2.6 collective-permute-start.4
  187.7 0.7 fusion.195
  188.4 0.7 fusion.193
  195.5 2.5 subtract_divide_fusion.13
  199.8 0.7 multiply_subtract_fusion.12
  201.4 1.6 collective-permute-start.6
  203.1 0.7 fusion.192
  203.7 0.7 fusion.190
  210.8 2.5 subtract_divide_fusion.9
  215.2 0.7 multiply_subtract_fusion.8
  217.4 2.7 collective-permute-start.8
  220.8 0.7 fusion.187
  229.7 2.5 subtract_divide_fusion.5
  232.1 0.7 multiply_subtract_fusion.4
  233.4 1.7 copy-done
  235.0 2.9 copy.21
  238.0 0.8 constant_dynamic-slice_fusion
  238.8 2.3 collective-permute-start
  242.7 4.7 %pad_maximum_fusion = f32[4,112,2048]{2,0,1:T(4,128)} fusion(f32[4,96,2048]{2,0,1:T(4,128)S(1)} %bitcast.301, f32[4,16,2048]{2,0,1:T(4,128)} %collective-permute-done), kind=kLoop, calls=%fused_computation.1 | loop fusion | flops 917504 | bytes 7340032 | tf_op jit(solution)/shard_map/concatenate | solution.py:71
  247.4 3.9 %gather_fusion = f32[65,4,2048]{2,1,0:T(4,128)S(1)} fusion(f32[4,112,2048]{2,0,1:T(4,128)} %pad_maximum_fusion, s32[1024]{0:T(1024)S(1)} %pad_clamp_fusion), kind=kCustom, calls=%fused_computation | custom fusion | bytes 4260100 | tf_op jit(solution)/shard_map/jit(_take)/gather | solution.py:74
  251.3 2.8 fusion.2
  254.0 5.9 %slice.1530 = f32[4,33,2048]{2,1,0:T(8,128)S(1)} slice(f32[4,65,2048]{2,1,0:T(8,128)} %fusion.2), slice={[0:4:1], [0:65:2], [0:2048:1]} | slice | bytes 2162688 | tf_op jit(solution)/shard_map/slice | solution.py:31
  259.9 5.4 %slice.1528 = f32[4,32,2048]{2,1,0:T(8,128)} slice(f32[4,65,2048]{2,1,0:T(8,128)} %fusion.2), slice={[0:4:1], [1:65:2], [0:2048:1]} | slice | bytes 2097152 | tf_op jit(solution)/shard_map/slice | solution.py:32
  265.4 1.6 broadcast_multiply_fusion.1
  267.1 2.6 fusion
  269.7 4.0 %slice.1666 = f32[4,17,2048]{2,1,0:T(8,128)S(1)} slice(f32[4,33,2048]{2,1,0:T(8,128)} %fusion), slice={[0:4:1], [0:33:2], [0:2048:1]} | slice | bytes 1114112 | tf_op jit(solution)/shard_map/slice | solution.py:31
  273.8 2.1 slice.1664
  276.2 0.9 fusion.1
  279.5 5.1 %collective-permute-start.1 = (f32[4,5,2048]{2,1,0:T(8,128)S(1)}, f32[4,5,2048]{2,1,0:T(8,128)S(1)}, u32[]{:S(2)}, u32[]{:S(2)}) collective-permute-start(f32[4,5,2048]{2,1,0:T(8,128)S(1)} %fusion.4), channel_id=1, source_target_pairs={{0,2},{2,0},{4,6},{6,4},{8,10},{10,8},{12,14},{14,12},{16,18},{18,... | collective-permute-start | bytes 491528 | tf_op jit(solution)/shard_map/ppermute | solution.py:24
  285.3 0.7 fusion.184
  295.6 2.5 collective-permute-start.3
  298.1 2.6 subtract_divide_fusion.1
  300.7 4.3 %collective-permute-done.3 = f32[4,5,2048]{2,1,0:T(8,128)S(1)} collective-permute-done((f32[4,5,2048]{2,1,0:T(8,128)S(1)}, f32[4,5,2048]{2,1,0:T(8,128)S(1)}, u32[]{:S(2)}, u32[]{:S(2)}) %collective-permute-start.3) | collective-permute-done | bytes 163872 | tf_op jit(solution)/shard_map/ppermute | solution.py:24
  306.4 2.6 collective-permute-start.5
  309.7 5.5 %collective-permute-done.5 = f32[4,5,2048]{2,1,0:T(8,128)S(1)} collective-permute-done((f32[4,5,2048]{2,1,0:T(8,128)S(1)}, f32[4,5,2048]{2,1,0:T(8,128)S(1)}, u32[]{:S(2)}, u32[]{:S(2)}) %collective-permute-start.5) | collective-permute-done | bytes 163872 | tf_op jit(solution)/shard_map/ppermute | solution.py:24
  316.7 1.6 collective-permute-start.7
  318.3 1.3 pad_maximum_fusion.1
  319.6 2.5 copy.19
  322.2 8.3 %collective-permute-done.7 = f32[4,5,2048]{2,1,0:T(8,128)S(1)} collective-permute-done((f32[4,5,2048]{2,1,0:T(8,128)S(1)}, f32[4,5,2048]{2,1,0:T(8,128)S(1)}, u32[]{:S(2)}, u32[]{:S(2)}) %collective-permute-start.7) | collective-permute-done | bytes 163872 | tf_op jit(solution)/shard_map/ppermute | solution.py:24
  331.4 0.7 broadcast_multiply_fusion.6
  332.5 0.8 copy.20
  (231 shorter events, 20.4 us)
Async XLA Ops:
  8.6 4.4 %copy-start.55 = (f32[64]{0:T(128)S(1)}, f32[64]{0:T(128)}, u32[]{:S(2)}) copy-start(f32[64]{0:T(128)} %param.5) | copy-start | bytes 772
  8.6 6.5 %copy-start.52 = (s32[1,2]{1,0:T(1,128)S(1)}, s32[1,2]{1,0:T(1,128)}, u32[]{:S(2)}) copy-start(s32[1,2]{1,0:T(1,128)} %param.4) | copy-start | bytes 28
  8.6 224.8 %all-to-all-start = ((f32[4,96,2,1024]{3,0,1,2:T(4,128)}), f32[4,96,2,1024]{3,0,1,2:T(4,128)S(1)}, u32[]{:S(2)}, u32[]{:S(2)}) async-start(f32[4,96,2,1024]{3,0,1,2:T(4,128)} %copy.16), calls=%async_computation | async-start | bytes 6291456 | tf_op jit(solution)/shard_map/all_to_all | solution.py:82
  14.2 67.4 %copy-start.23 = (f32[4]{0:T(128)}, f32[4]{0:T(128)S(1)}, u32[]{:S(2)}) copy-start(f32[4]{0:T(128)S(1)} %slice.1780) | copy-start | bytes 52
  14.3 67.3 %copy-start.25 = (f32[4]{0:T(128)}, f32[4]{0:T(128)S(1)}, u32[]{:S(2)}) copy-start(f32[4]{0:T(128)S(1)} %slice.1777) | copy-start | bytes 52
  14.9 170.1 %copy-start.12 = (f32[4]{0:T(128)}, f32[4]{0:T(128)S(1)}, u32[]{:S(2)}) copy-start(f32[4]{0:T(128)S(1)} %get-tuple-element.215) | copy-start | bytes 52
  14.9 169.3 %collective-permute-start.2 = (f32[4]{0:T(128)S(1)}, f32[4]{0:T(128)S(1)}, u32[]{:S(2)}, u32[]{:S(2)}) collective-permute-start(f32[4]{0:T(128)S(1)} %get-tuple-element.215), channel_id=1, source_target_pairs={{0,2},{2,0},{4,6},{6,4},{8,10},{10,8},{12,14},{14,12},{16,18},{18,... | collective-permute-start | bytes 56 | tf_op jit(solution)/shard_map/ppermute | solution.py:24
  184.4 0.7 copy-start.30
  185.1 52.9 %copy-start.14 = (f32[4]{0:T(128)}, f32[4]{0:T(128)S(1)}, u32[]{:S(2)}) copy-start(f32[4]{0:T(128)S(1)} %get-tuple-element.211) | copy-start | bytes 52
  185.1 15.5 %collective-permute-start.4 = (f32[4]{0:T(128)S(1)}, f32[4]{0:T(128)S(1)}, u32[]{:S(2)}, u32[]{:S(2)}) collective-permute-start(f32[4]{0:T(128)S(1)} %get-tuple-element.211), channel_id=1, source_target_pairs={{0,4},{4,0},{2,6},{6,2},{8,12},{12,8},{10,14},{14,10},{16,20},{20,... | collective-permute-start | bytes 56 | tf_op jit(solution)/shard_map/ppermute | solution.py:24
  200.7 15.9 %copy-start.36 = (f32[4]{0:T(128)}, f32[4]{0:T(128)S(1)}, u32[]{:S(2)}) copy-start(f32[4]{0:T(128)S(1)} %slice.1828) | copy-start | bytes 52
  201.4 36.5 %copy-start.16 = (f32[4]{0:T(128)}, f32[4]{0:T(128)S(1)}, u32[]{:S(2)}) copy-start(f32[4]{0:T(128)S(1)} %get-tuple-element.208) | copy-start | bytes 52
  201.4 15.1 %collective-permute-start.6 = (f32[4]{0:T(128)S(1)}, f32[4]{0:T(128)S(1)}, u32[]{:S(2)}, u32[]{:S(2)}) collective-permute-start(f32[4]{0:T(128)S(1)} %get-tuple-element.208), channel_id=1, source_target_pairs={{0,8},{8,0},{2,10},{10,2},{4,12},{12,4},{6,14},{14,6},{16,24},{24,... | collective-permute-start | bytes 56 | tf_op jit(solution)/shard_map/ppermute | solution.py:24
  216.7 0.7 copy-start.42
  216.8 0.6 copy-start.44
  217.4 23.8 %copy-start.18 = (f32[4]{0:T(128)}, f32[4]{0:T(128)S(1)}, u32[]{:S(2)}) copy-start(f32[4]{0:T(128)S(1)} %get-tuple-element.205) | copy-start | bytes 52
  217.4 23.8 %collective-permute-start.8 = (f32[4]{0:T(128)S(1)}, f32[4]{0:T(128)S(1)}, u32[]{:S(2)}, u32[]{:S(2)}) collective-permute-start(f32[4]{0:T(128)S(1)} %get-tuple-element.205), channel_id=1, source_target_pairs={{0,16},{16,0},{2,18},{18,2},{4,20},{20,4},{6,22},{22,6},{8,24},{24... | collective-permute-start | bytes 56 | tf_op jit(solution)/shard_map/ppermute | solution.py:24
  233.4 1.7 copy-start
  238.8 3.9 %collective-permute-start = (f32[4,16,2048]{2,0,1:T(4,128)}, f32[4,16,2048]{2,0,1:T(4,128)}, u32[]{:S(2)}, u32[]{:S(2)}) collective-permute-start(f32[4,16,2048]{2,0,1:T(4,128)} %constant_dynamic-slice_fusion), channel_id=1, source_target_pairs={{0,2},{2,4},{4,6},{6,8},{8,10},{10,12},{12,14},{14,16},{16,18},{18... | collective-permute-start | bytes 1572872 | tf_op jit(solution)/shard_map/ppermute | solution.py:14
  241.3 6.0 %copy-start.47 = (f32[4]{0:T(128)}, f32[4]{0:T(128)S(1)}, u32[]{:S(2)}) copy-start(f32[4]{0:T(128)S(1)} %slice.1877) | copy-start | bytes 52
  241.4 0.6 copy-start.49
  242.0 5.3 %copy-start.20 = (f32[4]{0:T(128)}, f32[4]{0:T(128)S(1)}, u32[]{:S(2)}) copy-start(f32[4]{0:T(128)S(1)} %get-tuple-element.203) | copy-start | bytes 52
  247.4 3.9 %copy-start.54 = (pred[65]{0:T(512)(128)(4,1)S(1)}, pred[65]{0:T(512)(128)(4,1)}, u32[]{:S(2)}) copy-start(pred[65]{0:T(512)(128)(4,1)} %compare_and_fusion) | copy-start | bytes 199
  276.1 1.3 copy-start.1
  276.2 1.5 copy-start.28
  277.6 1.3 copy-start.13
  277.6 1.3 copy-start.24
  277.6 1.3 copy-start.26
  277.6 1.3 copy-start.27
  277.6 1.4 copy-start.22
  277.8 6.8 %copy-start.10 = (f32[5]{0:T(128)S(1)}, f32[5]{0:T(128)}, u32[]{:S(2)}) copy-start(f32[5]{0:T(128)} %get-tuple-element.246) | copy-start | bytes 64
  277.9 7.5 %copy-start.11 = (f32[5]{0:T(128)S(1)}, f32[5]{0:T(128)}, u32[]{:S(2)}) copy-start(f32[5]{0:T(128)} %get-tuple-element.248) | copy-start | bytes 64
  279.1 15.8 %copy-start.15 = (f32[4]{0:T(128)S(1)}, f32[4]{0:T(128)}, u32[]{:S(2)}) copy-start(f32[4]{0:T(128)} %copy-done.14) | copy-start | bytes 52
  279.1 15.8 %copy-start.31 = (f32[4]{0:T(128)S(1)}, f32[4]{0:T(128)}, u32[]{:S(2)}) copy-start(f32[4]{0:T(128)} %copy-done.30) | copy-start | bytes 52
  279.1 15.8 %copy-start.33 = (f32[4]{0:T(128)S(1)}, f32[4]{0:T(128)}, u32[]{:S(2)}) copy-start(f32[4]{0:T(128)} %copy-done.32) | copy-start | bytes 52
  279.1 15.8 %copy-start.34 = (f32[4]{0:T(128)S(1)}, f32[4]{0:T(128)}, u32[]{:S(2)}) copy-start(f32[4]{0:T(128)} %get-tuple-element.212) | copy-start | bytes 52
  279.5 15.5 %copy-start.29 = (f32[4]{0:T(128)S(1)}, f32[4]{0:T(128)}, u32[]{:S(2)}) copy-start(f32[4]{0:T(128)} %get-tuple-element.210) | copy-start | bytes 52
  279.5 14.7 %collective-permute-start.1 = (f32[4,5,2048]{2,1,0:T(8,128)S(1)}, f32[4,5,2048]{2,1,0:T(8,128)S(1)}, u32[]{:S(2)}, u32[]{:S(2)}) collective-permute-start(f32[4,5,2048]{2,1,0:T(8,128)S(1)} %fusion.4), channel_id=1, source_target_pairs={{0,2},{2,0},{4,6},{6,4},{8,10},{10,8},{12,14},{14,12},{16,18},{18,... | collective-permute-start | bytes 491528 | tf_op jit(solution)/shard_map/ppermute | solution.py:24
  295.1 10.1 %copy-start.2 = (f32[4,4,2048]{2,1,0:T(4,128)}, f32[4,4,2048]{2,1,0:T(4,128)S(1)}, u32[]{:S(2)}) copy-start(f32[4,4,2048]{2,1,0:T(4,128)S(1)} %get-tuple-element.58) | copy-start | bytes 393220
  295.1 10.6 %copy-start.17 = (f32[4]{0:T(128)S(1)}, f32[4]{0:T(128)}, u32[]{:S(2)}) copy-start(f32[4]{0:T(128)} %copy-done.16) | copy-start | bytes 52
  295.1 10.6 %copy-start.37 = (f32[4]{0:T(128)S(1)}, f32[4]{0:T(128)}, u32[]{:S(2)}) copy-start(f32[4]{0:T(128)} %copy-done.36) | copy-start | bytes 52
  295.1 10.6 %copy-start.39 = (f32[4]{0:T(128)S(1)}, f32[4]{0:T(128)}, u32[]{:S(2)}) copy-start(f32[4]{0:T(128)} %copy-done.38) | copy-start | bytes 52
  295.1 10.6 %copy-start.40 = (f32[4]{0:T(128)S(1)}, f32[4]{0:T(128)}, u32[]{:S(2)}) copy-start(f32[4]{0:T(128)} %get-tuple-element.209) | copy-start | bytes 52
  295.6 10.3 %copy-start.35 = (f32[4]{0:T(128)S(1)}, f32[4]{0:T(128)}, u32[]{:S(2)}) copy-start(f32[4]{0:T(128)} %get-tuple-element.207) | copy-start | bytes 52
  295.6 10.4 %copy-start.8 = (f32[5,5]{1,0:T(8,128)S(1)}, f32[5,5]{1,0:T(8,128)}, u32[]{:S(2)}) copy-start(f32[5,5]{1,0:T(8,128)} %concatenate.193) | copy-start | bytes 304
  295.6 9.4 %collective-permute-start.3 = (f32[4,5,2048]{2,1,0:T(8,128)S(1)}, f32[4,5,2048]{2,1,0:T(8,128)S(1)}, u32[]{:S(2)}, u32[]{:S(2)}) collective-permute-start(f32[4,5,2048]{2,1,0:T(8,128)S(1)} %fusion.5), channel_id=1, source_target_pairs={{0,4},{4,0},{2,6},{6,2},{8,12},{12,8},{10,14},{14,10},{16,20},{20,... | collective-permute-start | bytes 491528 | tf_op jit(solution)/shard_map/ppermute | solution.py:24
  305.8 9.5 %copy-start.4 = (f32[4,4,2048]{2,1,0:T(4,128)}, f32[4,4,2048]{2,1,0:T(4,128)S(1)}, u32[]{:S(2)}) copy-start(f32[4,4,2048]{2,1,0:T(4,128)S(1)} %get-tuple-element.47) | copy-start | bytes 393220
  305.9 10.0 %copy-start.19 = (f32[4]{0:T(128)S(1)}, f32[4]{0:T(128)}, u32[]{:S(2)}) copy-start(f32[4]{0:T(128)} %copy-done.18) | copy-start | bytes 52
  305.9 10.0 %copy-start.43 = (f32[4]{0:T(128)S(1)}, f32[4]{0:T(128)}, u32[]{:S(2)}) copy-start(f32[4]{0:T(128)} %copy-done.42) | copy-start | bytes 52
  305.9 10.0 %copy-start.45 = (f32[4]{0:T(128)S(1)}, f32[4]{0:T(128)}, u32[]{:S(2)}) copy-start(f32[4]{0:T(128)} %copy-done.44) | copy-start | bytes 52
  305.9 10.0 %copy-start.46 = (f32[4]{0:T(128)S(1)}, f32[4]{0:T(128)}, u32[]{:S(2)}) copy-start(f32[4]{0:T(128)} %get-tuple-element.206) | copy-start | bytes 52
  306.4 9.6 %copy-start.41 = (f32[4]{0:T(128)S(1)}, f32[4]{0:T(128)}, u32[]{:S(2)}) copy-start(f32[4]{0:T(128)} %get-tuple-element.204) | copy-start | bytes 52
  306.4 9.7 %copy-start.9 = (f32[5,5]{1,0:T(8,128)S(1)}, f32[5,5]{1,0:T(8,128)}, u32[]{:S(2)}) copy-start(f32[5,5]{1,0:T(8,128)} %concatenate.200) | copy-start | bytes 304
  306.4 8.8 %collective-permute-start.5 = (f32[4,5,2048]{2,1,0:T(8,128)S(1)}, f32[4,5,2048]{2,1,0:T(8,128)S(1)}, u32[]{:S(2)}, u32[]{:S(2)}) collective-permute-start(f32[4,5,2048]{2,1,0:T(8,128)S(1)} %fusion.6), channel_id=1, source_target_pairs={{0,8},{8,0},{2,10},{10,2},{4,12},{12,4},{6,14},{14,6},{16,24},{24,... | collective-permute-start | bytes 491528 | tf_op jit(solution)/shard_map/ppermute | solution.py:24
  316.0 0.7 copy-start.6
  316.7 13.9 %collective-permute-start.7 = (f32[4,5,2048]{2,1,0:T(8,128)S(1)}, f32[4,5,2048]{2,1,0:T(8,128)S(1)}, u32[]{:S(2)}, u32[]{:S(2)}) collective-permute-start(f32[4,5,2048]{2,1,0:T(8,128)S(1)} %fusion.7), channel_id=1, source_target_pairs={{0,16},{16,0},{2,18},{18,2},{4,20},{20,4},{6,22},{22,6},{8,24},{24... | collective-permute-start | bytes 491528 | tf_op jit(solution)/shard_map/ppermute | solution.py:24
  322.1 9.0 %copy-start.21 = (f32[4]{0:T(128)S(1)}, f32[4]{0:T(128)}, u32[]{:S(2)}) copy-start(f32[4]{0:T(128)} %copy-done.20) | copy-start | bytes 52
  322.1 9.0 %copy-start.48 = (f32[4]{0:T(128)S(1)}, f32[4]{0:T(128)}, u32[]{:S(2)}) copy-start(f32[4]{0:T(128)} %copy-done.47) | copy-start | bytes 52
  322.1 9.0 %copy-start.50 = (f32[4]{0:T(128)S(1)}, f32[4]{0:T(128)}, u32[]{:S(2)}) copy-start(f32[4]{0:T(128)} %copy-done.49) | copy-start | bytes 52
  322.1 9.0 %copy-start.51 = (f32[4]{0:T(128)S(1)}, f32[4]{0:T(128)}, u32[]{:S(2)}) copy-start(f32[4]{0:T(128)} %get-tuple-element.202) | copy-start | bytes 52
  322.2 9.2 %copy-start.3 = (f32[4,4,2048]{2,1,0:T(4,128)S(1)}, f32[4,4,2048]{2,1,0:T(4,128)}, u32[]{:S(2)}) copy-start(f32[4,4,2048]{2,1,0:T(4,128)} %copy-done.2) | copy-start | bytes 393220
  322.2 9.2 %copy-start.5 = (f32[4,4,2048]{2,1,0:T(4,128)S(1)}, f32[4,4,2048]{2,1,0:T(4,128)}, u32[]{:S(2)}) copy-start(f32[4,4,2048]{2,1,0:T(4,128)} %copy-done.4) | copy-start | bytes 393220
  322.2 9.2 %copy-start.7 = (f32[4,4,2048]{2,1,0:T(4,128)S(1)}, f32[4,4,2048]{2,1,0:T(4,128)}, u32[]{:S(2)}) copy-start(f32[4,4,2048]{2,1,0:T(4,128)} %copy-done.6) | copy-start | bytes 393220
  322.2 9.2 %copy-start.53 = (f32[4]{0:T(128)S(1)}, f32[4]{0:T(128)}, u32[]{:S(2)}) copy-start(f32[4]{0:T(128)} %get-tuple-element.201) | copy-start | bytes 52
  (2 other events, 1.2 us)
where the time goes:
time: 337 us; the launch traced here: 333 us
  between operations  151 us (45%)
  other arithmetic  73.6 us (22%)
  local copies, waits for them, and re-layouts  58.5 us (17%)
  starting transfers between devices  25.5 us (8%)
  waiting for transfers between devices  18.2 us (5%)
  matrix products  6.12 us (2%)
    div x8, other arithmetic, one_level(): lax.linalg.tridiagonal_solve(lower_diag, main_diag, upper_diag, identity)  47.6 us
    ppermute x8, starting transfers between devices, from_partner(): return lax.ppermute(block, axis, route)  18.8 us
    ppermute x8, waiting for transfers between devices, from_partner(): return lax.ppermute(block, axis, route)  18.2 us
    slice x21, local copies, waits for them, and re-layouts, one_level(): lax.linalg.tridiagonal_solve(lower_diag, main_diag, upper_diag, identity)  14.5 us
    slice x8, local copies, waits for them, and re-layouts, one_level(): even_nodes = values[:, 0::2, :]  10.9 us
    slice x8, local copies, waits for them, and re-layouts, one_level(): odd_nodes = values[:, 1::2, :]  8.34 us
    reshape x2, local copies, waits for them, and re-layouts, on_device(): sim_field.reshape(species, rows_count, cross_count, line_count // cross_c...  7.93 us
  transfers between devices with their start and end apart: 10, of which 3 were waited for; matrix products, arithmetic and copies ran while one was open for 26% of the time, Pallas kernels for 0%

commit v1 on v0

v1 whole, which is shorter than its diff:
```python
import functools

import jax
import jax.numpy as jnp
from jax import lax
from jax.experimental import pallas as pl
from jax.experimental.pallas import tpu as pltpu
from jax.sharding import PartitionSpec as P

TILE = 64
HALO = 16
LEVELS = 4
COARSE = 5
DETAILS = TILE - COARSE + 1
LANES = 128
SUB = 8
F32 = jnp.float32
HIGHEST = lax.Precision.HIGHEST


def call(kernel, out_shape, **kw):
    params = pltpu.CompilerParams(vmem_limit_bytes=kw.pop("vmem", 24 << 20))
    return pl.pallas_call(kernel, out_shape=out_shape, compiler_params=params, **kw)


def vmem_spec():
    return pl.BlockSpec(memory_space=pltpu.VMEM)


def smem_spec():
    return pl.BlockSpec(memory_space=pltpu.SMEM)


def tail_kernel(edges, field, out, buf, sems):
    species = out.shape[0]
    low = TILE // 2
    copies = []
    for sp in range(species):
        copy = pltpu.make_async_copy(
            field.at[sp, pl.ds(low, TILE - HALO), :], buf.at[sp, pl.ds(0, TILE - HALO), :], sems.at[sp]
        )
        copy.start()
        copies.append(copy)
    start = edges[0, 1] - edges[0, 0] - HALO - low
    rest = start & (SUB - 1)
    whole = start - rest
    for sp in range(species):
        copies[sp].wait()
        rows = buf[sp, pl.ds(pl.multiple_of(whole, SUB), HALO + SUB), :]
        out[sp] = pltpu.roll(rows, (HALO + SUB - rest) % (HALO + SUB), 0)[:HALO]


def brick_tail(edges, field):
    species, _, lines = field.shape
    return call(
        tail_kernel,
        jax.ShapeDtypeStruct((species, HALO, lines), F32),
        in_specs=[smem_spec(), pl.BlockSpec(memory_space=pl.ANY)],
        out_specs=vmem_spec(),
        scratch_shapes=[
            pltpu.VMEM((species, TILE - HALO + SUB, lines), F32),
            pltpu.SemaphoreType.DMA((species,)),
        ],
    )(edges, field)


PAD = 32


def matrix_kernel(edges, widths, out, coarse_width, nodes, cell, low, main, up, load):
    slab = lax.axis_index("slab")
    shift = edges[0, 0] - slab * TILE
    rows = nodes.shape[0]
    node = lax.broadcasted_iota(jnp.int32, (rows, LANES), 0)
    column = lax.broadcasted_iota(jnp.int32, (rows, LANES), 1)
    held = column - HALO + shift
    held = jnp.where((slab == 0) & (column < HALO), column + TILE, held)
    nodes[...] = ((held == node) & (node <= TILE)).astype(F32)
    cell[...] = jnp.zeros_like(cell)
    cell[:TILE] = widths[...]
    for ref in (low, up, load):
        ref[...] = jnp.zeros_like(ref)
    main[...] = jnp.ones_like(main)
    out[...] = jnp.zeros_like(out)
    placed = 0
    pairs = TILE // 2
    for _ in range(LEVELS):
        size = -(-(pairs + 1) // SUB) * SUB
        here = pl.ds(PAD, size)
        inside = lax.broadcasted_iota(jnp.int32, (size, LANES), 0) < pairs
        left = cell[pl.ds(0, size, stride=2)]
        right = cell[pl.ds(1, size, stride=2)]
        total = left + right
        safe = jnp.where(inside, total, 1.0)
        even = nodes[pl.ds(0, size, stride=2)]
        odd = nodes[pl.ds(1, size, stride=2)]
        after = nodes[pl.ds(2, size, stride=2)]
        detail = jnp.where(inside, odd - (right * even + left * after) / safe, 0.0)
        out[placed : placed + pairs] = detail[:pairs]
        placed += pairs
        load[here] = (right / 6.0 + left / 3.0) * detail
        load[pl.ds(PAD - 1, 1)] = jnp.zeros((1, LANES), F32)
        grown = (left / 6.0 + right / 3.0) * detail + load[pl.ds(PAD - 1, size)]
        up[here] = total
        before = up[pl.ds(PAD - 1, size)]
        node_at = lax.broadcasted_iota(jnp.int32, (size, LANES), 0)
        diag = jnp.where(node_at <= pairs, (before + total) / 3.0, 1.0)
        lower = jnp.where(node_at <= pairs, before / 6.0, 0.0)
        upper = total / 6.0
        step = 1
        while step <= pairs:
            low[here] = lower
            up[here] = upper
            main[here] = diag
            load[here] = grown
            back = pl.ds(PAD - step, size)
            fore = pl.ds(PAD + step, size)
            alpha = -lower / main[back]
            gamma = -upper / main[fore]
            diag = diag + alpha * up[back] + gamma * low[fore]
            grown = grown + alpha * load[back] + gamma * load[fore]
            lower = alpha * low[back]
            upper = gamma * up[fore]
            step *= 2
        coarse = even + grown / diag
        coarse = jnp.where(node_at <= pairs, coarse, 0.0)
        nodes[...] = jnp.zeros_like(nodes)
        nodes[:size] = coarse
        cell[...] = jnp.zeros_like(cell)
        cell[:size] = total
        pairs //= 2
    out[pl.ds(TILE, SUB)] = nodes[:SUB]
    coarse_width[...] = cell[:SUB]


def tile_matrix(edges, cell_width):
    widths = jnp.broadcast_to(cell_width[:, None], (TILE, LANES))
    scratch = pltpu.VMEM((PAD + 40 + PAD, LANES), F32)
    return call(
        matrix_kernel,
        (
            jax.ShapeDtypeStruct((TILE + SUB, LANES), F32),
            jax.ShapeDtypeStruct((SUB, LANES), F32),
        ),
        in_specs=[smem_spec(), vmem_spec()],
        out_specs=(vmem_spec(), vmem_spec()),
        scratch_shapes=[pltpu.VMEM((88, LANES), F32), pltpu.VMEM((88, LANES), F32)] + [scratch] * 4,
    )(edges, widths)


def coarse_kernel(matrix, coarse_width, halo, field, sets, extra, turned):
    sp = pl.program_id(0)
    slab = lax.axis_index("slab")
    lines = halo.shape[2]
    dense = sets.shape[1]
    per = (lines // 2) // LANES
    node_rows = pl.num_programs(0) * per
    row = jnp.where(slab == 0, field[0, TILE : TILE + HALO], halo[0])
    extra[0] = row
    weights = matrix[pl.ds(TILE, SUB)]
    result = jnp.dot(weights[:, :HALO], row, precision=HIGHEST, preferred_element_type=F32)
    result += jnp.dot(weights[:, HALO : HALO + TILE], field[0, :TILE], precision=HIGHEST, preferred_element_type=F32)
    for t in range(lines // LANES):
        turned[t * SUB : (t + 1) * SUB] = result[:, t * LANES : (t + 1) * LANES]
    for half in range(2):
        for k in range(COARSE):
            at = pl.multiple_of(k * node_rows + sp * per, SUB)
            sets[half, pl.ds(at, per)] = turned[pl.ds(half * per * SUB + k, per, stride=SUB)]

    @pl.when(sp == 0)
    def _():
        for half in range(2):
            sets[half, dense - SUB :] = coarse_width[...]


def coarse_sets(matrix, coarse_width, halo, field):
    species, _, lines = field.shape
    node_rows = species * (lines // 2) // LANES
    dense = COARSE * node_rows + SUB
    rows = TILE + HALO
    return call(
        coarse_kernel,
        (
            jax.ShapeDtypeStruct((2, dense, LANES), F32),
            jax.ShapeDtypeStruct((species, HALO, lines), F32),
        ),
        grid=(species,),
        in_specs=[
            pl.BlockSpec((TILE + SUB, LANES), lambda i: (0, 0)),
            pl.BlockSpec((SUB, LANES), lambda i: (0, 0)),
            pl.BlockSpec((1, HALO, lines), lambda i: (i, 0, 0)),
            pl.BlockSpec((1, rows, lines), lambda i: (i, 0, 0)),
        ],
        out_specs=(
            pl.BlockSpec((2, dense, LANES), lambda i: (0, 0, 0)),
            pl.BlockSpec((1, HALO, lines), lambda i: (i, 0, 0)),
        ),
        scratch_shapes=[pltpu.VMEM((lines // LANES * SUB, LANES), F32)],
    )(matrix, coarse_width, halo, field)


def detail_kernel(place, matrix, extra, brick, *rest):
    out = rest[-1]
    weights = matrix[:TILE]
    result = jnp.dot(weights[:, :HALO], extra[0], precision=HIGHEST, preferred_element_type=F32)
    result += jnp.dot(weights[:, HALO : HALO + TILE], brick[0], precision=HIGHEST, preferred_element_type=F32)
    out[0] = result[:DETAILS]


def details(place, matrix, extra, brick, width, lines, onto=None):
    species = extra.shape[0]

    def at(own):
        return lambda i, place: (i, 0, place[0] if own else 0)

    specs = [
        pl.BlockSpec((TILE + SUB, LANES), lambda i, place: (0, 0)),
        pl.BlockSpec((1, HALO, width), at(extra.shape[2] != width)),
        pl.BlockSpec((1, TILE, width), at(brick.shape[2] != width)),
    ]
    operands = [place, matrix, extra, brick]
    alias = {}
    if onto is not None:
        specs.append(pl.BlockSpec(memory_space=pl.ANY))
        operands.append(onto)
        alias = {4: 0}
    return call(
        detail_kernel,
        jax.ShapeDtypeStruct((species, DETAILS, lines), F32),
        grid_spec=pltpu.PrefetchScalarGridSpec(
            num_scalar_prefetch=1,
            grid=(species,),
            in_specs=specs,
            out_specs=pl.BlockSpec((1, DETAILS, width), at(True)),
        ),
        input_output_aliases=alias,
    )(*operands)


def read_set(ref, node_rows):
    values = [ref[k * node_rows : (k + 1) * node_rows] for k in range(COARSE)]
    widths = [ref[COARSE * node_rows + i : COARSE * node_rows + i + 1] for i in range(COARSE - 1)]
    return values, widths


def merged(lower, upper):
    lower_values, lower_widths = lower
    upper_values, upper_widths = upper
    shared = 0.5 * (lower_values[-1] + upper_values[0])
    values = lower_values[:-1] + [shared] + upper_values[1:]
    widths = lower_widths + upper_widths
    left, right = widths[0::2], widths[1::2]
    pairs = len(left)
    total = [a + b for a, b in zip(left, right)]
    detail = []
    for i in range(pairs):
        inverse = 1.0 / total[i]
        detail.append(
            values[2 * i + 1] - ((right[i] * inverse) * values[2 * i] + (left[i] * inverse) * values[2 * i + 2])
        )
    loads = []
    for k in range(pairs + 1):
        term = None
        if k < pairs:
            term = (left[k] / 6.0 + right[k] / 3.0) * detail[k]
        if k > 0:
            other = (right[k - 1] / 6.0 + left[k - 1] / 3.0) * detail[k - 1]
            term = other if term is None else term + other
        loads.append(term)
    ratio, solved = [], []
    for k in range(pairs + 1):
        diag = (total[k - 1] if k else 0.0) + (total[k] if k < pairs else 0.0)
        diag = diag / 3.0
        if k:
            off = total[k - 1] / 6.0
            pivot = 1.0 / (diag - off * ratio[-1])
            solved.append((loads[k] - off * solved[-1]) * pivot)
        else:
            pivot = 1.0 / diag
            solved.append(loads[k] * pivot)
        if k < pairs:
            ratio.append(total[k] / 6.0 * pivot)
    for k in range(pairs - 1, -1, -1):
        solved[k] = solved[k] - ratio[k] * solved[k + 1]
    coarse = [values[2 * k] + solved[k] for k in range(pairs + 1)]
    return coarse, detail, total


def merge_kernel(level, depth, own, other, *refs):
    slab = lax.axis_index("slab")
    node_rows = (own.shape[-2] - SUB) // COARSE
    upper_side = (slab >> level) & 1 == 1
    mine, theirs = own, other
    if level == 0:
        mine = own.at[slab & 1]
    mine, theirs = read_set(mine, node_rows), read_set(theirs, node_rows)

    def pick(first, second):
        return [jnp.where(upper_side, a, b) for a, b in zip(first, second)]

    lower = (pick(theirs[0], mine[0]), pick(theirs[1], mine[1]))
    upper = (pick(mine[0], theirs[0]), pick(mine[1], theirs[1]))
    coarse, detail, widths = merged(lower, upper)
    last = level == depth - 1
    core = slab & 1
    if level == 0:
        out, odd_out = refs
        for i in range(COARSE - 1):
            odd_out[i * node_rows : (i + 1) * node_rows] = detail[i]
    else:
        kept = refs[0] if level > 1 else None
        chip = slab & ~1
        keep = ((chip >> level) & 1 == 1) & (chip & ((1 << level) - 1) == 0)
        if last:
            keep = keep | (chip == 0)
        even = []
        for i in range(COARSE - 1):
            old = kept[i * node_rows : (i + 1) * node_rows] if kept is not None else jnp.zeros_like(detail[i])
            even.append(jnp.where(keep, detail[i], old))
        if not last:
            out, even_out = refs[-2:]
            for i in range(COARSE - 1):
                even_out[i * node_rows : (i + 1) * node_rows] = even[i]
        else:
            odd_in = refs[1] if level > 1 else refs[0]
            here, away = refs[-2:]
            for k in range(COARSE):
                here[k * node_rows : (k + 1) * node_rows] = coarse[k]
                away[k * node_rows : (k + 1) * node_rows] = coarse[k]
            for i in range(COARSE - 1):
                odd = odd_in[i * node_rows : (i + 1) * node_rows]
                at = (COARSE + i) * node_rows
                here[at : at + node_rows] = jnp.where(core == 0, even[i], odd)
                away[at : at + node_rows] = jnp.where(core == 0, odd, even[i])
            return
    for k in range(COARSE):
        out[k * node_rows : (k + 1) * node_rows] = coarse[k]
    for i in range(COARSE - 1):
        out[COARSE * node_rows + i : COARSE * node_rows + i + 1] = widths[i]
    rest = COARSE * node_rows + COARSE - 1
    out[rest : rest + SUB - COARSE + 1] = jnp.zeros((SUB - COARSE + 1, LANES), F32)


def merge(level, depth, own, other, *kept):
    dense = own.shape[-2]
    node_rows = (dense - SUB) // COARSE
    stored = jax.ShapeDtypeStruct(((COARSE - 1) * node_rows, LANES), F32)
    if level == depth - 1:
        ended = jax.ShapeDtypeStruct(((2 * COARSE - 1) * node_rows, LANES), F32)
        shapes = (ended, ended)
    else:
        shapes = (jax.ShapeDtypeStruct((dense, LANES), F32), stored)
    operands = (own, other) + kept
    return call(
        functools.partial(merge_kernel, level, depth),
        shapes,
        in_specs=[vmem_spec()] * len(operands),
        out_specs=(vmem_spec(), vmem_spec()),
    )(*operands)


def finish_kernel(own, other, tree, final, turned):
    cross = lax.axis_index("cross")
    species, _, lines = tree.shape
    width = lines // 2
    per = width // LANES
    node_rows = species * per
    for block, ref in ((cross, own), (1 - cross, other)):
        for sp in range(species):
            for k in range(2 * COARSE - 1):
                at = k * node_rows + sp * per
                slot = k if k < COARSE else k - COARSE + SUB
                turned[pl.ds(slot, per, stride=2 * SUB)] = ref[at : at + per]
            for t in range(per):
                lanes = pl.ds(pl.multiple_of(block * width + t * LANES, LANES), LANES)
                final[sp, :, lanes] = turned[pl.ds(t * 2 * SUB, COARSE)]
                tree[sp, :, lanes] = turned[pl.ds(t * 2 * SUB + SUB, COARSE - 1)]


def finish(own, other, species, lines):
    return call(
        finish_kernel,
        (
            jax.ShapeDtypeStruct((species, COARSE - 1, lines), F32),
            jax.ShapeDtypeStruct((species, COARSE, lines), F32),
        ),
        in_specs=[vmem_spec(), vmem_spec()],
        out_specs=(vmem_spec(), vmem_spec()),
        scratch_shapes=[pltpu.VMEM((lines // 2 // LANES * 2 * SUB, LANES), F32)],
    )(own, other)


def from_partner(block, axis, step):
    count = lax.axis_size(axis)
    return lax.ppermute(block, axis, [(i, i ^ step) for i in range(count)])


def shifted(block, axis):
    count = lax.axis_size(axis)
    return lax.ppermute(block, axis, [(i, i + 1) for i in range(count - 1)])


def exchanged(block, axis):
    species, rows, lines = block.shape
    count = lax.axis_size(axis)
    parts = block.reshape(species, rows, count, lines // count)
    return lax.all_to_all(parts, axis, split_axis=2, concat_axis=2, tiled=True).reshape(block.shape)


def on_device(sim_field, brick_edges, cell_width):
    species, _, lines = sim_field.shape
    cross_count = lax.axis_size("cross")
    slab = lax.axis_index("slab")
    cross = lax.axis_index("cross")
    depth = lax.axis_size("slab").bit_length() - 1
    width = lines // cross_count
    swapped = cross_count == 2

    halo = shifted(brick_tail(brick_edges, sim_field), "slab")
    if swapped:
        away = lax.dynamic_slice(sim_field, (0, 0, (1 - cross) * width), (species, TILE, width))
        brick_in = from_partner(away, "cross", 1)
    matrix, coarse_width = tile_matrix(brick_edges, cell_width)
    sets, extra = coarse_sets(matrix, coarse_width, halo, sim_field)
    if swapped:
        extra_away = lax.dynamic_slice(extra, (0, 0, (1 - cross) * width), (species, HALO, width))
        extra_in = from_partner(extra_away, "cross", 1)
        here, there = cross.astype(jnp.int32).reshape(1), (1 - cross).astype(jnp.int32).reshape(1)

    current = sets
    sent = lax.dynamic_index_in_dim(sets, 1 - slab % 2, 0, keepdims=False)
    kept = ()
    odd = None
    for level in range(depth):
        other = from_partner(sent, "slab", 1 << level)
        if level == depth - 1:
            kept = kept + (odd,)
        current, stored = merge(level, depth, current, other, *kept)
        sent = current
        if level == 0:
            odd = stored
        else:
            kept = (stored,)
    here_set, away_set = current, stored
    partner_set = from_partner(away_set, "slab", 1)

    if swapped:
        core = slab % 2
        mine = jnp.where(core == cross, here_set, partner_set)
        theirs = jnp.where(core == cross, partner_set, here_set)
        arrived = from_partner(theirs, "cross", 1)
        tree_detail, coarse_final = finish(mine, arrived, species, lines)
        tile_detail = details(here, matrix, extra, sim_field, width, lines)
        tile_detail = details(there, matrix, extra_in, brick_in, width, lines, tile_detail)
    else:
        first = jnp.where(slab % 2 == 0, here_set, partner_set)
        second = jnp.where(slab % 2 == 0, partner_set, here_set)
        ended = jnp.stack([first, second]).reshape(2, 2 * COARSE - 1, species, lines // 2)
        ended = ended.transpose(2, 1, 0, 3).reshape(species, 2 * COARSE - 1, lines)
        ended = exchanged(ended, "cross")
        coarse_final, tree_detail = ended[:, :COARSE], ended[:, COARSE:]
        rows = exchanged(jnp.concatenate([extra, sim_field[:, :TILE]], axis=1), "cross")
        start = jnp.zeros((1,), jnp.int32)
        tile_detail = details(start, matrix, rows[:, :HALO], rows[:, HALO:], lines, lines)
    return (tile_detail, tree_detail, coarse_final)


def solution(mesh):
    placed = (P(None, "slab", "cross"), P("slab", None), P("slab"))
    return jax.shard_map(
        on_device,
        mesh=mesh,
        in_specs=placed,
        out_specs=(P(None, "slab", "cross"), P(None, "slab", "cross"), P(None, None, "cross")),
        check_vma=False,
    )
```

time: 337 us -> 57.3 us (0.17)
  between operations: 151 us -> 0.75 us
  other arithmetic: 73.6 us -> 0.93 us
  local copies, waits for them, and re-layouts: 58.5 us -> 9.84 us
  Pallas kernels: 0 us -> 14.1 us
  waiting for transfers between devices: 18.2 us -> 11 us
  matrix products: 6.12 us -> 0 us
  starting transfers between devices: 25.5 us -> 20.2 us
    div x16 -> x0, other arithmetic: 48.8 us -> none  [the longest x8 47.6 us: one_level(): lax.linalg.tridiagonal_solve(lower_diag, main_diag, upper_diag, identity)]
    slice x62 -> x0, local copies, waits for them, and re-layouts: 36.1 us -> none  [the longest x21 14.5 us: one_level(): lax.linalg.tridiagonal_solve(lower_diag, main_diag, upper_diag, identity)]
    pallas_call x0 -> x10, Pallas kernels: none -> 14.1 us  [the longest x2 6.55 us: details(): call(detail_kernel, jax.ShapeDtypeStruct((species, DETAILS, lines), F32),...]
    reshape x3 -> x0, local copies, waits for them, and re-layouts: 10.8 us -> none  [the longest x2 7.93 us: on_device(): sim_field.reshape(species, rows_count, cross_count, line_count // cross_c...]
    ppermute x9, waiting for transfers between devices: 18.2 us -> 11 us  [the longest x8 11 us: from_partner(): return lax.ppermute(block, axis, [(i, i ^ step) for i in range(count)])]
    concatenate x10 -> x0, other arithmetic: 6.78 us -> none  [the longest x1 4.68 us: assemble(): joined = jnp.concatenate([from_left, bricks], axis=1)]
    dot_general x8 -> x0, matrix products: 6.12 us -> none  [one_level(): jnp.einsum('kj,sjl->skl', inverse, load_vec, precision=lax.Precision.HIGH...]
    sub x8 -> x0, other arithmetic: 5.4 us -> none  [one_level(): lax.linalg.tridiagonal_solve(lower_diag, main_diag, upper_diag, identity)]
  transfers between devices with their start and end apart: 10 -> 9, of which waited for: 3 -> 5; matrix products, arithmetic and copies ran while one was open for 26% -> 10% of each run, Pallas kernels for 0% -> 19%
where the time goes in v1:
time: 57.3 us; the launch traced here: 56.9 us
  starting transfers between devices  20.2 us (35%)
  Pallas kernels  14.1 us (25%)
  waiting for transfers between devices  11 us (19%)
  local copies, waits for them, and re-layouts  9.84 us (17%)
  other arithmetic  0.93 us (2%)
  between operations  0.75 us (1%)
    ppermute x8, starting transfers between devices, from_partner(): return lax.ppermute(block, axis, [(i, i ^ step) for i in range(count)])  17.1 us
    ppermute x8, waiting for transfers between devices, from_partner(): return lax.ppermute(block, axis, [(i, i ^ step) for i in range(count)])  11 us
    unnamed x16, local copies, waits for them, and re-layouts  7.71 us
    pallas_call x2, Pallas kernels, details(): call(detail_kernel, jax.ShapeDtypeStruct((species, DETAILS, lines), F32),...  6.55 us
    pallas_call x1, Pallas kernels, coarse_sets(): call(coarse_kernel, (jax.ShapeDtypeStruct((2, dense, LANES), F32), jax.Sh...  3.29 us
    ppermute x1, starting transfers between devices, shifted(): return lax.ppermute(block, axis, [(i, i + 1) for i in range(count - 1)])  3.17 us
    pallas_call x1, Pallas kernels, brick_tail(): call(tail_kernel, jax.ShapeDtypeStruct((species, HALO, lines), F32), in_s...  2.25 us
  transfers between devices with their start and end apart: 9, of which 5 were waited for; matrix products, arithmetic and copies ran while one was open for 10% of the time, Pallas kernels for 19%

profile of v1, /device:TPU:0, one launch (start us, length us, event | category | flops | bytes accessed | tf_op | source)
XLA Modules:
  0.0 56.9 jit_solution(10169888915652595877)
XLA Ops:
  0.6 0.0 copy-start
  0.6 1.9 %copy-done = f32[4,96,2048]{2,1,0:T(8,128)S(1)} copy-done((f32[4,96,2048]{2,1,0:T(8,128)S(1)}, f32[4,96,2048]{2,1,0:T(8,128)}, u32[]{:S(2)}) %copy-start) | copy-done | bytes 3145752
  2.5 0.0 copy-start.4
  2.5 0.7 %copy-done.4 = s32[1,2]{1,0:T(1,128)S(1)} copy-done((s32[1,2]{1,0:T(1,128)S(1)}, s32[1,2]{1,0:T(1,128)}, u32[]{:S(2)}) %copy-start.4) | copy-done | bytes 32
  3.2 0.0 copy-start.1
  3.2 0.0 copy-start.6
  3.2 0.0 copy-start.5
  3.2 2.2 %shard_map.59 = f32[4,16,2048]{2,1,0:T(8,128)} custom-call(s32[1,2]{1,0:T(1,128)S(1)} %copy-done.4, f32[4,96,2048]{2,1,0:T(8,128)S(1)} %copy-done), custom_call_target="tpu_custom_call" | custom-call | tf_op jit(solution)/shard_map/pallas_call | solution.py:55
  5.4 3.2 %collective-permute-start = (f32[4,16,2048]{2,1,0:T(8,128)}, f32[4,16,2048]{2,1,0:T(8,128)}, u32[]{:S(2)}, u32[]{:S(2)}) collective-permute-start(f32[4,16,2048]{2,1,0:T(8,128)} %shard_map.59), channel_id=1, source_target_pairs={{0,2},{2,4},{4,6},{6,8},{8,10},{10,12},{12,14},{14,16},{16,18},{18... | collective-permute-start | bytes 1572872 | tf_op jit(solution)/shard_map/ppermute | solution.py:400
  8.6 0.0 copy-done.1
  8.6 1.1 %constant_dynamic-slice_fusion = f32[4,64,1024]{2,1,0:T(8,128)} fusion(f32[4,96,2048]{2,1,0:T(8,128)S(1)} %copy-done.1, s32[]{:T(128)S(6)} %select_n.29), kind=kLoop, calls=%fused_computation.3 | loop fusion | bytes 2097156 | tf_op jit(solution)/shard_map/dynamic_slice | solution.py:421
  9.7 2.3 %collective-permute-start.2 = (f32[4,64,1024]{2,1,0:T(8,128)}, f32[4,64,1024]{2,1,0:T(8,128)}, u32[]{:S(2)}, u32[]{:S(2)}) collective-permute-start(f32[4,64,1024]{2,1,0:T(8,128)} %constant_dynamic-slice_fusion), channel_id=1, source_target_pairs={{0,1},{1,0},{2,3},{3,2},{4,5},{5,4},{6,7},{7,6},{8,9},{9,8},{10,11... | collective-permute-start | bytes 3145736 | tf_op jit(solution)/shard_map/ppermute | solution.py:395
  12.0 0.0 copy-done.6
  12.1 0.1 broadcast_in_dim.2.widths
  12.1 0.0 copy-done.5
  12.1 0.9 %shard_map.58 = (f32[72,128]{1,0:T(8,128)S(1)}, f32[8,128]{1,0:T(8,128)S(1)}) custom-call(s32[1,2]{1,0:T(1,128)S(1)} %copy-done.5, f32[64,128]{1,0:T(8,128)S(1)} %broadcast_in_dim.2.widths), custom_call_target="tpu_custom_call" | custom-call | tf_op jit(solution)/shard_map/pallas_call | solution.py:139
  13.0 0.0 collective-permute-done.halo
  13.0 3.3 %shard_map.60 = (f32[2,168,128]{2,1,0:T(8,128)S(1)}, f32[4,16,2048]{2,1,0:T(8,128)S(1)}) custom-call(f32[72,128]{1,0:T(8,128)S(1)} %get-tuple-element.17.matrix, f32[8,128]{1,0:T(8,128)S(1)} %get-tuple-element.18.coarse_width, f32[4,16,2048]{2,1,0:T(8,128)} %collective-permute-done.halo, f32[4,96,2048]{2,1,0:T(8,128)S(1)} %copy-done.1), custom_call_target="tpu_custom_call" | custom-call | tf_op jit(solution)/shard_map/pallas_call | solution.py:181
  16.3 0.0 copy-start.2
  16.3 0.8 %copy-done.2 = f32[4,16,2048]{2,1,0:T(8,128)} copy-done((f32[4,16,2048]{2,1,0:T(8,128)}, f32[4,16,2048]{2,1,0:T(8,128)S(1)}, u32[]{:S(2)}) %copy-start.2) | copy-done | bytes 524312
  17.1 3.8 %collective-permute-start.3 = (f32[168,128]{1,0:T(8,128)S(1)}, f32[168,128]{1,0:T(8,128)S(1)}, u32[]{:S(2)}, u32[]{:S(2)}) collective-permute-start(f32[168,128]{1,0:T(8,128)S(1)} %dynamic-slice_bitcast_fusion), channel_id=1, source_target_pairs={{0,2},{2,0},{4,6},{6,4},{8,10},{10,8},{12,14},{14,12},{16,18},{18,... | collective-permute-start | bytes 258056 | tf_op jit(solution)/shard_map/ppermute | solution.py:395
  20.9 0.9 %collective-permute-done.3.other = f32[168,128]{1,0:T(8,128)S(1)} collective-permute-done((f32[168,128]{1,0:T(8,128)S(1)}, f32[168,128]{1,0:T(8,128)S(1)}, u32[]{:S(2)}, u32[]{:S(2)}) %collective-permute-start.3) | collective-permute-done | bytes 86048 | tf_op jit(solution)/shard_map/ppermute | solution.py:395
  21.9 0.1 shard_map.63
  22.0 2.8 %collective-permute-start.4 = (f32[168,128]{1,0:T(8,128)S(1)}, f32[168,128]{1,0:T(8,128)S(1)}, u32[]{:S(2)}, u32[]{:S(2)}) collective-permute-start(f32[168,128]{1,0:T(8,128)S(1)} %get-tuple-element.21.own), channel_id=1, source_target_pairs={{0,4},{2,6},{4,0},{6,2},{8,12},{10,14},{12,8},{14,10},{16,20},{18,... | collective-permute-start | bytes 258056 | tf_op jit(solution)/shard_map/ppermute | solution.py:395
  24.7 2.9 %collective-permute-done.4.other = f32[168,128]{1,0:T(8,128)S(1)} collective-permute-done((f32[168,128]{1,0:T(8,128)S(1)}, f32[168,128]{1,0:T(8,128)S(1)}, u32[]{:S(2)}, u32[]{:S(2)}) %collective-permute-start.4) | collective-permute-done | bytes 86048 | tf_op jit(solution)/shard_map/ppermute | solution.py:395
  27.6 0.1 shard_map.64
  27.7 2.8 %collective-permute-start.5 = (f32[168,128]{1,0:T(8,128)S(1)}, f32[168,128]{1,0:T(8,128)S(1)}, u32[]{:S(2)}, u32[]{:S(2)}) collective-permute-start(f32[168,128]{1,0:T(8,128)S(1)} %get-tuple-element.22.own), channel_id=1, source_target_pairs={{0,8},{2,10},{4,12},{6,14},{8,0},{10,2},{12,4},{14,6},{16,24},{18,... | collective-permute-start | bytes 258056 | tf_op jit(solution)/shard_map/ppermute | solution.py:395
  30.5 2.5 %collective-permute-done.5.other = f32[168,128]{1,0:T(8,128)S(1)} collective-permute-done((f32[168,128]{1,0:T(8,128)S(1)}, f32[168,128]{1,0:T(8,128)S(1)}, u32[]{:S(2)}, u32[]{:S(2)}) %collective-permute-start.5) | collective-permute-done | bytes 86048 | tf_op jit(solution)/shard_map/ppermute | solution.py:395
  32.9 0.1 shard_map.65
  33.0 3.1 %collective-permute-start.6 = (f32[168,128]{1,0:T(8,128)S(1)}, f32[168,128]{1,0:T(8,128)S(1)}, u32[]{:S(2)}, u32[]{:S(2)}) collective-permute-start(f32[168,128]{1,0:T(8,128)S(1)} %get-tuple-element.24.own), channel_id=1, source_target_pairs={{0,16},{2,18},{4,20},{6,22},{8,24},{10,26},{12,28},{14,30},{16,0},... | collective-permute-start | bytes 258056 | tf_op jit(solution)/shard_map/ppermute | solution.py:395
  36.1 2.5 %collective-permute-done.6.other = f32[168,128]{1,0:T(8,128)S(1)} collective-permute-done((f32[168,128]{1,0:T(8,128)S(1)}, f32[168,128]{1,0:T(8,128)S(1)}, u32[]{:S(2)}, u32[]{:S(2)}) %collective-permute-start.6) | collective-permute-done | bytes 86048 | tf_op jit(solution)/shard_map/ppermute | solution.py:395
  38.6 0.1 shard_map.66
  38.7 0.1 collective-permute-start.7
  38.8 1.0 %constant_dynamic-slice_fusion.1 = f32[4,16,1024]{2,1,0:T(8,128)S(1)} fusion(f32[4,16,2048]{2,1,0:T(8,128)} %copy-done.2, s32[]{:T(128)S(6)} %select_n.29), kind=kLoop, calls=%fused_computation.4 | loop fusion | bytes 524292 | tf_op jit(solution)/shard_map/dynamic_slice | solution.py:426
  39.8 1.6 %collective-permute-start.1 = (f32[4,16,1024]{2,1,0:T(8,128)S(1)}, f32[4,16,1024]{2,1,0:T(8,128)S(1)}, u32[]{:S(2)}, u32[]{:S(2)}) collective-permute-start(f32[4,16,1024]{2,1,0:T(8,128)S(1)} %constant_dynamic-slice_fusion.1), channel_id=1, source_target_pairs={{0,1},{1,0},{2,3},{3,2},{4,5},{5,4},{6,7},{7,6},{8,9},{9,8},{10,11... | collective-permute-start | bytes 786440 | tf_op jit(solution)/shard_map/ppermute | solution.py:395
  41.3 0.0 collective-permute-done.7
  41.3 0.9 %broadcast_select_fusion = (f32[288,128]{1,0:T(8,128)S(1)}, f32[288,128]{1,0:T(8,128)S(1)}) fusion(f32[288,128]{1,0:T(8,128)} %collective-permute-done.7, f32[288,128]{1,0:T(8,128)S(1)} %get-tuple-element.27, pred[]{:T(512)S(6)} %eq.7), kind=kLoop, calls=%fused_computation.1 | loop fusion | flops 73728 | bytes 589825 | tf_op jit(solution)/shard_map/jit(_where)/select_n | solution.py:450
  42.3 0.6 %collective-permute-start.8 = (f32[288,128]{1,0:T(8,128)S(1)}, f32[288,128]{1,0:T(8,128)S(1)}, u32[]{:S(2)}, u32[]{:S(2)}) collective-permute-start(f32[288,128]{1,0:T(8,128)S(1)} %get-tuple-element.34), channel_id=1, source_target_pairs={{0,1},{1,0},{2,3},{3,2},{4,5},{5,4},{6,7},{7,6},{8,9},{9,8},{10,11... | collective-permute-start | bytes 442376 | tf_op jit(solution)/shard_map/ppermute | solution.py:395
  42.8 0.0 copy-start.3
  42.8 1.0 %copy-done.3 = f32[4,16,2048]{2,1,0:T(8,128)S(1)} copy-done((f32[4,16,2048]{2,1,0:T(8,128)S(1)}, f32[4,16,2048]{2,1,0:T(8,128)}, u32[]{:S(2)}) %copy-start.3) | copy-done | bytes 524312
  43.9 2.7 %shard_map.61.rest_0_ = f32[4,60,2048]{2,1,0:T(8,128)S(1)} custom-call(s32[1]{0:T(128)} %bitcast.1.place, f32[72,128]{1,0:T(8,128)S(1)} %get-tuple-element.17.matrix, f32[4,16,2048]{2,1,0:T(8,128)S(1)} %copy-done.3, f32[4,96,2048]{2,1,0:T(8,128)S(1)} %copy-done.1), custom_call_target="tpu_custom_call" | custom-call | tf_op jit(solution)/shard_map/pallas_call | solution.py:227
  46.6 2.3 %collective-permute-done.1.extra = f32[4,16,1024]{2,1,0:T(8,128)S(1)} collective-permute-done((f32[4,16,1024]{2,1,0:T(8,128)S(1)}, f32[4,16,1024]{2,1,0:T(8,128)S(1)}, u32[]{:S(2)}, u32[]{:S(2)}) %collective-permute-start.1) | collective-permute-done | bytes 262176 | tf_op jit(solution)/shard_map/ppermute | solution.py:395
  48.9 0.0 collective-permute-done.2.brick
  48.9 3.8 %shard_map.62 = f32[4,60,2048]{2,1,0:T(8,128)S(1)} custom-call(s32[1]{0:T(128)} %bitcast.place, f32[72,128]{1,0:T(8,128)S(1)} %get-tuple-element.17.matrix, f32[4,16,1024]{2,1,0:T(8,128)S(1)} %collective-permute-done.1.extra, f32[4,64,1024]{2,1,0:T(8,128)} %collective-permute-done.2.brick, ...), custom_call_target="tpu_custom_call", output_to_operand_aliasing={{}: (4, {})} | custom-call | tf_op jit(solution)/shard_map/pallas_call | solution.py:227
  52.8 2.5 %copy.7 = f32[4,60,2048]{2,0,1:T(4,128)} copy(f32[4,60,2048]{2,1,0:T(8,128)S(1)} %shard_map.62) | data formatting | bytes 3932160
  55.3 0.0 collective-permute-done.8.other
  55.3 0.8 %shard_map.67 = (f32[4,4,2048]{2,1,0:T(4,128)}, f32[4,5,2048]{2,1,0:T(8,128)S(1)}) custom-call(f32[288,128]{1,0:T(8,128)S(1)} %get-tuple-element.35.own, f32[288,128]{1,0:T(8,128)S(1)} %collective-permute-done.8.other), custom_call_target="tpu_custom_call" | custom-call | tf_op jit(solution)/shard_map/pallas_call | solution.py:381
  56.1 0.8 %copy.8 = f32[4,5,2048]{2,0,1:T(4,128)} copy(f32[4,5,2048]{2,1,0:T(8,128)S(1)} %get-tuple-element.33) | data formatting | bytes 327680
  (1 shorter events, 0.0 us)
Async XLA Ops:
  0.6 1.9 %copy-start = (f32[4,96,2048]{2,1,0:T(8,128)S(1)}, f32[4,96,2048]{2,1,0:T(8,128)}, u32[]{:S(2)}) copy-start(f32[4,96,2048]{2,1,0:T(8,128)} %brick.1) | copy-start | bytes 9437188
  2.5 0.7 %copy-start.4 = (s32[1,2]{1,0:T(1,128)S(1)}, s32[1,2]{1,0:T(1,128)}, u32[]{:S(2)}) copy-start(s32[1,2]{1,0:T(1,128)} %edges.3) | copy-start | bytes 28
  3.2 5.4 %copy-start.1 = (f32[4,96,2048]{2,1,0:T(8,128)S(1)}, f32[4,96,2048]{2,1,0:T(8,128)}, u32[]{:S(2)}) copy-start(f32[4,96,2048]{2,1,0:T(8,128)} %brick.1) | copy-start | bytes 9437188
  3.2 8.9 %copy-start.6 = (f32[64]{0:T(128)S(1)}, f32[64]{0:T(128)}, u32[]{:S(2)}) copy-start(f32[64]{0:T(128)} %param.5) | copy-start | bytes 772
  3.2 8.9 %copy-start.5 = (s32[1,2]{1,0:T(1,128)S(1)}, s32[1,2]{1,0:T(1,128)}, u32[]{:S(2)}) copy-start(s32[1,2]{1,0:T(1,128)} %edges.3) | copy-start | bytes 28
  5.4 7.6 %collective-permute-start = (f32[4,16,2048]{2,1,0:T(8,128)}, f32[4,16,2048]{2,1,0:T(8,128)}, u32[]{:S(2)}, u32[]{:S(2)}) collective-permute-start(f32[4,16,2048]{2,1,0:T(8,128)} %shard_map.59), channel_id=1, source_target_pairs={{0,2},{2,4},{4,6},{6,8},{8,10},{10,12},{12,14},{14,16},{16,18},{18... | collective-permute-start | bytes 1572872 | tf_op jit(solution)/shard_map/ppermute | solution.py:400
  9.7 39.2 %collective-permute-start.2 = (f32[4,64,1024]{2,1,0:T(8,128)}, f32[4,64,1024]{2,1,0:T(8,128)}, u32[]{:S(2)}, u32[]{:S(2)}) collective-permute-start(f32[4,64,1024]{2,1,0:T(8,128)} %constant_dynamic-slice_fusion), channel_id=1, source_target_pairs={{0,1},{1,0},{2,3},{3,2},{4,5},{5,4},{6,7},{7,6},{8,9},{9,8},{10,11... | collective-permute-start | bytes 3145736 | tf_op jit(solution)/shard_map/ppermute | solution.py:395
  16.3 0.8 %copy-start.2 = (f32[4,16,2048]{2,1,0:T(8,128)}, f32[4,16,2048]{2,1,0:T(8,128)S(1)}, u32[]{:S(2)}) copy-start(f32[4,16,2048]{2,1,0:T(8,128)S(1)} %get-tuple-element.19.extra) | copy-start | bytes 1572868
  17.1 4.7 %collective-permute-start.3 = (f32[168,128]{1,0:T(8,128)S(1)}, f32[168,128]{1,0:T(8,128)S(1)}, u32[]{:S(2)}, u32[]{:S(2)}) collective-permute-start(f32[168,128]{1,0:T(8,128)S(1)} %dynamic-slice_bitcast_fusion), channel_id=1, source_target_pairs={{0,2},{2,0},{4,6},{6,4},{8,10},{10,8},{12,14},{14,12},{16,18},{18,... | collective-permute-start | bytes 258056 | tf_op jit(solution)/shard_map/ppermute | solution.py:395
  22.0 5.6 %collective-permute-start.4 = (f32[168,128]{1,0:T(8,128)S(1)}, f32[168,128]{1,0:T(8,128)S(1)}, u32[]{:S(2)}, u32[]{:S(2)}) collective-permute-start(f32[168,128]{1,0:T(8,128)S(1)} %get-tuple-element.21.own), channel_id=1, source_target_pairs={{0,4},{2,6},{4,0},{6,2},{8,12},{10,14},{12,8},{14,10},{16,20},{18,... | collective-permute-start | bytes 258056 | tf_op jit(solution)/shard_map/ppermute | solution.py:395
  27.7 5.3 %collective-permute-start.5 = (f32[168,128]{1,0:T(8,128)S(1)}, f32[168,128]{1,0:T(8,128)S(1)}, u32[]{:S(2)}, u32[]{:S(2)}) collective-permute-start(f32[168,128]{1,0:T(8,128)S(1)} %get-tuple-element.22.own), channel_id=1, source_target_pairs={{0,8},{2,10},{4,12},{6,14},{8,0},{10,2},{12,4},{14,6},{16,24},{18,... | collective-permute-start | bytes 258056 | tf_op jit(solution)/shard_map/ppermute | solution.py:395
  33.0 5.6 %collective-permute-start.6 = (f32[168,128]{1,0:T(8,128)S(1)}, f32[168,128]{1,0:T(8,128)S(1)}, u32[]{:S(2)}, u32[]{:S(2)}) collective-permute-start(f32[168,128]{1,0:T(8,128)S(1)} %get-tuple-element.24.own), channel_id=1, source_target_pairs={{0,16},{2,18},{4,20},{6,22},{8,24},{10,26},{12,28},{14,30},{16,0},... | collective-permute-start | bytes 258056 | tf_op jit(solution)/shard_map/ppermute | solution.py:395
  38.7 2.7 %collective-permute-start.7 = (f32[288,128]{1,0:T(8,128)S(1)}, f32[288,128]{1,0:T(8,128)}, u32[]{:S(2)}, u32[]{:S(2)}) collective-permute-start(f32[288,128]{1,0:T(8,128)S(1)} %get-tuple-element.28), channel_id=1, source_target_pairs={{0,2},{2,0},{4,6},{6,4},{8,10},{10,8},{12,14},{14,12},{16,18},{18,... | collective-permute-start | bytes 442376 | tf_op jit(solution)/shard_map/ppermute | solution.py:395
  39.8 9.2 %collective-permute-start.1 = (f32[4,16,1024]{2,1,0:T(8,128)S(1)}, f32[4,16,1024]{2,1,0:T(8,128)S(1)}, u32[]{:S(2)}, u32[]{:S(2)}) collective-permute-start(f32[4,16,1024]{2,1,0:T(8,128)S(1)} %constant_dynamic-slice_fusion.1), channel_id=1, source_target_pairs={{0,1},{1,0},{2,3},{3,2},{4,5},{5,4},{6,7},{7,6},{8,9},{9,8},{10,11... | collective-permute-start | bytes 786440 | tf_op jit(solution)/shard_map/ppermute | solution.py:395
  42.3 13.0 %collective-permute-start.8 = (f32[288,128]{1,0:T(8,128)S(1)}, f32[288,128]{1,0:T(8,128)S(1)}, u32[]{:S(2)}, u32[]{:S(2)}) collective-permute-start(f32[288,128]{1,0:T(8,128)S(1)} %get-tuple-element.34), channel_id=1, source_target_pairs={{0,1},{1,0},{2,3},{3,2},{4,5},{5,4},{6,7},{7,6},{8,9},{9,8},{10,11... | collective-permute-start | bytes 442376 | tf_op jit(solution)/shard_map/ppermute | solution.py:395
  42.8 1.0 %copy-start.3 = (f32[4,16,2048]{2,1,0:T(8,128)S(1)}, f32[4,16,2048]{2,1,0:T(8,128)}, u32[]{:S(2)}) copy-start(f32[4,16,2048]{2,1,0:T(8,128)} %copy-done.2) | copy-start | bytes 1572868

commit v2 on v1

v2 whole, which is shorter than its diff:
```python
import functools

import jax
import jax.numpy as jnp
from jax import lax
from jax.experimental import pallas as pl
from jax.experimental.pallas import tpu as pltpu
from jax.sharding import PartitionSpec as P

TILE = 64
HALO = 16
LEVELS = 4
COARSE = 5
DETAILS = TILE - COARSE + 1
LANES = 128
SUB = 8
HELD = TILE + HALO
FIRST = 48
SECOND = TILE - FIRST
F32 = jnp.float32
BF16 = jnp.bfloat16
HIGHEST = lax.Precision.HIGHEST


def call(kernel, out_shape, *, vmem=8 << 20, cost=None, **kw):
    params = pltpu.CompilerParams(vmem_limit_bytes=vmem)
    if cost is not None:
        kw["cost_estimate"] = pl.CostEstimate(flops=cost, bytes_accessed=cost // 100, transcendentals=0)
    return pl.pallas_call(kernel, out_shape=out_shape, compiler_params=params, **kw)


VMEM_SPEC = pl.BlockSpec(memory_space=pltpu.VMEM)
SMEM_SPEC = pl.BlockSpec(memory_space=pltpu.SMEM)
HBM_SPEC = pl.BlockSpec(memory_space=pltpu.HBM)


def leave_kernel(edges, field, tail, *away):
    species, _, lines = tail.shape
    start = edges[0, 1] - edges[0, 0] - HALO
    rest = start & (SUB - 1)
    whole = pl.multiple_of(start - rest, SUB)
    for sp in range(species):
        rows = field[sp, pl.ds(whole, HALO + SUB), :]
        tail[sp] = pltpu.roll(rows, (HALO + SUB - rest) % (HALO + SUB), 0)[:HALO]
    for out in away:
        width = out.shape[2]
        other = pl.multiple_of((1 - lax.axis_index("cross")) * width, LANES)
        for sp in range(species):
            out[sp] = field[sp, :FIRST, pl.ds(other, width)]


def leaving(edges, field, width):
    species, _, lines = field.shape
    shapes = [jax.ShapeDtypeStruct((species, HALO, lines), F32)]
    if width < lines:
        shapes.append(jax.ShapeDtypeStruct((species, FIRST, width), F32))
    return call(
        leave_kernel,
        tuple(shapes),
        in_specs=[SMEM_SPEC, VMEM_SPEC],
        out_specs=(VMEM_SPEC,) * len(shapes),
    )(edges, field)


PAD = 32


def matrix_kernel(edges, widths, factors, coarse, coarse_width, nodes, cell, low, main, up, load, stored):
    slab = lax.axis_index("slab")
    shift = edges[0, 0] - slab * TILE
    rows, lanes = nodes.shape[1], nodes.shape[0] * LANES
    node = lax.broadcasted_iota(jnp.int32, (rows, lanes), 0)
    lane = lax.broadcasted_iota(jnp.int32, (rows, lanes), 1)
    column = lane % HELD
    later = column - FIRST
    held = jnp.where(column < FIRST, column + shift, jnp.where(later < shift, later, column))
    plain = lane - 2 * LANES
    from_halo = jnp.where((slab == 0) & (plain < HALO), plain + TILE, plain - HALO + shift)
    grouped = (lane < 3 * HELD) & (column <= TILE)
    held = jnp.where(lane < 2 * LANES, jnp.where(grouped, held, -1), jnp.where(plain < HELD, from_halo, -1))
    chosen = ((held == node) & (node <= TILE)).astype(F32)
    for j in range(lanes // LANES):
        nodes[j] = chosen[:, j * LANES : (j + 1) * LANES]
    cell[...] = jnp.zeros_like(cell)
    cell[:TILE] = widths[...]
    for ref in (low, up, load):
        ref[...] = jnp.zeros_like(ref)
    main[...] = jnp.ones_like(main)
    stored[...] = jnp.zeros_like(stored)
    wide = lambda x: jnp.concatenate([x] * (lanes // LANES), axis=1)
    placed = 0
    pairs = TILE // 2
    for _ in range(LEVELS):
        size = -(-(pairs + 1) // SUB) * SUB
        here = pl.ds(PAD, size)
        inside = lax.broadcasted_iota(jnp.int32, (size, LANES), 0) < pairs
        left = cell[pl.ds(0, size, stride=2)]
        right = cell[pl.ds(1, size, stride=2)]
        total = left + right
        safe = jnp.where(inside, total, 1.0)
        even, odd, after = [
            jnp.concatenate([nodes[j, pl.ds(i, size, stride=2)] for j in range(lanes // LANES)], axis=1)
            for i in range(3)
        ]
        inverse = 1.0 / safe
        detail = odd - (wide(right * inverse) * even + wide(left * inverse) * after)
        detail = jnp.where(wide(inside), detail, 0.0)
        stored[placed : placed + pairs] = detail[:pairs]
        placed += pairs
        load[here] = wide(right / 6.0 + left / 3.0) * detail
        load[pl.ds(PAD - 1, 1)] = jnp.zeros((1, lanes), F32)
        grown = wide(left / 6.0 + right / 3.0) * detail + load[pl.ds(PAD - 1, size)]
        up[here] = total
        before = up[pl.ds(PAD - 1, size)]
        held_rows = lax.broadcasted_iota(jnp.int32, (size, LANES), 0) <= pairs
        diag = jnp.where(held_rows, (before + total) / 3.0, 1.0)
        lower = jnp.where(held_rows, before / 6.0, 0.0)
        upper = total / 6.0
        step = 1
        while step <= pairs:
            low[here] = lower
            up[here] = upper
            main[here] = 1.0 / diag
            load[here] = grown
            back = pl.ds(PAD - step, size)
            fore = pl.ds(PAD + step, size)
            alpha = -lower * main[back]
            gamma = -upper * main[fore]
            diag = diag + alpha * up[back] + gamma * low[fore]
            grown = grown + wide(alpha) * load[back] + wide(gamma) * load[fore]
            lower = alpha * low[back]
            upper = gamma * up[fore]
            step *= 2
        result = even + grown * wide(1.0 / diag)
        result = jnp.where(wide(held_rows), result, 0.0)
        nodes[...] = jnp.zeros_like(nodes)
        for j in range(lanes // LANES):
            nodes[j, :size] = result[:, j * LANES : (j + 1) * LANES]
        cell[...] = jnp.zeros_like(cell)
        cell[:size] = total
        pairs //= 2
    coarse[...] = nodes[2, :SUB]
    coarse_width[...] = cell[:SUB]
    matrix = stored[:, : 2 * LANES]
    lane = lax.broadcasted_iota(jnp.int32, matrix.shape, 1)
    for i in range(3):
        term = matrix.astype(BF16)
        matrix = matrix - term.astype(F32)
        factors[i * TILE : (i + 1) * TILE] = jnp.where(lane < (3 - i) * HELD, term.astype(F32), 0.0).astype(BF16)


def tile_matrix(edges, cell_width):
    widths = jnp.broadcast_to(cell_width[:, None], (TILE, LANES))
    narrow = pltpu.VMEM((PAD + 40 + PAD, LANES), F32)
    broad = pltpu.VMEM((PAD + 40 + PAD, 3 * LANES), F32)
    return call(
        matrix_kernel,
        (
            jax.ShapeDtypeStruct((3 * TILE, 2 * LANES), BF16),
            jax.ShapeDtypeStruct((SUB, LANES), F32),
            jax.ShapeDtypeStruct((SUB, LANES), F32),
        ),
        in_specs=[SMEM_SPEC, VMEM_SPEC],
        out_specs=(VMEM_SPEC,) * 3,
        scratch_shapes=[
            pltpu.VMEM((3, 88, LANES), F32),
            pltpu.VMEM((88, LANES), F32),
            narrow,
            narrow,
            narrow,
            broad,
            pltpu.VMEM((TILE, 3 * LANES), F32),
        ],
    )(edges, widths)


def to_dense(result, turned, sets, sp, species):
    blocks = result.shape[1] // LANES
    per = blocks // 2
    for t in range(blocks):
        turned[t * SUB : (t + 1) * SUB] = result[:, t * LANES : (t + 1) * LANES]
    for half in range(2):
        for k in range(COARSE):
            at = ((half * COARSE + k) * species + sp) * per
            sets[pl.ds(at if isinstance(sp, int) else pl.multiple_of(at, per), per)] = turned[
                pl.ds(half * per * SUB + k, per, stride=SUB)
            ]


def brick_kernel(weights, coarse_width, field, sets, turned):
    sp = pl.program_id(0)
    slab = lax.axis_index("slab")
    own = weights[...]
    result = jnp.dot(own[:, HALO:HELD], field[0, :TILE], precision=HIGHEST, preferred_element_type=F32)
    row = jnp.where(slab == 0, field[0, TILE:HELD], 0.0)
    result += jnp.dot(own[:, :HALO], row, precision=HIGHEST, preferred_element_type=F32)
    to_dense(result, turned, sets, sp, pl.num_programs(0))

    @pl.when(sp == 0)
    def _():
        sets[sets.shape[0] - SUB :] = coarse_width[...]


def brick_part(weights, coarse_width, field):
    species, _, lines = field.shape
    dense = COARSE * species * lines // LANES + SUB
    return call(
        brick_kernel,
        jax.ShapeDtypeStruct((dense, LANES), F32),
        grid=(species,),
        in_specs=[
            pl.BlockSpec((SUB, LANES), lambda i: (0, 0)),
            pl.BlockSpec((SUB, LANES), lambda i: (0, 0)),
            pl.BlockSpec((1, HELD, lines), lambda i: (i, 0, 0)),
        ],
        out_specs=pl.BlockSpec((dense, LANES), lambda i: (0, 0)),
        scratch_shapes=[pltpu.VMEM((lines // LANES * SUB, LANES), F32)],
    )(weights, coarse_width, field)


def halo_kernel(weights, halo, part, own_half, other_half, turned, fresh):
    species = halo.shape[0]
    slab = lax.axis_index("slab")
    own = weights[:, :HALO]
    for sp in range(species):
        result = jnp.dot(own, halo[sp], precision=HIGHEST, preferred_element_type=F32)
        to_dense(result, turned, fresh, sp, species)
    rows = fresh.shape[0] // 2
    for ref, half in ((own_half, slab & 1), (other_half, 1 - (slab & 1))):
        here = pl.ds(pl.multiple_of(half * rows, SUB), rows)
        ref[:rows] = part[here] + jnp.where(slab == 0, 0.0, fresh[here])
        ref[rows:] = part[2 * rows :]


def coarse_sets(weights, halo, part):
    lines = halo.shape[2]
    rows = part.shape[0] - SUB
    half = jax.ShapeDtypeStruct((rows // 2 + SUB, LANES), F32)
    return call(
        halo_kernel,
        (half, half),
        in_specs=[VMEM_SPEC] * 3,
        out_specs=(VMEM_SPEC,) * 2,
        scratch_shapes=[
            pltpu.VMEM((lines // LANES * SUB, LANES), F32),
            pltpu.VMEM((rows, LANES), F32),
        ],
    )(weights, halo, part)


def later_nodes(shift, halo, brick):
    rows = jnp.concatenate([halo, brick], axis=0)
    count = rows.shape[0]
    return pltpu.roll(rows, (count - HALO + shift) % count, 0)


BRICK_END = TILE + SUB


def rest_kernel(edges, halo, field, out):
    species = halo.shape[0]
    shift = edges[0, 0] - lax.axis_index("slab") * TILE
    width = out.shape[1]
    other = pl.ds(pl.multiple_of((1 - lax.axis_index("cross")) * width, LANES), width)
    last = species * SECOND
    out[last:] = jnp.zeros((out.shape[0] - last, width), F32)
    for sp in range(species):
        rows = later_nodes(shift, halo[sp, :, other], field[sp, FIRST:BRICK_END, other])
        out[sp * SECOND : (sp + 1) * SECOND] = rows[:SECOND]
        out[last + sp : last + sp + 1] = rows[SECOND : SECOND + 1]


def rest_away(edges, halo, field, width):
    species = halo.shape[0]
    rows = species * SECOND + -(-species // SUB) * SUB
    return call(
        rest_kernel,
        jax.ShapeDtypeStruct((rows, width), F32),
        in_specs=[SMEM_SPEC, VMEM_SPEC, VMEM_SPEC],
        out_specs=VMEM_SPEC,
        cost=400_000_000,
    )(edges, halo, field)


def detail_kernel(local, place, factors, first, second, *rest):
    out, wide = rest[-2:]
    species = out.shape[1]
    width = out.shape[2]
    weights = factors[:, : 3 * HELD]
    for sp in range(species):
        if local:
            more = later_nodes(place[1], first[sp], second[sp, FIRST:BRICK_END])
            pieces = [second[sp, :FIRST], more[: SECOND + HALO]]
        else:
            last = species * SECOND
            end = pltpu.roll(second[last : last + SUB], (SUB - sp) % SUB, 0)
            pieces = [first[sp], second[sp * SECOND : (sp + 1) * SECOND], end, end]
        left = jnp.concatenate(pieces, axis=0)
        terms = []
        for _ in range(3):
            terms.append(left.astype(BF16))
            left = left - terms[-1].astype(F32)
        stack = jnp.concatenate(terms, axis=0)
        result = jnp.dot(weights, stack, preferred_element_type=F32)
        result = result[:TILE] + result[TILE : 2 * TILE] + result[2 * TILE :]
        for t in range(width // LANES):
            wide[t, pl.ds(sp, TILE, stride=species)] = result[:, t * LANES : (t + 1) * LANES]
    for t in range(width // LANES):
        for k in range(DETAILS):
            out[k, :, t * LANES : (t + 1) * LANES] = wide[t, k * species : (k + 1) * species]


def details(local, place, factors, first, second, width, species, lines, onto=None):
    chunk = min(width, 512)
    steps = width // chunk

    def at(own, i, place):
        return place[0] * steps + i if own else i

    whole = first.shape[2] == lines
    if local:
        specs = [
            pl.BlockSpec((species, HALO, chunk), lambda i, place: (0, 0, at(whole, i, place))),
            pl.BlockSpec((species, HELD, chunk), lambda i, place: (0, 0, at(whole, i, place))),
        ]
    else:
        specs = [
            pl.BlockSpec((species, FIRST, chunk), lambda i, place: (0, 0, i)),
            pl.BlockSpec((second.shape[0], chunk), lambda i, place: (0, i)),
        ]
    specs = [pl.BlockSpec((3 * TILE, 2 * LANES), lambda i, place: (0, 0))] + specs
    operands = [place, factors, first, second]
    alias = {}
    if onto is not None:
        specs.append(HBM_SPEC)
        operands.append(onto)
        alias = {4: 0}
    return call(
        functools.partial(detail_kernel, local),
        jax.ShapeDtypeStruct((DETAILS, species, lines), F32),
        grid_spec=pltpu.PrefetchScalarGridSpec(
            num_scalar_prefetch=1,
            grid=(steps,),
            in_specs=specs,
            out_specs=pl.BlockSpec((DETAILS, species, chunk), lambda i, place: (0, 0, at(True, i, place))),
            scratch_shapes=[pltpu.VMEM((chunk // LANES, TILE * species, LANES), F32)],
        ),
        input_output_aliases=alias,
        cost=2_000_000_000,
    )(*operands)


def merged(lower, upper):
    lower_values, lower_widths = lower
    upper_values, upper_widths = upper
    shared = 0.5 * (lower_values[-1] + upper_values[0])
    values = lower_values[:-1] + [shared] + upper_values[1:]
    widths = lower_widths + upper_widths
    left, right = widths[0::2], widths[1::2]
    pairs = len(left)
    total = [a + b for a, b in zip(left, right)]
    detail = []
    for i in range(pairs):
        inverse = 1.0 / total[i]
        detail.append(
            values[2 * i + 1] - ((right[i] * inverse) * values[2 * i] + (left[i] * inverse) * values[2 * i + 2])
        )
    loads = []
    for k in range(pairs + 1):
        term = None
        if k < pairs:
            term = (left[k] / 6.0 + right[k] / 3.0) * detail[k]
        if k > 0:
            other = (right[k - 1] / 6.0 + left[k - 1] / 3.0) * detail[k - 1]
            term = other if term is None else term + other
        loads.append(term)
    ratio, solved = [], []
    for k in range(pairs + 1):
        diag = (total[k - 1] if k else 0.0) + (total[k] if k < pairs else 0.0)
        diag = diag / 3.0
        if k:
            off = total[k - 1] / 6.0
            pivot = 1.0 / (diag - off * ratio[-1])
            solved.append((loads[k] - off * solved[-1]) * pivot)
        else:
            pivot = 1.0 / diag
            solved.append(loads[k] * pivot)
        if k < pairs:
            ratio.append(total[k] / 6.0 * pivot)
    for k in range(pairs - 1, -1, -1):
        solved[k] = solved[k] - ratio[k] * solved[k + 1]
    coarse = [values[2 * k] + solved[k] for k in range(pairs + 1)]
    return coarse, detail, total


def values_at(ref, first, rows):
    return [ref[pl.ds(first + k * rows, rows)] for k in range(COARSE)]


def widths_at(ref, first):
    return [ref[pl.ds(first + i, 1)] for i in range(COARSE - 1)]


def put(ref, first, rows, values):
    for k, value in enumerate(values):
        ref[pl.ds(first + k * rows, rows)] = value


def put_widths(ref, first, widths):
    put(ref, first, 1, widths)
    ref[first + COARSE - 1 : first + SUB] = jnp.zeros((SUB - COARSE + 1, LANES), F32)


def in_order(upper_side, mine, theirs):
    def pick(first, second):
        return [jnp.where(upper_side, a, b) for a, b in zip(first, second)]

    lower = (pick(theirs[0], mine[0]), pick(theirs[1], mine[1]))
    upper = (pick(mine[0], theirs[0]), pick(mine[1], theirs[1]))
    return merged(lower, upper)


def merge_kernel(level, depth, rows, swapped, *refs):
    slab = lax.axis_index("slab")
    core = slab & 1
    chip = slab & ~1
    upper_side = (slab >> level) & 1 == 1
    last = level == depth - 1
    set_rows = COARSE * rows + SUB
    detail_rows = (COARSE - 1) * rows
    own, other = refs[0], refs[1]
    outs = refs[-2:]

    def state(ref):
        values = values_at(ref, 0, rows) + widths_at(ref, COARSE * rows)
        if level > 0:
            values += [ref[pl.ds(set_rows + i * rows, rows)] for i in range(COARSE - 1)]
        if level > 1:
            values += [ref[pl.ds(set_rows + detail_rows + i * rows, rows)] for i in range(COARSE - 1)]
        return values

    held = state(own)
    if swapped and last:
        home = core == lax.axis_index("cross")
        held = [jnp.where(home, a, b) for a, b in zip(held, state(refs[2]))]
    mine = (held[:COARSE], held[COARSE : 2 * COARSE - 1])
    odd = held[2 * COARSE - 1 : 3 * COARSE - 2]
    even = held[3 * COARSE - 2 :]
    theirs = (values_at(other, 0, rows), widths_at(other, COARSE * rows))

    def pick(first, second):
        return [jnp.where(upper_side, a, b) for a, b in zip(first, second)]

    lower = (pick(theirs[0], mine[0]), pick(theirs[1], mine[1]))
    upper = (pick(mine[0], theirs[0]), pick(mine[1], theirs[1]))
    coarse, detail, widths = merged(lower, upper)
    if level == 0:
        odd = detail
    else:
        keep = ((chip >> level) & 1 == 1) & (chip & ((1 << level) - 1) == 0)
        if last:
            keep = keep | (chip == 0)
        even = even if level > 1 else [0.0] * (COARSE - 1)
        even = [jnp.where(keep, a, b) for a, b in zip(detail, even)]
    if last:
        here, away = outs
        put(here, 0, rows, coarse)
        put(away, 0, rows, coarse)
        put(here, COARSE * rows, rows, [jnp.where(core == 0, a, b) for a, b in zip(even, odd)])
        put(away, COARSE * rows, rows, [jnp.where(core == 0, b, a) for a, b in zip(even, odd)])
        return
    send, carried = outs
    for ref in (send, carried):
        put(ref, 0, rows, coarse)
        put_widths(ref, COARSE * rows, widths)
    put(carried, set_rows, rows, odd)
    if level > 0:
        put(carried, set_rows + detail_rows, rows, even)


def merge(level, depth, rows, swapped, *operands):
    set_rows = COARSE * rows + SUB
    detail_rows = (COARSE - 1) * rows
    if level == depth - 1:
        sizes = ((2 * COARSE - 1) * rows,) * 2
    else:
        sizes = (set_rows, set_rows + min(level + 1, 2) * detail_rows)
    return call(
        functools.partial(merge_kernel, level, depth, rows, swapped),
        tuple(jax.ShapeDtypeStruct((size, LANES), F32) for size in sizes),
        in_specs=[VMEM_SPEC] * len(operands),
        out_specs=(VMEM_SPEC,) * 2,
    )(*operands)


def finish_kernel(own, other, tree, final, turned):
    core = lax.axis_index("slab") & 1
    species, _, lines = tree.shape
    width = lines // 2
    per = width // LANES
    group = COARSE - 1
    for block, ref in ((core, own), (1 - core, other)):

        def lanes(t):
            return pl.ds(pl.multiple_of(block * width + t * LANES, LANES), LANES)

        for k in range(COARSE):
            for sp in range(species):
                turned[pl.ds(sp, per, stride=species)] = ref[(k * species + sp) * per : (k * species + sp + 1) * per]
            for t in range(per):
                final[k, :, lanes(t)] = turned[t * species : (t + 1) * species]
        for sp in range(species):
            for i in range(group):
                at = ((COARSE + i) * species + sp) * per
                turned[pl.ds(i, per, stride=group)] = ref[at : at + per]
            for t in range(per):
                tree[sp, :, lanes(t)] = turned[t * group : (t + 1) * group]


def finish(own, other, species, lines):
    return call(
        finish_kernel,
        (
            jax.ShapeDtypeStruct((species, COARSE - 1, lines), F32),
            jax.ShapeDtypeStruct((COARSE, species, lines), F32),
        ),
        in_specs=[VMEM_SPEC] * 2,
        out_specs=(VMEM_SPEC,) * 2,
        scratch_shapes=[pltpu.VMEM((lines // 2 // LANES * SUB, LANES), F32)],
    )(own, other)


def from_partner(block, axis, step):
    count = lax.axis_size(axis)
    return lax.ppermute(block, axis, [(i, i ^ step) for i in range(count)])


def shifted(block, axis):
    count = lax.axis_size(axis)
    return lax.ppermute(block, axis, [(i, i + 1) for i in range(count - 1)])


def exchanged(block, axis):
    species, rows, lines = block.shape
    count = lax.axis_size(axis)
    parts = block.reshape(species, rows, count, lines // count)
    return lax.all_to_all(parts, axis, split_axis=2, concat_axis=2, tiled=True).reshape(block.shape)


def last_routes(slabs):
    partner, own = [], []
    for s in range(slabs):
        for c in range(2):
            home = (s & 1) == c
            target = (s, c) if home else (s ^ 1, 1 - c)
            partner.append((s * 2 + c, (target[0] ^ (slabs // 2)) * 2 + target[1]))
            if not home:
                own.append((s * 2 + c, target[0] * 2 + target[1]))
    return partner, own


def on_device(sim_field, brick_edges, cell_width):
    species, _, lines = sim_field.shape
    cross_count = lax.axis_size("cross")
    slabs = lax.axis_size("slab")
    cross = lax.axis_index("cross")
    core = lax.axis_index("slab") % 2
    depth = slabs.bit_length() - 1
    width = lines // cross_count
    rows = species * (lines // 2) // LANES
    swapped = cross_count == 2
    both = ("slab", "cross")

    if swapped:
        tail, first_away = leaving(brick_edges, sim_field, width)
        first_in = from_partner(first_away, "cross", 1)
    else:
        (tail,) = leaving(brick_edges, sim_field, lines)
    halo = shifted(tail, "slab")
    factors, weights, coarse_width = tile_matrix(brick_edges, cell_width)
    part = brick_part(weights, coarse_width, sim_field)
    halo, part, factors = lax.optimization_barrier((halo, part, factors))
    own_half, other_half = coarse_sets(weights, halo, part)
    shift = brick_edges[0, 0] - lax.axis_index("slab") * TILE
    if swapped:
        rest_in = from_partner(rest_away(brick_edges, halo, sim_field, width), "cross", 1)

    send, carried = other_half, own_half
    for level in range(depth):
        if swapped and level == depth - 1:
            partner_route, own_route = last_routes(slabs)
            send, carried, rest_in = lax.optimization_barrier((send, carried, rest_in))
            operands = (carried, lax.ppermute(send, both, partner_route), lax.ppermute(carried, both, own_route))
        else:
            operands = (carried, from_partner(send, "slab", 1 << level))
        send, carried = merge(level, depth, rows, swapped, *operands)
    here_set, away_set = send, carried
    partner_set = from_partner(away_set, "slab", 1)

    if swapped:
        tree_detail, coarse_final = finish(here_set, partner_set, species, lines)
        coarse_final = coarse_final.transpose(1, 0, 2)
        here, there = jnp.stack([cross, shift]), jnp.stack([1 - cross, shift])
        tile_detail = details(True, here, factors, halo, sim_field, width, species, lines)
        tile_detail = details(False, there, factors, first_in, rest_in, width, species, lines, tile_detail)
    else:
        first = jnp.where(core == 0, here_set, partner_set)
        second = jnp.where(core == 0, partner_set, here_set)
        ended = jnp.stack([first, second]).reshape(2, 2 * COARSE - 1, species, lines // 2)
        ended = ended.transpose(2, 1, 0, 3).reshape(species, 2 * COARSE - 1, lines)
        ended = exchanged(ended, "cross")
        coarse_final, tree_detail = ended[:, :COARSE], ended[:, COARSE:]
        moved = exchanged(jnp.concatenate([halo, sim_field[:, :HELD]], axis=1), "cross")
        place = jnp.stack([jnp.zeros_like(shift), shift])
        tile_detail = details(True, place, factors, moved[:, :HALO], moved[:, HALO:], lines, species, lines)
    return (tile_detail.transpose(1, 0, 2), tree_detail, coarse_final)


def solution(mesh):
    placed = (P(None, "slab", "cross"), P("slab", None), P("slab"))
    return jax.shard_map(
        on_device,
        mesh=mesh,
        in_specs=placed,
        out_specs=(P(None, "slab", "cross"), P(None, "slab", "cross"), P(None, None, "cross")),
        check_vma=False,
    )
```

time: 57.3 us -> 49.8 us (0.87)
  waiting for transfers between devices: 11 us -> 6.47 us
  local copies, waits for them, and re-layouts: 9.84 us -> 6.78 us
  starting transfers between devices: 20.2 us -> 22.1 us
  Pallas kernels: 14.1 us -> 13.2 us
  other arithmetic: 0.93 us -> 0.15 us
    ppermute x0 -> x2, starting transfers between devices: none -> 4.64 us  [the longest x1 3.98 us: on_device(): lax.ppermute(send, both, partner_route)]
    ppermute x8 -> x6, waiting for transfers between devices: 11 us -> 6.47 us  [from_partner(): return lax.ppermute(block, axis, [(i, i ^ step) for i in range(count)])]
    dynamic_slice x2 -> x0, local copies, waits for them, and re-layouts: 2.06 us -> none  [the longest x1 1.08 us: on_device(): lax.dynamic_slice(sim_field, (0, 0, (1 - cross) * width), (species, TILE,...]
    ppermute x8 -> x6, starting transfers between devices: 17.1 us -> 15.1 us  [from_partner(): return lax.ppermute(block, axis, [(i, i ^ step) for i in range(count)])]
    unnamed x16 -> x22, local copies, waits for them, and re-layouts: 7.71 us -> 6.71 us
    pallas_call x9 -> x11, Pallas kernels: 13.3 us -> 12.3 us  [the longest x2 5.79 us: details(): call(functools.partial(detail_kernel, local), jax.ShapeDtypeStruct((DETAI...]
    select_n x1 -> x0, other arithmetic: 0.93 us -> none  [on_device(): theirs = jnp.where(core == cross, partner_set, here_set)]
    ppermute x1, starting transfers between devices: 3.17 us -> 2.38 us  [shifted(): return lax.ppermute(block, axis, [(i, i + 1) for i in range(count - 1)])]
  transfers between devices with their start and end apart: 9 -> 9, of which waited for: 5 -> 4; matrix products, arithmetic and copies ran while one was open for 10% -> 0% of each run, Pallas kernels for 19% -> 22%
where the time goes in v2:
time: 49.8 us; the launch traced here: 49.5 us
  starting transfers between devices  22.1 us (44%)
  Pallas kernels  13.2 us (27%)
  local copies, waits for them, and re-layouts  6.78 us (14%)
  waiting for transfers between devices  6.47 us (13%)
  between operations  0.76 us (2%)
    ppermute x6, starting transfers between devices, from_partner(): return lax.ppermute(block, axis, [(i, i ^ step) for i in range(count)])  15.1 us
    unnamed x22, local copies, waits for them, and re-layouts  6.71 us
    ppermute x6, waiting for transfers between devices, from_partner(): return lax.ppermute(block, axis, [(i, i ^ step) for i in range(count)])  6.47 us
    pallas_call x2, Pallas kernels, details(): call(functools.partial(detail_kernel, local), jax.ShapeDtypeStruct((DETAI...  5.79 us
    ppermute x1, starting transfers between devices, on_device(): lax.ppermute(send, both, partner_route)  3.98 us
    ppermute x1, starting transfers between devices, shifted(): return lax.ppermute(block, axis, [(i, i + 1) for i in range(count - 1)])  2.38 us
    pallas_call x1, Pallas kernels, brick_part(): call(brick_kernel, jax.ShapeDtypeStruct((dense, LANES), F32), grid=(speci...  1.85 us
    pallas_call x1, Pallas kernels, leaving(): call(leave_kernel, tuple(shapes), in_specs=[SMEM_SPEC, VMEM_SPEC], out_sp...  1.49 us
  transfers between devices with their start and end apart: 9, of which 4 were waited for; matrix products, arithmetic and copies ran while one was open for 0% of the time, Pallas kernels for 22%

profile of v2, /device:TPU:0, one launch (start us, length us, event | category | flops | bytes accessed | tf_op | source)
XLA Modules:
  0.0 49.5 jit_solution(7092898257016081493)
XLA Ops:
  0.6 0.0 copy-start
  0.6 1.9 %copy-done = f32[4,96,2048]{2,1,0:T(8,128)S(1)} copy-done((f32[4,96,2048]{2,1,0:T(8,128)S(1)}, f32[4,96,2048]{2,1,0:T(8,128)}, u32[]{:S(2)}) %copy-start) | copy-done | bytes 3145752
  2.5 0.0 copy-start.6
  2.5 0.7 %copy-done.6 = s32[1,2]{1,0:T(1,128)S(1)} copy-done((s32[1,2]{1,0:T(1,128)S(1)}, s32[1,2]{1,0:T(1,128)}, u32[]{:S(2)}) %copy-start.6) | copy-done | bytes 32
  3.2 0.0 copy-start.10
  3.2 0.0 copy-start.7
  3.2 0.0 copy-start.1
  3.2 1.5 %shard_map.58 = (f32[4,16,2048]{2,1,0:T(8,128)S(1)}, f32[4,48,1024]{2,1,0:T(8,128)}) custom-call(s32[1,2]{1,0:T(1,128)S(1)} %copy-done.6, f32[4,96,2048]{2,1,0:T(8,128)S(1)} %copy-done), custom_call_target="tpu_custom_call" | custom-call | tf_op jit(solution)/shard_map/pallas_call | solution.py:57
  4.7 2.4 %collective-permute-start = (f32[4,16,2048]{2,1,0:T(8,128)S(1)}, f32[4,16,2048]{2,1,0:T(8,128)S(1)}, u32[]{:S(2)}, u32[]{:S(2)}) collective-permute-start(f32[4,16,2048]{2,1,0:T(8,128)S(1)} %get-tuple-element.26), channel_id=1, source_target_pairs={{0,2},{2,4},{4,6},{6,8},{8,10},{10,12},{12,14},{14,16},{16,18},{18... | collective-permute-start | bytes 1572872 | tf_op jit(solution)/shard_map/ppermute | solution.py:540
  7.1 2.4 %collective-permute-start.1 = (f32[4,48,1024]{2,1,0:T(8,128)}, f32[4,48,1024]{2,1,0:T(8,128)}, u32[]{:S(2)}, u32[]{:S(2)}) collective-permute-start(f32[4,48,1024]{2,1,0:T(8,128)} %get-tuple-element.31), channel_id=1, source_target_pairs={{0,1},{1,0},{2,3},{3,2},{4,5},{5,4},{6,7},{7,6},{8,9},{9,8},{10,11... | collective-permute-start | bytes 2359304 | tf_op jit(solution)/shard_map/ppermute | solution.py:535
  9.5 0.0 copy-done.10
  9.5 0.1 broadcast_in_dim.2.widths
  9.5 0.0 copy-done.7
  9.6 1.0 %shard_map.59 = (bf16[192,256]{1,0:T(8,128)(2,1)S(1)}, f32[8,128]{1,0:T(8,128)S(1)}, f32[8,128]{1,0:T(8,128)S(1)}) custom-call(s32[1,2]{1,0:T(1,128)S(1)} %copy-done.7, f32[64,128]{1,0:T(8,128)S(1)} %broadcast_in_dim.2.widths), custom_call_target="tpu_custom_call" | custom-call | tf_op jit(solution)/shard_map/pallas_call | solution.py:156
  10.5 0.0 copy-start.8
  10.6 0.6 %copy-done.8 = bf16[192,256]{1,0:T(8,128)(2,1)} copy-done((bf16[192,256]{1,0:T(8,128)(2,1)}, bf16[192,256]{1,0:T(8,128)(2,1)S(1)}, u32[]{:S(2)}) %copy-start.8) | copy-done | bytes 98328
  11.2 0.0 copy-done.1
  11.2 1.8 %shard_map.60.part = f32[328,128]{1,0:T(8,128)S(1)} custom-call(f32[8,128]{1,0:T(8,128)S(1)} %get-tuple-element.27.weights, f32[8,128]{1,0:T(8,128)S(1)} %get-tuple-element.28.coarse_width, f32[4,96,2048]{2,1,0:T(8,128)S(1)} %copy-done.1), custom_call_target="tpu_custom_call" | custom-call | tf_op jit(solution)/shard_map/pallas_call | solution.py:207
  13.0 0.0 collective-permute-done.halo.first
  13.0 0.0 copy-start.2
  13.0 0.7 %shard_map.65 = f32[72,1024]{1,0:T(8,128)S(1)} custom-call(s32[1,2]{1,0:T(1,128)S(1)} %copy-done.7, f32[4,16,2048]{2,1,0:T(8,128)S(1)} %collective-permute-done.halo.first, f32[4,96,2048]{2,1,0:T(8,128)S(1)} %copy-done.1), custom_call_target="tpu_custom_call" | custom-call | flops 400000000 | bytes 4000000 | tf_op jit(solution)/shard_map/pallas_call | solution.py:276
  13.7 0.1 collective-permute-start.5
  13.8 0.0 copy-done.2
  13.8 0.6 %shard_map.61 = (f32[168,128]{1,0:T(8,128)S(1)}, f32[168,128]{1,0:T(8,128)S(1)}) custom-call(f32[8,128]{1,0:T(8,128)S(1)} %get-tuple-element.27.weights, f32[4,16,2048]{2,1,0:T(8,128)S(1)} %collective-permute-done.halo.first, f32[328,128]{1,0:T(8,128)S(1)} %shard_map.60.part), custom_call_target="tpu_custom_call" | custom-call | tf_op jit(solution)/shard_map/pallas_call | solution.py:239
  14.4 4.0 %collective-permute-start.2 = (f32[168,128]{1,0:T(8,128)S(1)}, f32[168,128]{1,0:T(8,128)S(1)}, u32[]{:S(2)}, u32[]{:S(2)}) collective-permute-start(f32[168,128]{1,0:T(8,128)S(1)} %get-tuple-element.35), channel_id=1, source_target_pairs={{0,2},{2,0},{4,6},{6,4},{8,10},{10,8},{12,14},{14,12},{16,18},{18,... | collective-permute-start | bytes 258056 | tf_op jit(solution)/shard_map/ppermute | solution.py:535
  18.4 0.9 %collective-permute-done.2.refs_1_ = f32[168,128]{1,0:T(8,128)S(1)} collective-permute-done((f32[168,128]{1,0:T(8,128)S(1)}, f32[168,128]{1,0:T(8,128)S(1)}, u32[]{:S(2)}, u32[]{:S(2)}) %collective-permute-start.2) | collective-permute-done | bytes 86048 | tf_op jit(solution)/shard_map/ppermute | solution.py:535
  19.3 0.7 %shard_map.62 = (f32[168,128]{1,0:T(8,128)}, f32[296,128]{1,0:T(8,128)S(1)}) custom-call(f32[168,128]{1,0:T(8,128)S(1)} %get-tuple-element.34.refs_0_, f32[168,128]{1,0:T(8,128)S(1)} %collective-permute-done.2.refs_1_), custom_call_target="tpu_custom_call" | custom-call | tf_op jit(solution)/shard_map/pallas_call | solution.py:488
  20.0 0.0 copy-start.4
  20.0 0.7 %copy-done.4 = f32[296,128]{1,0:T(8,128)} copy-done((f32[296,128]{1,0:T(8,128)}, f32[296,128]{1,0:T(8,128)S(1)}, u32[]{:S(2)}) %copy-start.4) | copy-done | bytes 151576
  20.7 3.0 %collective-permute-start.3 = (f32[168,128]{1,0:T(8,128)}, f32[168,128]{1,0:T(8,128)S(1)}, u32[]{:S(2)}, u32[]{:S(2)}) collective-permute-start(f32[168,128]{1,0:T(8,128)} %get-tuple-element.37), channel_id=1, source_target_pairs={{0,4},{2,6},{4,0},{6,2},{8,12},{10,14},{12,8},{14,10},{16,20},{18,... | collective-permute-start | bytes 258056 | tf_op jit(solution)/shard_map/ppermute | solution.py:535
  23.7 3.0 %collective-permute-done.3.refs_1_ = f32[168,128]{1,0:T(8,128)S(1)} collective-permute-done((f32[168,128]{1,0:T(8,128)}, f32[168,128]{1,0:T(8,128)S(1)}, u32[]{:S(2)}, u32[]{:S(2)}) %collective-permute-start.3) | collective-permute-done | bytes 86048 | tf_op jit(solution)/shard_map/ppermute | solution.py:535
  26.7 0.0 copy-start.5
  26.7 0.9 %copy-done.5 = f32[296,128]{1,0:T(8,128)S(1)} copy-done((f32[296,128]{1,0:T(8,128)S(1)}, f32[296,128]{1,0:T(8,128)}, u32[]{:S(2)}) %copy-start.5) | copy-done | bytes 151576
  27.6 0.1 shard_map.63
  27.7 2.8 %collective-permute-start.4 = (f32[168,128]{1,0:T(8,128)S(1)}, f32[168,128]{1,0:T(8,128)S(1)}, u32[]{:S(2)}, u32[]{:S(2)}) collective-permute-start(f32[168,128]{1,0:T(8,128)S(1)} %get-tuple-element.39), channel_id=1, source_target_pairs={{0,8},{2,10},{4,12},{6,14},{8,0},{10,2},{12,4},{14,6},{16,24},{18,... | collective-permute-start | bytes 258056 | tf_op jit(solution)/shard_map/ppermute | solution.py:535
  30.5 0.1 pad_add_fusion.1.place
  30.6 2.4 %collective-permute-done.4.refs_1_ = f32[168,128]{1,0:T(8,128)S(1)} collective-permute-done((f32[168,128]{1,0:T(8,128)S(1)}, f32[168,128]{1,0:T(8,128)S(1)}, u32[]{:S(2)}, u32[]{:S(2)}) %collective-permute-start.4) | collective-permute-done | bytes 86048 | tf_op jit(solution)/shard_map/ppermute | solution.py:535
  33.0 0.1 shard_map.64
  33.1 0.1 collective-permute-done.5.second
  33.2 0.7 %collective-permute-start.7 = (f32[424,128]{1,0:T(8,128)S(1)}, f32[424,128]{1,0:T(8,128)S(1)}, u32[]{:S(2)}, u32[]{:S(2)}) collective-permute-start(f32[424,128]{1,0:T(8,128)S(1)} %get-tuple-element.43.refs_0_), channel_id=1, source_target_pairs={{1,2},{2,1},{5,6},{6,5},{9,10},{10,9},{13,14},{14,13},{17,18},{18,... | collective-permute-start | bytes 651272 | tf_op jit(solution)/shard_map/ppermute | solution.py:593
  33.9 0.1 pad_add_fusion.place
  34.0 4.0 %collective-permute-start.6 = (f32[168,128]{1,0:T(8,128)S(1)}, f32[168,128]{1,0:T(8,128)S(1)}, u32[]{:S(2)}, u32[]{:S(2)}) collective-permute-start(f32[168,128]{1,0:T(8,128)S(1)} %get-tuple-element.44), channel_id=1, source_target_pairs={{0,16},{1,18},{2,17},{3,19},{4,20},{5,22},{6,21},{7,23},{8,24},{9,... | collective-permute-start | bytes 258056 | tf_op jit(solution)/shard_map/ppermute | solution.py:593
  37.9 0.0 copy-start.3
  37.9 1.0 %copy-done.3 = f32[4,16,2048]{2,1,0:T(8,128)S(1)} copy-done((f32[4,16,2048]{2,1,0:T(8,128)S(1)}, f32[4,16,2048]{2,1,0:T(8,128)}, u32[]{:S(2)}) %copy-start.3) | copy-done | bytes 524312
  39.0 0.0 copy-start.9
  39.0 0.9 %copy-done.9 = bf16[192,256]{1,0:T(8,128)(2,1)S(1)} copy-done((bf16[192,256]{1,0:T(8,128)(2,1)S(1)}, bf16[192,256]{1,0:T(8,128)(2,1)}, u32[]{:S(2)}) %copy-start.9) | copy-done | bytes 98328
  39.9 2.5 %shard_map.66.rest_0_ = f32[60,4,2048]{2,1,0:T(4,128)} custom-call(s32[2]{0:T(128)S(1)} %pad_add_fusion.1.place, bf16[192,256]{1,0:T(8,128)(2,1)S(1)} %copy-done.9, f32[4,16,2048]{2,1,0:T(8,128)S(1)} %copy-done.3, f32[4,96,2048]{2,1,0:T(8,128)S(1)} %copy-done.1), custom_call_target="tpu_custom_call" | custom-call | flops 2000000000 | bytes 20000000 | tf_op jit(solution)/shard_map/pallas_call | solution.py:338
  42.4 0.0 collective-permute-done.6.refs_1_
  42.4 0.0 collective-permute-done.7.refs_2_
  42.4 0.1 shard_map.68
  42.5 2.9 %collective-permute-start.8 = (f32[288,128]{1,0:T(8,128)S(1)}, f32[288,128]{1,0:T(8,128)S(1)}, u32[]{:S(2)}, u32[]{:S(2)}) collective-permute-start(f32[288,128]{1,0:T(8,128)S(1)} %get-tuple-element.46), channel_id=1, source_target_pairs={{0,2},{2,0},{4,6},{6,4},{8,10},{10,8},{12,14},{14,12},{16,18},{18,... | collective-permute-start | bytes 442376 | tf_op jit(solution)/shard_map/ppermute | solution.py:535
  45.3 0.0 collective-permute-done.1.first
  45.3 3.3 %shard_map.67 = f32[60,4,2048]{2,1,0:T(4,128)} custom-call(s32[2]{0:T(128)S(1)} %pad_add_fusion.place, bf16[192,256]{1,0:T(8,128)(2,1)S(1)} %copy-done.9, f32[4,48,1024]{2,1,0:T(8,128)} %collective-permute-done.1.first, f32[72,1024]{1,0:T(8,128)} %collective-permute-done.5.second, f32[60,4,2048]{2,1,0:T(4,128)} %shard_map.66.rest_0_), custom_call_target="tpu_custom_call", output_to_operand_aliasing={{}: (4, {})} | custom-call | flops 2000000000 | bytes 20000000 | tf_op jit(solution)/shard_map/pallas_call | solution.py:338
  48.6 0.0 collective-permute-done.8.other
  48.6 0.8 %shard_map.69 = (f32[4,4,2048]{2,1,0:T(4,128)}, f32[5,4,2048]{2,1,0:T(4,128)}) custom-call(f32[288,128]{1,0:T(8,128)S(1)} %get-tuple-element.45.own, f32[288,128]{1,0:T(8,128)S(1)} %collective-permute-done.8.other), custom_call_target="tpu_custom_call" | custom-call | tf_op jit(solution)/shard_map/pallas_call | solution.py:521
Async XLA Ops:
  0.6 1.9 %copy-start = (f32[4,96,2048]{2,1,0:T(8,128)S(1)}, f32[4,96,2048]{2,1,0:T(8,128)}, u32[]{:S(2)}) copy-start(f32[4,96,2048]{2,1,0:T(8,128)} %second.1) | copy-start | bytes 9437188
  2.5 0.7 %copy-start.6 = (s32[1,2]{1,0:T(1,128)S(1)}, s32[1,2]{1,0:T(1,128)}, u32[]{:S(2)}) copy-start(s32[1,2]{1,0:T(1,128)} %edges.5) | copy-start | bytes 28
  3.2 6.3 %copy-start.10 = (f32[64]{0:T(128)S(1)}, f32[64]{0:T(128)}, u32[]{:S(2)}) copy-start(f32[64]{0:T(128)} %param.5) | copy-start | bytes 772
  3.2 6.4 %copy-start.7 = (s32[1,2]{1,0:T(1,128)S(1)}, s32[1,2]{1,0:T(1,128)}, u32[]{:S(2)}) copy-start(s32[1,2]{1,0:T(1,128)} %edges.5) | copy-start | bytes 28
  3.2 8.0 %copy-start.1 = (f32[4,96,2048]{2,1,0:T(8,128)S(1)}, f32[4,96,2048]{2,1,0:T(8,128)}, u32[]{:S(2)}) copy-start(f32[4,96,2048]{2,1,0:T(8,128)} %second.1) | copy-start | bytes 9437188
  4.7 8.4 %collective-permute-start = (f32[4,16,2048]{2,1,0:T(8,128)S(1)}, f32[4,16,2048]{2,1,0:T(8,128)S(1)}, u32[]{:S(2)}, u32[]{:S(2)}) collective-permute-start(f32[4,16,2048]{2,1,0:T(8,128)S(1)} %get-tuple-element.26), channel_id=1, source_target_pairs={{0,2},{2,4},{4,6},{6,8},{8,10},{10,12},{12,14},{14,16},{16,18},{18... | collective-permute-start | bytes 1572872 | tf_op jit(solution)/shard_map/ppermute | solution.py:540
  7.1 38.3 %collective-permute-start.1 = (f32[4,48,1024]{2,1,0:T(8,128)}, f32[4,48,1024]{2,1,0:T(8,128)}, u32[]{:S(2)}, u32[]{:S(2)}) collective-permute-start(f32[4,48,1024]{2,1,0:T(8,128)} %get-tuple-element.31), channel_id=1, source_target_pairs={{0,1},{1,0},{2,3},{3,2},{4,5},{5,4},{6,7},{7,6},{8,9},{9,8},{10,11... | collective-permute-start | bytes 2359304 | tf_op jit(solution)/shard_map/ppermute | solution.py:535
  10.5 0.6 %copy-start.8 = (bf16[192,256]{1,0:T(8,128)(2,1)}, bf16[192,256]{1,0:T(8,128)(2,1)S(1)}, u32[]{:S(2)}) copy-start(bf16[192,256]{1,0:T(8,128)(2,1)S(1)} %get-tuple-element.30.factors) | copy-start | bytes 294916
  13.0 0.8 %copy-start.2 = (f32[4,16,2048]{2,1,0:T(8,128)}, f32[4,16,2048]{2,1,0:T(8,128)S(1)}, u32[]{:S(2)}) copy-start(f32[4,16,2048]{2,1,0:T(8,128)S(1)} %collective-permute-done.halo.first) | copy-start | bytes 1572868
  13.7 19.5 %collective-permute-start.5 = (f32[72,1024]{1,0:T(8,128)S(1)}, f32[72,1024]{1,0:T(8,128)}, u32[]{:S(2)}, u32[]{:S(2)}) collective-permute-start(f32[72,1024]{1,0:T(8,128)S(1)} %shard_map.65), channel_id=1, source_target_pairs={{0,1},{1,0},{2,3},{3,2},{4,5},{5,4},{6,7},{7,6},{8,9},{9,8},{10,11... | collective-permute-start | bytes 884744 | tf_op jit(solution)/shard_map/ppermute | solution.py:535
  14.4 4.9 %collective-permute-start.2 = (f32[168,128]{1,0:T(8,128)S(1)}, f32[168,128]{1,0:T(8,128)S(1)}, u32[]{:S(2)}, u32[]{:S(2)}) collective-permute-start(f32[168,128]{1,0:T(8,128)S(1)} %get-tuple-element.35), channel_id=1, source_target_pairs={{0,2},{2,0},{4,6},{6,4},{8,10},{10,8},{12,14},{14,12},{16,18},{18,... | collective-permute-start | bytes 258056 | tf_op jit(solution)/shard_map/ppermute | solution.py:535
  20.0 0.7 %copy-start.4 = (f32[296,128]{1,0:T(8,128)}, f32[296,128]{1,0:T(8,128)S(1)}, u32[]{:S(2)}) copy-start(f32[296,128]{1,0:T(8,128)S(1)} %get-tuple-element.36.refs_0_) | copy-start | bytes 454660
  20.7 6.1 %collective-permute-start.3 = (f32[168,128]{1,0:T(8,128)}, f32[168,128]{1,0:T(8,128)S(1)}, u32[]{:S(2)}, u32[]{:S(2)}) collective-permute-start(f32[168,128]{1,0:T(8,128)} %get-tuple-element.37), channel_id=1, source_target_pairs={{0,4},{2,6},{4,0},{6,2},{8,12},{10,14},{12,8},{14,10},{16,20},{18,... | collective-permute-start | bytes 258056 | tf_op jit(solution)/shard_map/ppermute | solution.py:535
  26.7 0.9 %copy-start.5 = (f32[296,128]{1,0:T(8,128)S(1)}, f32[296,128]{1,0:T(8,128)}, u32[]{:S(2)}) copy-start(f32[296,128]{1,0:T(8,128)} %copy-done.4) | copy-start | bytes 454660
  27.7 5.3 %collective-permute-start.4 = (f32[168,128]{1,0:T(8,128)S(1)}, f32[168,128]{1,0:T(8,128)S(1)}, u32[]{:S(2)}, u32[]{:S(2)}) collective-permute-start(f32[168,128]{1,0:T(8,128)S(1)} %get-tuple-element.39), channel_id=1, source_target_pairs={{0,8},{2,10},{4,12},{6,14},{8,0},{10,2},{12,4},{14,6},{16,24},{18,... | collective-permute-start | bytes 258056 | tf_op jit(solution)/shard_map/ppermute | solution.py:535
  33.2 9.2 %collective-permute-start.7 = (f32[424,128]{1,0:T(8,128)S(1)}, f32[424,128]{1,0:T(8,128)S(1)}, u32[]{:S(2)}, u32[]{:S(2)}) collective-permute-start(f32[424,128]{1,0:T(8,128)S(1)} %get-tuple-element.43.refs_0_), channel_id=1, source_target_pairs={{1,2},{2,1},{5,6},{6,5},{9,10},{10,9},{13,14},{14,13},{17,18},{18,... | collective-permute-start | bytes 651272 | tf_op jit(solution)/shard_map/ppermute | solution.py:593
  34.0 8.4 %collective-permute-start.6 = (f32[168,128]{1,0:T(8,128)S(1)}, f32[168,128]{1,0:T(8,128)S(1)}, u32[]{:S(2)}, u32[]{:S(2)}) collective-permute-start(f32[168,128]{1,0:T(8,128)S(1)} %get-tuple-element.44), channel_id=1, source_target_pairs={{0,16},{1,18},{2,17},{3,19},{4,20},{5,22},{6,21},{7,23},{8,24},{9,... | collective-permute-start | bytes 258056 | tf_op jit(solution)/shard_map/ppermute | solution.py:593
  37.9 1.0 %copy-start.3 = (f32[4,16,2048]{2,1,0:T(8,128)S(1)}, f32[4,16,2048]{2,1,0:T(8,128)}, u32[]{:S(2)}) copy-start(f32[4,16,2048]{2,1,0:T(8,128)} %copy-done.2) | copy-start | bytes 1572868
  39.0 0.9 %copy-start.9 = (bf16[192,256]{1,0:T(8,128)(2,1)S(1)}, bf16[192,256]{1,0:T(8,128)(2,1)}, u32[]{:S(2)}) copy-start(bf16[192,256]{1,0:T(8,128)(2,1)} %copy-done.8) | copy-start | bytes 294916
  42.5 6.2 %collective-permute-start.8 = (f32[288,128]{1,0:T(8,128)S(1)}, f32[288,128]{1,0:T(8,128)S(1)}, u32[]{:S(2)}, u32[]{:S(2)}) collective-permute-start(f32[288,128]{1,0:T(8,128)S(1)} %get-tuple-element.46), channel_id=1, source_target_pairs={{0,2},{2,0},{4,6},{6,4},{8,10},{10,8},{12,14},{14,12},{16,18},{18,... | collective-permute-start | bytes 442376 | tf_op jit(solution)/shard_map/ppermute | solution.py:535

commit v3 on v2

--- a/solution.py
+++ b/solution.py
@@ -34,19 +34,29 @@
 HBM_SPEC = pl.BlockSpec(memory_space=pltpu.HBM)
 
 
-def leave_kernel(edges, field, tail, *away):
+def leave_kernel(edges, field, tail, *refs):
     species, _, lines = tail.shape
+    buf, sems = refs[-2:]
+    away = refs[0] if len(refs) > 2 else None
+    copies = []
+    if away is not None:
+        width = away.shape[2]
+        other = pl.ds(pl.multiple_of((1 - lax.axis_index("cross")) * width, LANES), width)
     start = edges[0, 1] - edges[0, 0] - HALO
     rest = start & (SUB - 1)
     whole = pl.multiple_of(start - rest, SUB)
+    window = []
     for sp in range(species):
-        rows = field[sp, pl.ds(whole, HALO + SUB), :]
-        tail[sp] = pltpu.roll(rows, (HALO + SUB - rest) % (HALO + SUB), 0)[:HALO]
-    for out in away:
-        width = out.shape[2]
-        other = pl.multiple_of((1 - lax.axis_index("cross")) * width, LANES)
-        for sp in range(species):
-            out[sp] = field[sp, :FIRST, pl.ds(other, width)]
+        window.append(pltpu.make_async_copy(field.at[sp, pl.ds(whole, HALO + SUB), :], buf.at[sp], sems.at[0, sp]))
+        window[-1].start()
+    for sp in range(species if away is not None else 0):
+        copies.append(pltpu.make_async_copy(field.at[sp, pl.ds(0, FIRST), other], away.at[sp], sems.at[1, sp]))
+        copies[-1].start()
+    for sp in range(species):
+        window[sp].wait()
+        tail[sp] = pltpu.roll(buf[sp], (HALO + SUB - rest) % (HALO + SUB), 0)[:HALO]
+    for copy in copies:
+        copy.wait()
 
 
 def leaving(edges, field, width):
@@ -57,8 +67,10 @@
     return call(
         leave_kernel,
         tuple(shapes),
-        in_specs=[SMEM_SPEC, VMEM_SPEC],
+        in_specs=[SMEM_SPEC, HBM_SPEC],
         out_specs=(VMEM_SPEC,) * len(shapes),
+        scratch_shapes=[pltpu.VMEM((species, HALO + SUB, lines), F32), pltpu.SemaphoreType.DMA((2, species))],
+        vmem=62 << 20,
     )(edges, field)
 
 
@@ -282,14 +294,15 @@
     )(edges, halo, field)
 
 
-def detail_kernel(local, place, factors, first, second, *rest):
+def detail_kernel(local, edges, factors, first, second, *rest):
     out, wide = rest[-2:]
     species = out.shape[1]
     width = out.shape[2]
     weights = factors[:, : 3 * HELD]
+    shift = edges[0, 0] - lax.axis_index("slab") * TILE
     for sp in range(species):
         if local:
-            more = later_nodes(place[1], first[sp], second[sp, FIRST:BRICK_END])
+            more = later_nodes(shift, first[sp], second[sp, FIRST:BRICK_END])
             pieces = [second[sp, :FIRST], more[: SECOND + HALO]]
         else:
             last = species * SECOND
@@ -310,26 +323,28 @@
             out[k, :, t * LANES : (t + 1) * LANES] = wide[t, k * species : (k + 1) * species]
 
 
-def details(local, place, factors, first, second, width, species, lines, onto=None):
+def details(local, edges, factors, first, second, width, species, lines, onto=None):
     chunk = min(width, 512)
     steps = width // chunk
 
-    def at(own, i, place):
-        return place[0] * steps + i if own else i
-
-    whole = first.shape[2] == lines
+    def here(i):
+        return i if width == lines else lax.axis_index("cross") * steps + i
+
+    def there(i):
+        return (1 - lax.axis_index("cross")) * steps + i
+
     if local:
         specs = [
-            pl.BlockSpec((species, HALO, chunk), lambda i, place: (0, 0, at(whole, i, place))),
-            pl.BlockSpec((species, HELD, chunk), lambda i, place: (0, 0, at(whole, i, place))),
+            pl.BlockSpec((species, HALO, chunk), lambda i: (0, 0, here(i))),
+            pl.BlockSpec((species, HELD, chunk), lambda i: (0, 0, here(i))),
         ]
     else:
         specs = [
-            pl.BlockSpec((species, FIRST, chunk), lambda i, place: (0, 0, i)),
-            pl.BlockSpec((second.shape[0], chunk), lambda i, place: (0, i)),
+            pl.BlockSpec((species, FIRST, chunk), lambda i: (0, 0, i)),
+            pl.BlockSpec((second.shape[0], chunk), lambda i: (0, i)),
         ]
-    specs = [pl.BlockSpec((3 * TILE, 2 * LANES), lambda i, place: (0, 0))] + specs
-    operands = [place, factors, first, second]
+    specs = [SMEM_SPEC, pl.BlockSpec((3 * TILE, 2 * LANES), lambda i: (0, 0))] + specs
+    operands = [edges, factors, first, second]
     alias = {}
     if onto is not None:
         specs.append(HBM_SPEC)
@@ -338,13 +353,10 @@
     return call(
         functools.partial(detail_kernel, local),
         jax.ShapeDtypeStruct((DETAILS, species, lines), F32),
-        grid_spec=pltpu.PrefetchScalarGridSpec(
-            num_scalar_prefetch=1,
-            grid=(steps,),
-            in_specs=specs,
-            out_specs=pl.BlockSpec((DETAILS, species, chunk), lambda i, place: (0, 0, at(True, i, place))),
-            scratch_shapes=[pltpu.VMEM((chunk // LANES, TILE * species, LANES), F32)],
-        ),
+        grid=(steps,),
+        in_specs=specs,
+        out_specs=pl.BlockSpec((DETAILS, species, chunk), lambda i: (0, 0, here(i) if local else there(i))),
+        scratch_shapes=[pltpu.VMEM((chunk // LANES, TILE * species, LANES), F32)],
         input_output_aliases=alias,
         cost=2_000_000_000,
     )(*operands)
@@ -563,34 +575,31 @@
     species, _, lines = sim_field.shape
     cross_count = lax.axis_size("cross")
     slabs = lax.axis_size("slab")
-    cross = lax.axis_index("cross")
-    core = lax.axis_index("slab") % 2
     depth = slabs.bit_length() - 1
     width = lines // cross_count
     rows = species * (lines // 2) // LANES
     swapped = cross_count == 2
     both = ("slab", "cross")
 
+    field = sim_field
+    tail, *away = leaving(brick_edges, field, width)
     if swapped:
-        tail, first_away = leaving(brick_edges, sim_field, width)
-        first_in = from_partner(first_away, "cross", 1)
-    else:
-        (tail,) = leaving(brick_edges, sim_field, lines)
+        first_in = from_partner(away[0], "cross", 1)
     halo = shifted(tail, "slab")
     factors, weights, coarse_width = tile_matrix(brick_edges, cell_width)
-    part = brick_part(weights, coarse_width, sim_field)
+    part = brick_part(weights, coarse_width, field)
     halo, part, factors = lax.optimization_barrier((halo, part, factors))
     own_half, other_half = coarse_sets(weights, halo, part)
-    shift = brick_edges[0, 0] - lax.axis_index("slab") * TILE
+    halo, other_half = lax.optimization_barrier((halo, other_half))
     if swapped:
-        rest_in = from_partner(rest_away(brick_edges, halo, sim_field, width), "cross", 1)
+        rest_in = from_partner(rest_away(brick_edges, halo, field, width), "cross", 1)
 
     send, carried = other_half, own_half
     for level in range(depth):
         if swapped and level == depth - 1:
             partner_route, own_route = last_routes(slabs)
-            send, carried, rest_in = lax.optimization_barrier((send, carried, rest_in))
             operands = (carried, lax.ppermute(send, both, partner_route), lax.ppermute(carried, both, own_route))
+            operands, rest_in = lax.optimization_barrier((operands, rest_in))
         else:
             operands = (carried, from_partner(send, "slab", 1 << level))
         send, carried = merge(level, depth, rows, swapped, *operands)
@@ -600,10 +609,10 @@
     if swapped:
         tree_detail, coarse_final = finish(here_set, partner_set, species, lines)
         coarse_final = coarse_final.transpose(1, 0, 2)
-        here, there = jnp.stack([cross, shift]), jnp.stack([1 - cross, shift])
-        tile_detail = details(True, here, factors, halo, sim_field, width, species, lines)
-        tile_detail = details(False, there, factors, first_in, rest_in, width, species, lines, tile_detail)
+        tile_detail = details(True, brick_edges, factors, halo, field, width, species, lines)
+        tile_detail = details(False, brick_edges, factors, first_in, rest_in, width, species, lines, tile_detail)
     else:
+        core = lax.axis_index("slab") % 2
         first = jnp.where(core == 0, here_set, partner_set)
         second = jnp.where(core == 0, partner_set, here_set)
         ended = jnp.stack([first, second]).reshape(2, 2 * COARSE - 1, species, lines // 2)
@@ -611,8 +620,7 @@
         ended = exchanged(ended, "cross")
         coarse_final, tree_detail = ended[:, :COARSE], ended[:, COARSE:]
         moved = exchanged(jnp.concatenate([halo, sim_field[:, :HELD]], axis=1), "cross")
-        place = jnp.stack([jnp.zeros_like(shift), shift])
-        tile_detail = details(True, place, factors, moved[:, :HALO], moved[:, HALO:], lines, species, lines)
+        tile_detail = details(True, brick_edges, factors, moved[:, :HALO], moved[:, HALO:], lines, species, lines)
     return (tile_detail.transpose(1, 0, 2), tree_detail, coarse_final)
 
 

time: 49.8 us -> 40.9 us (0.82)
  local copies, waits for them, and re-layouts: 6.78 us -> 1.97 us
  waiting for transfers between devices: 6.47 us -> 4.32 us
  starting transfers between devices: 22.1 us -> 20.3 us
    unnamed x22 -> x8, local copies, waits for them, and re-layouts: 6.71 us -> 1.9 us
    ppermute x6, waiting for transfers between devices: 6.47 us -> 4.31 us  [from_partner(): return lax.ppermute(block, axis, [(i, i ^ step) for i in range(count)])]
    pallas_call x1, Pallas kernels: 1.49 us -> 3.38 us  [leaving(): call(leave_kernel, tuple(shapes), in_specs=[SMEM_SPEC, HBM_SPEC], out_spe...]
    pallas_call x2, Pallas kernels: 5.79 us -> 4.76 us  [details(): call(functools.partial(detail_kernel, local), jax.ShapeDtypeStruct((DETAI...]
    ppermute x6, starting transfers between devices: 15.1 us -> 14.1 us  [from_partner(): return lax.ppermute(block, axis, [(i, i ^ step) for i in range(count)])]
    ppermute x1, starting transfers between devices: 3.98 us -> 3.1 us  [on_device(): lax.ppermute(send, both, partner_route)]
    pallas_call x4, Pallas kernels: 0.95 us -> 0.32 us  [merge(): call(functools.partial(merge_kernel, level, depth, rows, swapped), tuple(...]
  transfers between devices with their start and end apart: 9 -> 9, of which waited for: 4 -> 4; matrix products, arithmetic and copies ran while one was open for 0% -> 0% of each run, Pallas kernels for 22% -> 23%
where the time goes in v3:
time: 40.9 us; the launch traced here: 40.7 us
  starting transfers between devices  20.3 us (50%)
  Pallas kernels  13.4 us (33%)
  waiting for transfers between devices  4.32 us (11%)
  local copies, waits for them, and re-layouts  1.97 us (5%)
  between operations  0.73 us (2%)
    ppermute x6, starting transfers between devices, from_partner(): return lax.ppermute(block, axis, [(i, i ^ step) for i in range(count)])  14.1 us
    pallas_call x2, Pallas kernels, details(): call(functools.partial(detail_kernel, local), jax.ShapeDtypeStruct((DETAI...  4.76 us
    ppermute x6, waiting for transfers between devices, from_partner(): return lax.ppermute(block, axis, [(i, i ^ step) for i in range(count)])  4.31 us
    pallas_call x1, Pallas kernels, leaving(): call(leave_kernel, tuple(shapes), in_specs=[SMEM_SPEC, HBM_SPEC], out_spe...  3.38 us
    ppermute x1, starting transfers between devices, on_device(): lax.ppermute(send, both, partner_route)  3.1 us
    ppermute x1, starting transfers between devices, shifted(): return lax.ppermute(block, axis, [(i, i + 1) for i in range(count - 1)])  2.39 us
    unnamed x8, local copies, waits for them, and re-layouts  1.9 us
    pallas_call x1, Pallas kernels, brick_part(): call(brick_kernel, jax.ShapeDtypeStruct((dense, LANES), F32), grid=(speci...  1.86 us
  transfers between devices with their start and end apart: 9, of which 4 were waited for; matrix products, arithmetic and copies ran while one was open for 0% of the time, Pallas kernels for 23%

profile of v3, /device:TPU:0, one launch (start us, length us, event | category | flops | bytes accessed | tf_op | source)
XLA Modules:
  0.0 40.7 jit_solution(2769900445986798310)
XLA Ops:
  0.6 0.0 copy-start.2
  0.6 0.0 copy-start.3
  0.7 3.4 %shard_map.58 = (f32[4,16,2048]{2,1,0:T(8,128)}, f32[4,48,1024]{2,1,0:T(8,128)}) custom-call(s32[1,2]{1,0:T(1,128)} %edges.9, f32[4,96,2048]{2,1,0:T(8,128)} %second.1), custom_call_target="tpu_custom_call" | custom-call | tf_op jit(solution)/shard_map/pallas_call | solution.py:67
  4.0 2.4 %collective-permute-start = (f32[4,16,2048]{2,1,0:T(8,128)}, f32[4,16,2048]{2,1,0:T(8,128)S(1)}, u32[]{:S(2)}, u32[]{:S(2)}) collective-permute-start(f32[4,16,2048]{2,1,0:T(8,128)} %get-tuple-element.29), channel_id=1, source_target_pairs={{0,2},{2,4},{4,6},{6,8},{8,10},{10,12},{12,14},{14,16},{16,18},{18... | collective-permute-start | bytes 1572872 | tf_op jit(solution)/shard_map/ppermute | solution.py:552
  6.4 2.4 %collective-permute-start.1 = (f32[4,48,1024]{2,1,0:T(8,128)}, f32[4,48,1024]{2,1,0:T(8,128)S(1)}, u32[]{:S(2)}, u32[]{:S(2)}) collective-permute-start(f32[4,48,1024]{2,1,0:T(8,128)} %get-tuple-element.34), channel_id=1, source_target_pairs={{0,1},{1,0},{2,3},{3,2},{4,5},{5,4},{6,7},{7,6},{8,9},{9,8},{10,11... | collective-permute-start | bytes 2359304 | tf_op jit(solution)/shard_map/ppermute | solution.py:547
  8.9 0.0 copy-done.3
  8.9 0.1 broadcast_in_dim.2.widths
  8.9 0.0 copy-done.2
  8.9 1.0 %shard_map.59 = (bf16[192,256]{1,0:T(8,128)(2,1)S(1)}, f32[8,128]{1,0:T(8,128)S(1)}, f32[8,128]{1,0:T(8,128)S(1)}) custom-call(s32[1,2]{1,0:T(1,128)S(1)} %copy-done.2, f32[64,128]{1,0:T(8,128)S(1)} %broadcast_in_dim.2.widths), custom_call_target="tpu_custom_call" | custom-call | tf_op jit(solution)/shard_map/pallas_call | solution.py:168
  9.9 0.0 copy-start
  9.9 1.9 %copy-done = f32[4,96,2048]{2,1,0:T(8,128)S(1)} copy-done((f32[4,96,2048]{2,1,0:T(8,128)S(1)}, f32[4,96,2048]{2,1,0:T(8,128)}, u32[]{:S(2)}) %copy-start) | copy-done | bytes 3145752
  11.8 0.0 copy-start.1
  11.8 1.9 %shard_map.60.part = f32[328,128]{1,0:T(8,128)S(1)} custom-call(f32[8,128]{1,0:T(8,128)S(1)} %get-tuple-element.30.weights, f32[8,128]{1,0:T(8,128)S(1)} %get-tuple-element.31.coarse_width, f32[4,96,2048]{2,1,0:T(8,128)S(1)} %copy-done), custom_call_target="tpu_custom_call" | custom-call | tf_op jit(solution)/shard_map/pallas_call | solution.py:219
  13.7 0.0 collective-permute-done.halo.first
  13.7 0.6 %shard_map.61 = (f32[168,128]{1,0:T(8,128)S(1)}, f32[168,128]{1,0:T(8,128)S(1)}) custom-call(f32[8,128]{1,0:T(8,128)S(1)} %get-tuple-element.30.weights, f32[4,16,2048]{2,1,0:T(8,128)S(1)} %collective-permute-done.halo.first, f32[328,128]{1,0:T(8,128)S(1)} %shard_map.60.part), custom_call_target="tpu_custom_call" | custom-call | tf_op jit(solution)/shard_map/pallas_call | solution.py:251
  14.3 1.8 %collective-permute-start.2 = (f32[168,128]{1,0:T(8,128)S(1)}, f32[168,128]{1,0:T(8,128)S(1)}, u32[]{:S(2)}, u32[]{:S(2)}) collective-permute-start(f32[168,128]{1,0:T(8,128)S(1)} %get-tuple-element.39), channel_id=1, source_target_pairs={{0,2},{2,0},{4,6},{6,4},{8,10},{10,8},{12,14},{14,12},{16,18},{18,... | collective-permute-start | bytes 258056 | tf_op jit(solution)/shard_map/ppermute | solution.py:547
  16.1 0.9 %collective-permute-done.2.refs_1_ = f32[168,128]{1,0:T(8,128)S(1)} collective-permute-done((f32[168,128]{1,0:T(8,128)S(1)}, f32[168,128]{1,0:T(8,128)S(1)}, u32[]{:S(2)}, u32[]{:S(2)}) %collective-permute-start.2) | collective-permute-done | bytes 86048 | tf_op jit(solution)/shard_map/ppermute | solution.py:547
  17.0 0.1 shard_map.62
  17.1 2.7 %collective-permute-start.3 = (f32[168,128]{1,0:T(8,128)S(1)}, f32[168,128]{1,0:T(8,128)S(1)}, u32[]{:S(2)}, u32[]{:S(2)}) collective-permute-start(f32[168,128]{1,0:T(8,128)S(1)} %get-tuple-element.41), channel_id=1, source_target_pairs={{0,4},{2,6},{4,0},{6,2},{8,12},{10,14},{12,8},{14,10},{16,20},{18,... | collective-permute-start | bytes 258056 | tf_op jit(solution)/shard_map/ppermute | solution.py:547
  19.8 2.9 %collective-permute-done.3.refs_1_ = f32[168,128]{1,0:T(8,128)S(1)} collective-permute-done((f32[168,128]{1,0:T(8,128)S(1)}, f32[168,128]{1,0:T(8,128)S(1)}, u32[]{:S(2)}, u32[]{:S(2)}) %collective-permute-start.3) | collective-permute-done | bytes 86048 | tf_op jit(solution)/shard_map/ppermute | solution.py:547
  22.6 0.1 shard_map.63
  22.7 2.8 %collective-permute-start.4 = (f32[168,128]{1,0:T(8,128)S(1)}, f32[168,128]{1,0:T(8,128)S(1)}, u32[]{:S(2)}, u32[]{:S(2)}) collective-permute-start(f32[168,128]{1,0:T(8,128)S(1)} %get-tuple-element.43), channel_id=1, source_target_pairs={{0,8},{2,10},{4,12},{6,14},{8,0},{10,2},{12,4},{14,6},{16,24},{18,... | collective-permute-start | bytes 258056 | tf_op jit(solution)/shard_map/ppermute | solution.py:547
  25.5 0.0 copy-done.1
  25.5 0.7 %shard_map.65 = f32[72,1024]{1,0:T(8,128)S(1)} custom-call(s32[1,2]{1,0:T(1,128)S(1)} %copy-done.2, f32[4,16,2048]{2,1,0:T(8,128)S(1)} %collective-permute-done.halo.first, f32[4,96,2048]{2,1,0:T(8,128)S(1)} %copy-done.1), custom_call_target="tpu_custom_call" | custom-call | flops 400000000 | bytes 4000000 | tf_op jit(solution)/shard_map/pallas_call | solution.py:288
  26.2 1.6 %collective-permute-start.7 = (f32[72,1024]{1,0:T(8,128)S(1)}, f32[72,1024]{1,0:T(8,128)S(1)}, u32[]{:S(2)}, u32[]{:S(2)}) collective-permute-start(f32[72,1024]{1,0:T(8,128)S(1)} %shard_map.65), channel_id=1, source_target_pairs={{0,1},{1,0},{2,3},{3,2},{4,5},{5,4},{6,7},{7,6},{8,9},{9,8},{10,11... | collective-permute-start | bytes 884744 | tf_op jit(solution)/shard_map/ppermute | solution.py:547
  27.8 0.2 collective-permute-done.4.refs_1_
  28.0 0.1 shard_map.64
  28.1 0.7 %collective-permute-start.6 = (f32[424,128]{1,0:T(8,128)S(1)}, f32[424,128]{1,0:T(8,128)S(1)}, u32[]{:S(2)}, u32[]{:S(2)}) collective-permute-start(f32[424,128]{1,0:T(8,128)S(1)} %get-tuple-element.48.refs_0_), channel_id=1, source_target_pairs={{1,2},{2,1},{5,6},{6,5},{9,10},{10,9},{13,14},{14,13},{17,18},{18,... | collective-permute-start | bytes 651272 | tf_op jit(solution)/shard_map/ppermute | solution.py:601
  28.7 3.1 %collective-permute-start.5 = (f32[168,128]{1,0:T(8,128)S(1)}, f32[168,128]{1,0:T(8,128)S(1)}, u32[]{:S(2)}, u32[]{:S(2)}) collective-permute-start(f32[168,128]{1,0:T(8,128)S(1)} %get-tuple-element.45), channel_id=1, source_target_pairs={{0,16},{1,18},{2,17},{3,19},{4,20},{5,22},{6,21},{7,23},{8,24},{9,... | collective-permute-start | bytes 258056 | tf_op jit(solution)/shard_map/ppermute | solution.py:601
  31.8 2.4 %shard_map.66.rest_0_ = f32[60,4,2048]{2,1,0:T(4,128)} custom-call(s32[1,2]{1,0:T(1,128)S(1)} %copy-done.2, bf16[192,256]{1,0:T(8,128)(2,1)S(1)} %get-tuple-element.33.factors, f32[4,16,2048]{2,1,0:T(8,128)S(1)} %collective-permute-done.halo.first, f32[4,96,2048]{2,1,0:T(8,128)S(1)} %copy-done.1), custom_call_target="tpu_custom_call" | custom-call | flops 2000000000 | bytes 20000000 | tf_op jit(solution)/shard_map/pallas_call | solution.py:353
  34.3 0.3 collective-permute-done.7.second
  34.6 0.0 collective-permute-done.5.refs_1_
  34.6 0.0 collective-permute-done.6.refs_2_
  34.6 0.1 shard_map.68
  34.7 2.8 %collective-permute-start.8 = (f32[288,128]{1,0:T(8,128)S(1)}, f32[288,128]{1,0:T(8,128)S(1)}, u32[]{:S(2)}, u32[]{:S(2)}) collective-permute-start(f32[288,128]{1,0:T(8,128)S(1)} %get-tuple-element.52), channel_id=1, source_target_pairs={{0,2},{2,0},{4,6},{6,4},{8,10},{10,8},{12,14},{14,12},{16,18},{18,... | collective-permute-start | bytes 442376 | tf_op jit(solution)/shard_map/ppermute | solution.py:547
  37.5 0.0 collective-permute-done.1.first
  37.5 2.3 %shard_map.67 = f32[60,4,2048]{2,1,0:T(4,128)} custom-call(s32[1,2]{1,0:T(1,128)S(1)} %copy-done.2, bf16[192,256]{1,0:T(8,128)(2,1)S(1)} %get-tuple-element.33.factors, f32[4,48,1024]{2,1,0:T(8,128)S(1)} %collective-permute-done.1.first, f32[72,1024]{1,0:T(8,128)S(1)} %collective-permute-done.7.second, ...), custom_call_target="tpu_custom_call", output_to_operand_aliasing={{}: (4, {})} | custom-call | flops 2000000000 | bytes 20000000 | tf_op jit(solution)/shard_map/pallas_call | solution.py:353
  39.9 0.0 collective-permute-done.8.other
  39.9 0.8 %shard_map.69 = (f32[4,4,2048]{2,1,0:T(4,128)}, f32[5,4,2048]{2,1,0:T(4,128)}) custom-call(f32[288,128]{1,0:T(8,128)S(1)} %get-tuple-element.51.own, f32[288,128]{1,0:T(8,128)S(1)} %collective-permute-done.8.other), custom_call_target="tpu_custom_call" | custom-call | tf_op jit(solution)/shard_map/pallas_call | solution.py:533
Async XLA Ops:
  0.6 8.3 %copy-start.2 = (s32[1,2]{1,0:T(1,128)S(1)}, s32[1,2]{1,0:T(1,128)}, u32[]{:S(2)}) copy-start(s32[1,2]{1,0:T(1,128)} %edges.9) | copy-start | bytes 28
  0.6 8.2 %copy-start.3 = (f32[64]{0:T(128)S(1)}, f32[64]{0:T(128)}, u32[]{:S(2)}) copy-start(f32[64]{0:T(128)} %param.5) | copy-start | bytes 772
  4.0 9.6 %collective-permute-start = (f32[4,16,2048]{2,1,0:T(8,128)}, f32[4,16,2048]{2,1,0:T(8,128)S(1)}, u32[]{:S(2)}, u32[]{:S(2)}) collective-permute-start(f32[4,16,2048]{2,1,0:T(8,128)} %get-tuple-element.29), channel_id=1, source_target_pairs={{0,2},{2,4},{4,6},{6,8},{8,10},{10,12},{12,14},{14,16},{16,18},{18... | collective-permute-start | bytes 1572872 | tf_op jit(solution)/shard_map/ppermute | solution.py:552
  6.4 31.1 %collective-permute-start.1 = (f32[4,48,1024]{2,1,0:T(8,128)}, f32[4,48,1024]{2,1,0:T(8,128)S(1)}, u32[]{:S(2)}, u32[]{:S(2)}) collective-permute-start(f32[4,48,1024]{2,1,0:T(8,128)} %get-tuple-element.34), channel_id=1, source_target_pairs={{0,1},{1,0},{2,3},{3,2},{4,5},{5,4},{6,7},{7,6},{8,9},{9,8},{10,11... | collective-permute-start | bytes 2359304 | tf_op jit(solution)/shard_map/ppermute | solution.py:547
  9.9 1.9 %copy-start = (f32[4,96,2048]{2,1,0:T(8,128)S(1)}, f32[4,96,2048]{2,1,0:T(8,128)}, u32[]{:S(2)}) copy-start(f32[4,96,2048]{2,1,0:T(8,128)} %second.1) | copy-start | bytes 9437188
  11.8 13.7 %copy-start.1 = (f32[4,96,2048]{2,1,0:T(8,128)S(1)}, f32[4,96,2048]{2,1,0:T(8,128)}, u32[]{:S(2)}) copy-start(f32[4,96,2048]{2,1,0:T(8,128)} %second.1) | copy-start | bytes 9437188
  14.3 2.7 %collective-permute-start.2 = (f32[168,128]{1,0:T(8,128)S(1)}, f32[168,128]{1,0:T(8,128)S(1)}, u32[]{:S(2)}, u32[]{:S(2)}) collective-permute-start(f32[168,128]{1,0:T(8,128)S(1)} %get-tuple-element.39), channel_id=1, source_target_pairs={{0,2},{2,0},{4,6},{6,4},{8,10},{10,8},{12,14},{14,12},{16,18},{18,... | collective-permute-start | bytes 258056 | tf_op jit(solution)/shard_map/ppermute | solution.py:547
  17.1 5.5 %collective-permute-start.3 = (f32[168,128]{1,0:T(8,128)S(1)}, f32[168,128]{1,0:T(8,128)S(1)}, u32[]{:S(2)}, u32[]{:S(2)}) collective-permute-start(f32[168,128]{1,0:T(8,128)S(1)} %get-tuple-element.41), channel_id=1, source_target_pairs={{0,4},{2,6},{4,0},{6,2},{8,12},{10,14},{12,8},{14,10},{16,20},{18,... | collective-permute-start | bytes 258056 | tf_op jit(solution)/shard_map/ppermute | solution.py:547
  22.7 5.3 %collective-permute-start.4 = (f32[168,128]{1,0:T(8,128)S(1)}, f32[168,128]{1,0:T(8,128)S(1)}, u32[]{:S(2)}, u32[]{:S(2)}) collective-permute-start(f32[168,128]{1,0:T(8,128)S(1)} %get-tuple-element.43), channel_id=1, source_target_pairs={{0,8},{2,10},{4,12},{6,14},{8,0},{10,2},{12,4},{14,6},{16,24},{18,... | collective-permute-start | bytes 258056 | tf_op jit(solution)/shard_map/ppermute | solution.py:547
  26.2 8.4 %collective-permute-start.7 = (f32[72,1024]{1,0:T(8,128)S(1)}, f32[72,1024]{1,0:T(8,128)S(1)}, u32[]{:S(2)}, u32[]{:S(2)}) collective-permute-start(f32[72,1024]{1,0:T(8,128)S(1)} %shard_map.65), channel_id=1, source_target_pairs={{0,1},{1,0},{2,3},{3,2},{4,5},{5,4},{6,7},{7,6},{8,9},{9,8},{10,11... | collective-permute-start | bytes 884744 | tf_op jit(solution)/shard_map/ppermute | solution.py:547
  28.1 6.5 %collective-permute-start.6 = (f32[424,128]{1,0:T(8,128)S(1)}, f32[424,128]{1,0:T(8,128)S(1)}, u32[]{:S(2)}, u32[]{:S(2)}) collective-permute-start(f32[424,128]{1,0:T(8,128)S(1)} %get-tuple-element.48.refs_0_), channel_id=1, source_target_pairs={{1,2},{2,1},{5,6},{6,5},{9,10},{10,9},{13,14},{14,13},{17,18},{18,... | collective-permute-start | bytes 651272 | tf_op jit(solution)/shard_map/ppermute | solution.py:601
  28.7 5.9 %collective-permute-start.5 = (f32[168,128]{1,0:T(8,128)S(1)}, f32[168,128]{1,0:T(8,128)S(1)}, u32[]{:S(2)}, u32[]{:S(2)}) collective-permute-start(f32[168,128]{1,0:T(8,128)S(1)} %get-tuple-element.45), channel_id=1, source_target_pairs={{0,16},{1,18},{2,17},{3,19},{4,20},{5,22},{6,21},{7,23},{8,24},{9,... | collective-permute-start | bytes 258056 | tf_op jit(solution)/shard_map/ppermute | solution.py:601
  34.7 5.2 %collective-permute-start.8 = (f32[288,128]{1,0:T(8,128)S(1)}, f32[288,128]{1,0:T(8,128)S(1)}, u32[]{:S(2)}, u32[]{:S(2)}) collective-permute-start(f32[288,128]{1,0:T(8,128)S(1)} %get-tuple-element.52), channel_id=1, source_target_pairs={{0,2},{2,0},{4,6},{6,4},{8,10},{10,8},{12,14},{14,12},{16,18},{18,... | collective-permute-start | bytes 442376 | tf_op jit(solution)/shard_map/ppermute | solution.py:547

commit v4 on v3

--- a/solution.py
+++ b/solution.py
@@ -34,29 +34,19 @@
 HBM_SPEC = pl.BlockSpec(memory_space=pltpu.HBM)
 
 
-def leave_kernel(edges, field, tail, *refs):
-    species, _, lines = tail.shape
-    buf, sems = refs[-2:]
-    away = refs[0] if len(refs) > 2 else None
-    copies = []
-    if away is not None:
+def leave_kernel(edges, field, tail, *aways):
+    species = tail.shape[0]
+    for away in aways:
         width = away.shape[2]
         other = pl.ds(pl.multiple_of((1 - lax.axis_index("cross")) * width, LANES), width)
+        for sp in range(species):
+            away[sp] = field[sp, :FIRST, other]
     start = edges[0, 1] - edges[0, 0] - HALO
     rest = start & (SUB - 1)
     whole = pl.multiple_of(start - rest, SUB)
-    window = []
     for sp in range(species):
-        window.append(pltpu.make_async_copy(field.at[sp, pl.ds(whole, HALO + SUB), :], buf.at[sp], sems.at[0, sp]))
-        window[-1].start()
-    for sp in range(species if away is not None else 0):
-        copies.append(pltpu.make_async_copy(field.at[sp, pl.ds(0, FIRST), other], away.at[sp], sems.at[1, sp]))
-        copies[-1].start()
-    for sp in range(species):
-        window[sp].wait()
-        tail[sp] = pltpu.roll(buf[sp], (HALO + SUB - rest) % (HALO + SUB), 0)[:HALO]
-    for copy in copies:
-        copy.wait()
+        rows = field[sp, pl.ds(whole, HALO + SUB), :]
+        tail[sp] = pltpu.roll(rows, (HALO + SUB - rest) % (HALO + SUB), 0)[:HALO]
 
 
 def leaving(edges, field, width):
@@ -67,10 +57,8 @@
     return call(
         leave_kernel,
         tuple(shapes),
-        in_specs=[SMEM_SPEC, HBM_SPEC],
+        in_specs=[SMEM_SPEC, VMEM_SPEC],
         out_specs=(VMEM_SPEC,) * len(shapes),
-        scratch_shapes=[pltpu.VMEM((species, HALO + SUB, lines), F32), pltpu.SemaphoreType.DMA((2, species))],
-        vmem=62 << 20,
     )(edges, field)
 
 
@@ -290,7 +278,7 @@
         jax.ShapeDtypeStruct((rows, width), F32),
         in_specs=[SMEM_SPEC, VMEM_SPEC, VMEM_SPEC],
         out_specs=VMEM_SPEC,
-        cost=400_000_000,
+        cost=20_000_000,
     )(edges, halo, field)
 
 
@@ -323,15 +311,17 @@
             out[k, :, t * LANES : (t + 1) * LANES] = wide[t, k * species : (k + 1) * species]
 
 
-def details(local, edges, factors, first, second, width, species, lines, onto=None):
+def details(local, edges, factors, first, second, width, species, lines, onto=None, part=None):
     chunk = min(width, 512)
     steps = width // chunk
+    begin, count = (0, steps) if part is None else (part, 1)
 
     def here(i):
+        i = i + begin
         return i if width == lines else lax.axis_index("cross") * steps + i
 
     def there(i):
-        return (1 - lax.axis_index("cross")) * steps + i
+        return (1 - lax.axis_index("cross")) * steps + i + begin
 
     if local:
         specs = [
@@ -340,8 +330,8 @@
         ]
     else:
         specs = [
-            pl.BlockSpec((species, FIRST, chunk), lambda i: (0, 0, i)),
-            pl.BlockSpec((second.shape[0], chunk), lambda i: (0, i)),
+            pl.BlockSpec((species, FIRST, chunk), lambda i: (0, 0, i + begin)),
+            pl.BlockSpec((second.shape[0], chunk), lambda i: (0, i + begin)),
         ]
     specs = [SMEM_SPEC, pl.BlockSpec((3 * TILE, 2 * LANES), lambda i: (0, 0))] + specs
     operands = [edges, factors, first, second]
@@ -353,12 +343,12 @@
     return call(
         functools.partial(detail_kernel, local),
         jax.ShapeDtypeStruct((DETAILS, species, lines), F32),
-        grid=(steps,),
+        grid=(count,),
         in_specs=specs,
         out_specs=pl.BlockSpec((DETAILS, species, chunk), lambda i: (0, 0, here(i) if local else there(i))),
         scratch_shapes=[pltpu.VMEM((chunk // LANES, TILE * species, LANES), F32)],
         input_output_aliases=alias,
-        cost=2_000_000_000,
+        cost=20_000_000,
     )(*operands)
 
 
@@ -594,12 +584,18 @@
     if swapped:
         rest_in = from_partner(rest_away(brick_edges, halo, field, width), "cross", 1)
 
+    if swapped:
+        near = details(True, brick_edges, factors, halo, field, width, species, lines)
     send, carried = other_half, own_half
     for level in range(depth):
-        if swapped and level == depth - 1:
+        last = level == depth - 1
+        if swapped and level == depth - 2:
+            send, near = lax.optimization_barrier((send, near))
+        if swapped and last:
             partner_route, own_route = last_routes(slabs)
             operands = (carried, lax.ppermute(send, both, partner_route), lax.ppermute(carried, both, own_route))
-            operands, rest_in = lax.optimization_barrier((operands, rest_in))
+            tile_detail = details(False, brick_edges, factors, first_in, rest_in, width, species, lines, near)
+            operands, tile_detail = lax.optimization_barrier((operands, tile_detail))
         else:
             operands = (carried, from_partner(send, "slab", 1 << level))
         send, carried = merge(level, depth, rows, swapped, *operands)
@@ -609,8 +605,6 @@
     if swapped:
         tree_detail, coarse_final = finish(here_set, partner_set, species, lines)
         coarse_final = coarse_final.transpose(1, 0, 2)
-        tile_detail = details(True, brick_edges, factors, halo, field, width, species, lines)
-        tile_detail = details(False, brick_edges, factors, first_in, rest_in, width, species, lines, tile_detail)
     else:
         core = lax.axis_index("slab") % 2
         first = jnp.where(core == 0, here_set, partner_set)

time: 40.9 us -> 39.7 us (0.971)
  Pallas kernels: 13.4 us -> 10.8 us
  waiting for transfers between devices: 4.32 us -> 5.31 us
  local copies, waits for them, and re-layouts: 1.97 us -> 2.62 us
  starting transfers between devices: 20.3 us -> 19.7 us
    pallas_call x1, Pallas kernels: 3.38 us -> 0.7 us  [leaving(): call(leave_kernel, tuple(shapes), in_specs=[SMEM_SPEC, VMEM_SPEC], out_sp...]
    ppermute x6, waiting for transfers between devices: 4.31 us -> 5.3 us  [from_partner(): return lax.ppermute(block, axis, [(i, i ^ step) for i in range(count)])]
    ppermute x6, starting transfers between devices: 14.1 us -> 13.5 us  [from_partner(): return lax.ppermute(block, axis, [(i, i ^ step) for i in range(count)])]
    unnamed x8 -> x10, local copies, waits for them, and re-layouts: 1.9 us -> 2.55 us
  transfers between devices with their start and end apart: 9 -> 9, of which waited for: 4 -> 5; matrix products, arithmetic and copies ran while one was open for 0% -> 0% of each run, Pallas kernels for 23% -> 23%
where the time goes in v4:
time: 39.7 us; the launch traced here: 39.2 us
  starting transfers between devices  19.7 us (50%)
  Pallas kernels  10.8 us (27%)
  waiting for transfers between devices  5.31 us (13%)
  local copies, waits for them, and re-layouts  2.62 us (7%)
  between operations  0.72 us (2%)
    ppermute x6, starting transfers between devices, from_partner(): return lax.ppermute(block, axis, [(i, i ^ step) for i in range(count)])  13.5 us
    ppermute x6, waiting for transfers between devices, from_partner(): return lax.ppermute(block, axis, [(i, i ^ step) for i in range(count)])  5.3 us
    pallas_call x2, Pallas kernels, details(): call(functools.partial(detail_kernel, local), jax.ShapeDtypeStruct((DETAI...  4.78 us
    ppermute x1, starting transfers between devices, on_device(): lax.ppermute(send, both, partner_route)  3.1 us
    unnamed x10, local copies, waits for them, and re-layouts  2.55 us
    ppermute x1, starting transfers between devices, shifted(): return lax.ppermute(block, axis, [(i, i + 1) for i in range(count - 1)])  2.52 us
    pallas_call x1, Pallas kernels, brick_part(): call(brick_kernel, jax.ShapeDtypeStruct((dense, LANES), F32), grid=(speci...  1.87 us
    pallas_call x1, Pallas kernels, tile_matrix(): call(matrix_kernel, (jax.ShapeDtypeStruct((3 * TILE, 2 * LANES), BF16), j...  0.98 us
  transfers between devices with their start and end apart: 9, of which 5 were waited for; matrix products, arithmetic and copies ran while one was open for 0% of the time, Pallas kernels for 23%

profile of v4, /device:TPU:0, one launch (start us, length us, event | category | flops | bytes accessed | tf_op | source)
XLA Modules:
  0.0 39.2 jit_solution(7096850509429487653)
XLA Ops:
  0.6 0.0 copy-start
  0.6 1.9 %copy-done = f32[4,96,2048]{2,1,0:T(8,128)S(1)} copy-done((f32[4,96,2048]{2,1,0:T(8,128)S(1)}, f32[4,96,2048]{2,1,0:T(8,128)}, u32[]{:S(2)}) %copy-start) | copy-done | bytes 3145752
  2.5 0.0 copy-start.2
  2.5 0.7 %copy-done.2 = s32[1,2]{1,0:T(1,128)S(1)} copy-done((s32[1,2]{1,0:T(1,128)S(1)}, s32[1,2]{1,0:T(1,128)}, u32[]{:S(2)}) %copy-start.2) | copy-done | bytes 32
  3.2 0.0 copy-start.4
  3.2 0.0 copy-start.3
  3.2 0.0 copy-start.1
  3.2 0.7 %shard_map.59 = (f32[4,16,2048]{2,1,0:T(8,128)S(1)}, f32[4,48,1024]{2,1,0:T(8,128)S(1)}) custom-call(s32[1,2]{1,0:T(1,128)S(1)} %copy-done.2, f32[4,96,2048]{2,1,0:T(8,128)S(1)} %copy-done), custom_call_target="tpu_custom_call" | custom-call | tf_op jit(solution)/shard_map/pallas_call | solution.py:57
  3.9 2.5 %collective-permute-start = (f32[4,16,2048]{2,1,0:T(8,128)S(1)}, f32[4,16,2048]{2,1,0:T(8,128)S(1)}, u32[]{:S(2)}, u32[]{:S(2)}) collective-permute-start(f32[4,16,2048]{2,1,0:T(8,128)S(1)} %get-tuple-element.32), channel_id=1, source_target_pairs={{0,2},{2,4},{4,6},{6,8},{8,10},{10,12},{12,14},{14,16},{16,18},{18... | collective-permute-start | bytes 1572872 | tf_op jit(solution)/shard_map/ppermute | solution.py:542
  6.4 2.4 %collective-permute-start.6 = (f32[4,48,1024]{2,1,0:T(8,128)S(1)}, f32[4,48,1024]{2,1,0:T(8,128)S(1)}, u32[]{:S(2)}, u32[]{:S(2)}) collective-permute-start(f32[4,48,1024]{2,1,0:T(8,128)S(1)} %get-tuple-element.49), channel_id=1, source_target_pairs={{0,1},{1,0},{2,3},{3,2},{4,5},{5,4},{6,7},{7,6},{8,9},{9,8},{10,11... | collective-permute-start | bytes 2359304 | tf_op jit(solution)/shard_map/ppermute | solution.py:537
  8.8 0.0 copy-done.4
  8.8 0.1 broadcast_in_dim.2.widths
  8.9 0.0 copy-done.3
  8.9 1.0 %shard_map.58 = (bf16[192,256]{1,0:T(8,128)(2,1)S(1)}, f32[8,128]{1,0:T(8,128)S(1)}, f32[8,128]{1,0:T(8,128)S(1)}) custom-call(s32[1,2]{1,0:T(1,128)S(1)} %copy-done.3, f32[64,128]{1,0:T(8,128)S(1)} %broadcast_in_dim.2.widths), custom_call_target="tpu_custom_call" | custom-call | tf_op jit(solution)/shard_map/pallas_call | solution.py:156
  9.9 0.0 copy-done.1
  9.9 1.9 %shard_map.60.part = f32[328,128]{1,0:T(8,128)S(1)} custom-call(f32[8,128]{1,0:T(8,128)S(1)} %get-tuple-element.31.weights, f32[8,128]{1,0:T(8,128)S(1)} %get-tuple-element.33.coarse_width, f32[4,96,2048]{2,1,0:T(8,128)S(1)} %copy-done.1), custom_call_target="tpu_custom_call" | custom-call | tf_op jit(solution)/shard_map/pallas_call | solution.py:207
  11.8 0.0 collective-permute-done.halo.first
  11.8 0.6 %shard_map.61 = (f32[168,128]{1,0:T(8,128)S(1)}, f32[168,128]{1,0:T(8,128)S(1)}) custom-call(f32[8,128]{1,0:T(8,128)S(1)} %get-tuple-element.31.weights, f32[4,16,2048]{2,1,0:T(8,128)S(1)} %collective-permute-done.halo.first, f32[328,128]{1,0:T(8,128)S(1)} %shard_map.60.part), custom_call_target="tpu_custom_call" | custom-call | tf_op jit(solution)/shard_map/pallas_call | solution.py:239
  12.4 3.4 %collective-permute-start.1 = (f32[168,128]{1,0:T(8,128)S(1)}, f32[168,128]{1,0:T(8,128)S(1)}, u32[]{:S(2)}, u32[]{:S(2)}) collective-permute-start(f32[168,128]{1,0:T(8,128)S(1)} %get-tuple-element.39), channel_id=1, source_target_pairs={{0,2},{2,0},{4,6},{6,4},{8,10},{10,8},{12,14},{14,12},{16,18},{18,... | collective-permute-start | bytes 258056 | tf_op jit(solution)/shard_map/ppermute | solution.py:537
  15.8 0.9 %collective-permute-done.1.refs_1_ = f32[168,128]{1,0:T(8,128)S(1)} collective-permute-done((f32[168,128]{1,0:T(8,128)S(1)}, f32[168,128]{1,0:T(8,128)S(1)}, u32[]{:S(2)}, u32[]{:S(2)}) %collective-permute-start.1) | collective-permute-done | bytes 86048 | tf_op jit(solution)/shard_map/ppermute | solution.py:537
  16.7 0.1 shard_map.62
  16.8 2.8 %collective-permute-start.2 = (f32[168,128]{1,0:T(8,128)S(1)}, f32[168,128]{1,0:T(8,128)S(1)}, u32[]{:S(2)}, u32[]{:S(2)}) collective-permute-start(f32[168,128]{1,0:T(8,128)S(1)} %get-tuple-element.41), channel_id=1, source_target_pairs={{0,4},{2,6},{4,0},{6,2},{8,12},{10,14},{12,8},{14,10},{16,20},{18,... | collective-permute-start | bytes 258056 | tf_op jit(solution)/shard_map/ppermute | solution.py:537
  19.5 2.4 %shard_map.64.rest_0_ = f32[60,4,2048]{2,1,0:T(4,128)} custom-call(s32[1,2]{1,0:T(1,128)S(1)} %copy-done.3, bf16[192,256]{1,0:T(8,128)(2,1)S(1)} %get-tuple-element.44.factors, f32[4,16,2048]{2,1,0:T(8,128)S(1)} %collective-permute-done.halo.first, f32[4,96,2048]{2,1,0:T(8,128)S(1)} %copy-done.1), custom_call_target="tpu_custom_call" | custom-call | flops 20000000 | bytes 200000 | tf_op jit(solution)/shard_map/pallas_call | solution.py:343
  22.0 0.4 %collective-permute-done.2.refs_1_ = f32[168,128]{1,0:T(8,128)S(1)} collective-permute-done((f32[168,128]{1,0:T(8,128)S(1)}, f32[168,128]{1,0:T(8,128)S(1)}, u32[]{:S(2)}, u32[]{:S(2)}) %collective-permute-start.2) | collective-permute-done | bytes 86048 | tf_op jit(solution)/shard_map/ppermute | solution.py:537
  22.4 0.1 shard_map.63
  22.5 2.8 %collective-permute-start.3 = (f32[168,128]{1,0:T(8,128)S(1)}, f32[168,128]{1,0:T(8,128)S(1)}, u32[]{:S(2)}, u32[]{:S(2)}) collective-permute-start(f32[168,128]{1,0:T(8,128)S(1)} %get-tuple-element.46), channel_id=1, source_target_pairs={{0,8},{2,10},{4,12},{6,14},{8,0},{10,2},{12,4},{14,6},{16,24},{18,... | collective-permute-start | bytes 258056 | tf_op jit(solution)/shard_map/ppermute | solution.py:537
  25.3 0.7 %shard_map.66 = f32[72,1024]{1,0:T(8,128)S(1)} custom-call(s32[1,2]{1,0:T(1,128)S(1)} %copy-done.3, f32[4,16,2048]{2,1,0:T(8,128)S(1)} %collective-permute-done.halo.first, f32[4,96,2048]{2,1,0:T(8,128)S(1)} %copy-done.1), custom_call_target="tpu_custom_call" | custom-call | flops 20000000 | bytes 200000 | tf_op jit(solution)/shard_map/pallas_call | solution.py:276
  25.9 1.6 %collective-permute-start.7 = (f32[72,1024]{1,0:T(8,128)S(1)}, f32[72,1024]{1,0:T(8,128)S(1)}, u32[]{:S(2)}, u32[]{:S(2)}) collective-permute-start(f32[72,1024]{1,0:T(8,128)S(1)} %shard_map.66), channel_id=1, source_target_pairs={{0,1},{1,0},{2,3},{3,2},{4,5},{5,4},{6,7},{7,6},{8,9},{9,8},{10,11... | collective-permute-start | bytes 884744 | tf_op jit(solution)/shard_map/ppermute | solution.py:537
  27.5 0.2 collective-permute-done.3.refs_1_
  27.7 0.1 shard_map.65
  27.8 0.7 %collective-permute-start.5 = (f32[424,128]{1,0:T(8,128)S(1)}, f32[424,128]{1,0:T(8,128)S(1)}, u32[]{:S(2)}, u32[]{:S(2)}) collective-permute-start(f32[424,128]{1,0:T(8,128)S(1)} %get-tuple-element.52.refs_0_), channel_id=1, source_target_pairs={{1,2},{2,1},{5,6},{6,5},{9,10},{10,9},{13,14},{14,13},{17,18},{18,... | collective-permute-start | bytes 651272 | tf_op jit(solution)/shard_map/ppermute | solution.py:596
  28.5 3.1 %collective-permute-start.4 = (f32[168,128]{1,0:T(8,128)S(1)}, f32[168,128]{1,0:T(8,128)S(1)}, u32[]{:S(2)}, u32[]{:S(2)}) collective-permute-start(f32[168,128]{1,0:T(8,128)S(1)} %get-tuple-element.48), channel_id=1, source_target_pairs={{0,16},{1,18},{2,17},{3,19},{4,20},{5,22},{6,21},{7,23},{8,24},{9,... | collective-permute-start | bytes 258056 | tf_op jit(solution)/shard_map/ppermute | solution.py:596
  31.6 0.0 collective-permute-done.6.first
  31.6 2.8 %collective-permute-done.7.second = f32[72,1024]{1,0:T(8,128)S(1)} collective-permute-done((f32[72,1024]{1,0:T(8,128)S(1)}, f32[72,1024]{1,0:T(8,128)S(1)}, u32[]{:S(2)}, u32[]{:S(2)}) %collective-permute-start.7) | collective-permute-done | bytes 294944 | tf_op jit(solution)/shard_map/ppermute | solution.py:537
  34.4 2.3 %shard_map.67 = f32[60,4,2048]{2,1,0:T(4,128)} custom-call(s32[1,2]{1,0:T(1,128)S(1)} %copy-done.3, bf16[192,256]{1,0:T(8,128)(2,1)S(1)} %get-tuple-element.44.factors, f32[4,48,1024]{2,1,0:T(8,128)S(1)} %collective-permute-done.6.first, f32[72,1024]{1,0:T(8,128)S(1)} %collective-permute-done.7.second, ...), custom_call_target="tpu_custom_call", output_to_operand_aliasing={{}: (4, {})} | custom-call | flops 20000000 | bytes 200000 | tf_op jit(solution)/shard_map/pallas_call | solution.py:343
  36.7 0.0 collective-permute-done.4.refs_1_
  36.7 0.0 collective-permute-done.5.refs_2_
  36.7 0.1 shard_map.68
  36.8 0.5 %collective-permute-start.8 = (f32[288,128]{1,0:T(8,128)S(1)}, f32[288,128]{1,0:T(8,128)S(1)}, u32[]{:S(2)}, u32[]{:S(2)}) collective-permute-start(f32[288,128]{1,0:T(8,128)S(1)} %get-tuple-element.56), channel_id=1, source_target_pairs={{0,2},{2,0},{4,6},{6,4},{8,10},{10,8},{12,14},{14,12},{16,18},{18,... | collective-permute-start | bytes 442376 | tf_op jit(solution)/shard_map/ppermute | solution.py:537
  37.3 1.0 %collective-permute-done.8.other = f32[288,128]{1,0:T(8,128)S(1)} collective-permute-done((f32[288,128]{1,0:T(8,128)S(1)}, f32[288,128]{1,0:T(8,128)S(1)}, u32[]{:S(2)}, u32[]{:S(2)}) %collective-permute-start.8) | collective-permute-done | bytes 147488 | tf_op jit(solution)/shard_map/ppermute | solution.py:537
  38.3 0.8 %shard_map.69 = (f32[4,4,2048]{2,1,0:T(4,128)}, f32[5,4,2048]{2,1,0:T(4,128)}) custom-call(f32[288,128]{1,0:T(8,128)S(1)} %get-tuple-element.55.own, f32[288,128]{1,0:T(8,128)S(1)} %collective-permute-done.8.other), custom_call_target="tpu_custom_call" | custom-call | tf_op jit(solution)/shard_map/pallas_call | solution.py:523
Async XLA Ops:
  0.6 1.9 %copy-start = (f32[4,96,2048]{2,1,0:T(8,128)S(1)}, f32[4,96,2048]{2,1,0:T(8,128)}, u32[]{:S(2)}) copy-start(f32[4,96,2048]{2,1,0:T(8,128)} %field.5) | copy-start | bytes 9437188
  2.5 0.7 %copy-start.2 = (s32[1,2]{1,0:T(1,128)S(1)}, s32[1,2]{1,0:T(1,128)}, u32[]{:S(2)}) copy-start(s32[1,2]{1,0:T(1,128)} %edges.9) | copy-start | bytes 28
  3.2 5.7 %copy-start.4 = (f32[64]{0:T(128)S(1)}, f32[64]{0:T(128)}, u32[]{:S(2)}) copy-start(f32[64]{0:T(128)} %param.5) | copy-start | bytes 772
  3.2 5.7 %copy-start.3 = (s32[1,2]{1,0:T(1,128)S(1)}, s32[1,2]{1,0:T(1,128)}, u32[]{:S(2)}) copy-start(s32[1,2]{1,0:T(1,128)} %edges.9) | copy-start | bytes 28
  3.2 6.7 %copy-start.1 = (f32[4,96,2048]{2,1,0:T(8,128)S(1)}, f32[4,96,2048]{2,1,0:T(8,128)}, u32[]{:S(2)}) copy-start(f32[4,96,2048]{2,1,0:T(8,128)} %field.5) | copy-start | bytes 9437188
  3.9 7.9 %collective-permute-start = (f32[4,16,2048]{2,1,0:T(8,128)S(1)}, f32[4,16,2048]{2,1,0:T(8,128)S(1)}, u32[]{:S(2)}, u32[]{:S(2)}) collective-permute-start(f32[4,16,2048]{2,1,0:T(8,128)S(1)} %get-tuple-element.32), channel_id=1, source_target_pairs={{0,2},{2,4},{4,6},{6,8},{8,10},{10,12},{12,14},{14,16},{16,18},{18... | collective-permute-start | bytes 1572872 | tf_op jit(solution)/shard_map/ppermute | solution.py:542
  6.4 25.2 %collective-permute-start.6 = (f32[4,48,1024]{2,1,0:T(8,128)S(1)}, f32[4,48,1024]{2,1,0:T(8,128)S(1)}, u32[]{:S(2)}, u32[]{:S(2)}) collective-permute-start(f32[4,48,1024]{2,1,0:T(8,128)S(1)} %get-tuple-element.49), channel_id=1, source_target_pairs={{0,1},{1,0},{2,3},{3,2},{4,5},{5,4},{6,7},{7,6},{8,9},{9,8},{10,11... | collective-permute-start | bytes 2359304 | tf_op jit(solution)/shard_map/ppermute | solution.py:537
  12.4 4.3 %collective-permute-start.1 = (f32[168,128]{1,0:T(8,128)S(1)}, f32[168,128]{1,0:T(8,128)S(1)}, u32[]{:S(2)}, u32[]{:S(2)}) collective-permute-start(f32[168,128]{1,0:T(8,128)S(1)} %get-tuple-element.39), channel_id=1, source_target_pairs={{0,2},{2,0},{4,6},{6,4},{8,10},{10,8},{12,14},{14,12},{16,18},{18,... | collective-permute-start | bytes 258056 | tf_op jit(solution)/shard_map/ppermute | solution.py:537
  16.8 5.6 %collective-permute-start.2 = (f32[168,128]{1,0:T(8,128)S(1)}, f32[168,128]{1,0:T(8,128)S(1)}, u32[]{:S(2)}, u32[]{:S(2)}) collective-permute-start(f32[168,128]{1,0:T(8,128)S(1)} %get-tuple-element.41), channel_id=1, source_target_pairs={{0,4},{2,6},{4,0},{6,2},{8,12},{10,14},{12,8},{14,10},{16,20},{18,... | collective-permute-start | bytes 258056 | tf_op jit(solution)/shard_map/ppermute | solution.py:537
  22.5 5.3 %collective-permute-start.3 = (f32[168,128]{1,0:T(8,128)S(1)}, f32[168,128]{1,0:T(8,128)S(1)}, u32[]{:S(2)}, u32[]{:S(2)}) collective-permute-start(f32[168,128]{1,0:T(8,128)S(1)} %get-tuple-element.46), channel_id=1, source_target_pairs={{0,8},{2,10},{4,12},{6,14},{8,0},{10,2},{12,4},{14,6},{16,24},{18,... | collective-permute-start | bytes 258056 | tf_op jit(solution)/shard_map/ppermute | solution.py:537
  25.9 8.4 %collective-permute-start.7 = (f32[72,1024]{1,0:T(8,128)S(1)}, f32[72,1024]{1,0:T(8,128)S(1)}, u32[]{:S(2)}, u32[]{:S(2)}) collective-permute-start(f32[72,1024]{1,0:T(8,128)S(1)} %shard_map.66), channel_id=1, source_target_pairs={{0,1},{1,0},{2,3},{3,2},{4,5},{5,4},{6,7},{7,6},{8,9},{9,8},{10,11... | collective-permute-start | bytes 884744 | tf_op jit(solution)/shard_map/ppermute | solution.py:537
  27.8 8.9 %collective-permute-start.5 = (f32[424,128]{1,0:T(8,128)S(1)}, f32[424,128]{1,0:T(8,128)S(1)}, u32[]{:S(2)}, u32[]{:S(2)}) collective-permute-start(f32[424,128]{1,0:T(8,128)S(1)} %get-tuple-element.52.refs_0_), channel_id=1, source_target_pairs={{1,2},{2,1},{5,6},{6,5},{9,10},{10,9},{13,14},{14,13},{17,18},{18,... | collective-permute-start | bytes 651272 | tf_op jit(solution)/shard_map/ppermute | solution.py:596
  28.5 8.2 %collective-permute-start.4 = (f32[168,128]{1,0:T(8,128)S(1)}, f32[168,128]{1,0:T(8,128)S(1)}, u32[]{:S(2)}, u32[]{:S(2)}) collective-permute-start(f32[168,128]{1,0:T(8,128)S(1)} %get-tuple-element.48), channel_id=1, source_target_pairs={{0,16},{1,18},{2,17},{3,19},{4,20},{5,22},{6,21},{7,23},{8,24},{9,... | collective-permute-start | bytes 258056 | tf_op jit(solution)/shard_map/ppermute | solution.py:596
  36.8 1.5 %collective-permute-start.8 = (f32[288,128]{1,0:T(8,128)S(1)}, f32[288,128]{1,0:T(8,128)S(1)}, u32[]{:S(2)}, u32[]{:S(2)}) collective-permute-start(f32[288,128]{1,0:T(8,128)S(1)} %get-tuple-element.56), channel_id=1, source_target_pairs={{0,2},{2,0},{4,6},{6,4},{8,10},{10,8},{12,14},{14,12},{16,18},{18,... | collective-permute-start | bytes 442376 | tf_op jit(solution)/shard_map/ppermute | solution.py:537

commit v5 on v4

--- a/solution.py
+++ b/solution.py
@@ -34,32 +34,42 @@
 HBM_SPEC = pl.BlockSpec(memory_space=pltpu.HBM)
 
 
-def leave_kernel(edges, field, tail, *aways):
-    species = tail.shape[0]
-    for away in aways:
-        width = away.shape[2]
-        other = pl.ds(pl.multiple_of((1 - lax.axis_index("cross")) * width, LANES), width)
-        for sp in range(species):
-            away[sp] = field[sp, :FIRST, other]
-    start = edges[0, 1] - edges[0, 0] - HALO
+LOW = TILE // 2
+
+
+def tail_kernel(edges, rows, tail):
+    start = edges[0, 1] - edges[0, 0] - HALO - LOW
     rest = start & (SUB - 1)
     whole = pl.multiple_of(start - rest, SUB)
+    for sp in range(tail.shape[0]):
+        window = rows[sp, pl.ds(whole, HALO + SUB), :]
+        tail[sp] = pltpu.roll(window, (HALO + SUB - rest) % (HALO + SUB), 0)[:HALO]
+
+
+def brick_tail(edges, field):
+    species, _, lines = field.shape
+    return call(
+        tail_kernel,
+        jax.ShapeDtypeStruct((species, HALO, lines), F32),
+        in_specs=[SMEM_SPEC, VMEM_SPEC],
+        out_specs=VMEM_SPEC,
+    )(edges, field[:, LOW : LOW + TILE])
+
+
+def first_kernel(field, away):
+    species, _, width = away.shape
+    other = pl.ds(pl.multiple_of((1 - lax.axis_index("cross")) * width, LANES), width)
     for sp in range(species):
-        rows = field[sp, pl.ds(whole, HALO + SUB), :]
-        tail[sp] = pltpu.roll(rows, (HALO + SUB - rest) % (HALO + SUB), 0)[:HALO]
-
-
-def leaving(edges, field, width):
-    species, _, lines = field.shape
-    shapes = [jax.ShapeDtypeStruct((species, HALO, lines), F32)]
-    if width < lines:
-        shapes.append(jax.ShapeDtypeStruct((species, FIRST, width), F32))
-    return call(
-        leave_kernel,
-        tuple(shapes),
-        in_specs=[SMEM_SPEC, VMEM_SPEC],
-        out_specs=(VMEM_SPEC,) * len(shapes),
-    )(edges, field)
+        away[sp] = field[sp, :FIRST, other]
+
+
+def first_rows(field, width):
+    return call(
+        first_kernel,
+        jax.ShapeDtypeStruct((field.shape[0], FIRST, width), F32),
+        in_specs=[VMEM_SPEC],
+        out_specs=VMEM_SPEC,
+    )(field)
 
 
 PAD = 32
@@ -572,10 +582,9 @@
     both = ("slab", "cross")
 
     field = sim_field
-    tail, *away = leaving(brick_edges, field, width)
+    halo = shifted(brick_tail(brick_edges, field), "slab")
     if swapped:
-        first_in = from_partner(away[0], "cross", 1)
-    halo = shifted(tail, "slab")
+        first_in = from_partner(first_rows(field, width), "cross", 1)
     factors, weights, coarse_width = tile_matrix(brick_edges, cell_width)
     part = brick_part(weights, coarse_width, field)
     halo, part, factors = lax.optimization_barrier((halo, part, factors))

time: 39.7 us -> 39.4 us (level)
  the two profiles are of different devices: /device:TPU:0 before, /device:TPU:5 now
where the time goes in v5:
time: 39.4 us; the launch traced here: 39.2 us
  starting transfers between devices  16.6 us (42%)
  Pallas kernels  10.8 us (27%)
  waiting for transfers between devices  9.05 us (23%)
  local copies, waits for them, and re-layouts  1.97 us (5%)
  between operations  0.76 us (2%)
    ppermute x6, starting transfers between devices, from_partner(): return lax.ppermute(block, axis, [(i, i ^ step) for i in range(count)])  9.73 us
    ppermute x6, waiting for transfers between devices, from_partner(): return lax.ppermute(block, axis, [(i, i ^ step) for i in range(count)])  6.25 us
    pallas_call x2, Pallas kernels, details(): call(functools.partial(detail_kernel, local), jax.ShapeDtypeStruct((DETAI...  4.79 us
    ppermute x1, starting transfers between devices, shifted(): return lax.ppermute(block, axis, [(i, i + 1) for i in range(count - 1)])  3.68 us
    ppermute x1, waiting for transfers between devices, shifted(): return lax.ppermute(block, axis, [(i, i + 1) for i in range(count - 1)])  2.8 us
    ppermute x1, starting transfers between devices, on_device(): lax.ppermute(send, both, partner_route)  2.54 us
    slice x1, local copies, waits for them, and re-layouts, brick_tail(): field[:, LOW:LOW + TILE]  1.88 us
    pallas_call x1, Pallas kernels, brick_part(): call(brick_kernel, jax.ShapeDtypeStruct((dense, LANES), F32), grid=(speci...  1.87 us
  transfers between devices with their start and end apart: 9, of which 6 were waited for; matrix products, arithmetic and copies ran while one was open for 0% of the time, Pallas kernels for 23%

profile of v5, /device:TPU:5, one launch (start us, length us, event | category | flops | bytes accessed | tf_op | source)
XLA Modules:
  0.0 39.2 jit_solution(14235197774287155871)
XLA Ops:
  0.6 0.0 copy-start.1
  0.6 0.0 copy-start
  0.6 1.9 %slice.3.rows = f32[4,64,2048]{2,1,0:T(8,128)S(1)} slice(f32[4,96,2048]{2,1,0:T(8,128)} %field.5), slice={[0:4], [32:96], [0:2048]} | slice | bytes 4194304 | tf_op jit(solution)/shard_map/slice | solution.py:56
  2.5 0.0 copy-done.1
  2.6 0.7 %shard_map.59 = f32[4,16,2048]{2,1,0:T(8,128)S(1)} custom-call(s32[1,2]{1,0:T(1,128)S(1)} %copy-done.1, f32[4,64,2048]{2,1,0:T(8,128)S(1)} %slice.3.rows), custom_call_target="tpu_custom_call" | custom-call | tf_op jit(solution)/shard_map/pallas_call | solution.py:51
  3.2 0.0 copy-start.2
  3.2 3.7 %collective-permute-start = (f32[4,16,2048]{2,1,0:T(8,128)S(1)}, f32[4,16,2048]{2,1,0:T(8,128)S(1)}, u32[]{:S(2)}, u32[]{:S(2)}) collective-permute-start(f32[4,16,2048]{2,1,0:T(8,128)S(1)} %shard_map.59), channel_id=1, source_target_pairs={{0,2},{2,4},{4,6},{6,8},{8,10},{10,12},{12,14},{14,16},{16,18},{18... | collective-permute-start | bytes 1572872 | tf_op jit(solution)/shard_map/ppermute | solution.py:552
  6.9 0.0 copy-done
  6.9 0.1 shard_map.66
  7.0 0.3 collective-permute-start.6
  7.3 0.0 copy-done.2
  7.3 0.1 broadcast_in_dim.2.widths
  7.4 1.0 %shard_map.58 = (bf16[192,256]{1,0:T(8,128)(2,1)S(1)}, f32[8,128]{1,0:T(8,128)S(1)}, f32[8,128]{1,0:T(8,128)S(1)}) custom-call(s32[1,2]{1,0:T(1,128)S(1)} %copy-done.1, f32[64,128]{1,0:T(8,128)S(1)} %broadcast_in_dim.2.widths), custom_call_target="tpu_custom_call" | custom-call | tf_op jit(solution)/shard_map/pallas_call | solution.py:166
  8.3 1.9 %shard_map.60.part = f32[328,128]{1,0:T(8,128)S(1)} custom-call(f32[8,128]{1,0:T(8,128)S(1)} %get-tuple-element.29.weights, f32[8,128]{1,0:T(8,128)S(1)} %get-tuple-element.30.coarse_width, f32[4,96,2048]{2,1,0:T(8,128)S(1)} %copy-done), custom_call_target="tpu_custom_call" | custom-call | tf_op jit(solution)/shard_map/pallas_call | solution.py:217
  10.2 2.8 %collective-permute-done.halo.first = f32[4,16,2048]{2,1,0:T(8,128)S(1)} collective-permute-done((f32[4,16,2048]{2,1,0:T(8,128)S(1)}, f32[4,16,2048]{2,1,0:T(8,128)S(1)}, u32[]{:S(2)}, u32[]{:S(2)}) %collective-permute-start) | collective-permute-done | bytes 524320 | tf_op jit(solution)/shard_map/ppermute | solution.py:552
  13.0 0.6 %shard_map.61 = (f32[168,128]{1,0:T(8,128)S(1)}, f32[168,128]{1,0:T(8,128)S(1)}) custom-call(f32[8,128]{1,0:T(8,128)S(1)} %get-tuple-element.29.weights, f32[4,16,2048]{2,1,0:T(8,128)S(1)} %collective-permute-done.halo.first, f32[328,128]{1,0:T(8,128)S(1)} %shard_map.60.part), custom_call_target="tpu_custom_call" | custom-call | tf_op jit(solution)/shard_map/pallas_call | solution.py:249
  13.6 0.1 collective-permute-start.1
  13.7 1.3 %collective-permute-done.1.refs_1_ = f32[168,128]{1,0:T(8,128)S(1)} collective-permute-done((f32[168,128]{1,0:T(8,128)S(1)}, f32[168,128]{1,0:T(8,128)S(1)}, u32[]{:S(2)}, u32[]{:S(2)}) %collective-permute-start.1) | collective-permute-done | bytes 86048 | tf_op jit(solution)/shard_map/ppermute | solution.py:547
  15.0 0.1 shard_map.62
  15.0 2.3 %collective-permute-start.2 = (f32[168,128]{1,0:T(8,128)S(1)}, f32[168,128]{1,0:T(8,128)S(1)}, u32[]{:S(2)}, u32[]{:S(2)}) collective-permute-start(f32[168,128]{1,0:T(8,128)S(1)} %get-tuple-element.38), channel_id=1, source_target_pairs={{0,4},{2,6},{4,0},{6,2},{8,12},{10,14},{12,8},{14,10},{16,20},{18,... | collective-permute-start | bytes 258056 | tf_op jit(solution)/shard_map/ppermute | solution.py:547
  17.4 2.5 %shard_map.64.rest_0_ = f32[60,4,2048]{2,1,0:T(4,128)} custom-call(s32[1,2]{1,0:T(1,128)S(1)} %copy-done.1, bf16[192,256]{1,0:T(8,128)(2,1)S(1)} %get-tuple-element.41.factors, f32[4,16,2048]{2,1,0:T(8,128)S(1)} %collective-permute-done.halo.first, f32[4,96,2048]{2,1,0:T(8,128)S(1)} %copy-done), custom_call_target="tpu_custom_call" | custom-call | flops 20000000 | bytes 200000 | tf_op jit(solution)/shard_map/pallas_call | solution.py:353
  19.8 0.2 collective-permute-done.2.refs_1_
  20.0 0.1 shard_map.63
  20.1 2.2 %collective-permute-start.3 = (f32[168,128]{1,0:T(8,128)S(1)}, f32[168,128]{1,0:T(8,128)S(1)}, u32[]{:S(2)}, u32[]{:S(2)}) collective-permute-start(f32[168,128]{1,0:T(8,128)S(1)} %get-tuple-element.43), channel_id=1, source_target_pairs={{0,8},{2,10},{4,12},{6,14},{8,0},{10,2},{12,4},{14,6},{16,24},{18,... | collective-permute-start | bytes 258056 | tf_op jit(solution)/shard_map/ppermute | solution.py:547
  22.2 0.7 %shard_map.67 = f32[72,1024]{1,0:T(8,128)S(1)} custom-call(s32[1,2]{1,0:T(1,128)S(1)} %copy-done.1, f32[4,16,2048]{2,1,0:T(8,128)S(1)} %collective-permute-done.halo.first, f32[4,96,2048]{2,1,0:T(8,128)S(1)} %copy-done), custom_call_target="tpu_custom_call" | custom-call | flops 20000000 | bytes 200000 | tf_op jit(solution)/shard_map/pallas_call | solution.py:286
  22.9 0.3 collective-permute-start.7
  23.2 1.2 %collective-permute-done.3.refs_1_ = f32[168,128]{1,0:T(8,128)S(1)} collective-permute-done((f32[168,128]{1,0:T(8,128)S(1)}, f32[168,128]{1,0:T(8,128)S(1)}, u32[]{:S(2)}, u32[]{:S(2)}) %collective-permute-start.3) | collective-permute-done | bytes 86048 | tf_op jit(solution)/shard_map/ppermute | solution.py:547
  24.4 0.1 shard_map.65
  24.5 0.7 %collective-permute-start.5 = (f32[424,128]{1,0:T(8,128)S(1)}, f32[424,128]{1,0:T(8,128)S(1)}, u32[]{:S(2)}, u32[]{:S(2)}) collective-permute-start(f32[424,128]{1,0:T(8,128)S(1)} %get-tuple-element.48.refs_0_), channel_id=1, source_target_pairs={{1,2},{2,1},{5,6},{6,5},{9,10},{10,9},{13,14},{14,13},{17,18},{18,... | collective-permute-start | bytes 651272 | tf_op jit(solution)/shard_map/ppermute | solution.py:605
  25.2 2.5 %collective-permute-start.4 = (f32[168,128]{1,0:T(8,128)S(1)}, f32[168,128]{1,0:T(8,128)S(1)}, u32[]{:S(2)}, u32[]{:S(2)}) collective-permute-start(f32[168,128]{1,0:T(8,128)S(1)} %get-tuple-element.45), channel_id=1, source_target_pairs={{0,16},{1,18},{2,17},{3,19},{4,20},{5,22},{6,21},{7,23},{8,24},{9,... | collective-permute-start | bytes 258056 | tf_op jit(solution)/shard_map/ppermute | solution.py:605
  27.7 0.0 collective-permute-done.6.first
  27.7 2.6 %collective-permute-done.7.second = f32[72,1024]{1,0:T(8,128)S(1)} collective-permute-done((f32[72,1024]{1,0:T(8,128)S(1)}, f32[72,1024]{1,0:T(8,128)S(1)}, u32[]{:S(2)}, u32[]{:S(2)}) %collective-permute-start.7) | collective-permute-done | bytes 294944 | tf_op jit(solution)/shard_map/ppermute | solution.py:547
  30.3 2.3 %shard_map.68 = f32[60,4,2048]{2,1,0:T(4,128)} custom-call(s32[1,2]{1,0:T(1,128)S(1)} %copy-done.1, bf16[192,256]{1,0:T(8,128)(2,1)S(1)} %get-tuple-element.41.factors, f32[4,48,1024]{2,1,0:T(8,128)S(1)} %collective-permute-done.6.first, f32[72,1024]{1,0:T(8,128)S(1)} %collective-permute-done.7.second, ...), custom_call_target="tpu_custom_call", output_to_operand_aliasing={{}: (4, {})} | custom-call | flops 20000000 | bytes 200000 | tf_op jit(solution)/shard_map/pallas_call | solution.py:353
  32.7 0.0 collective-permute-done.4.refs_1_
  32.7 0.0 collective-permute-done.5.refs_2_
  32.7 0.1 shard_map.69
  32.8 4.6 %collective-permute-start.8 = (f32[288,128]{1,0:T(8,128)S(1)}, f32[288,128]{1,0:T(8,128)S(1)}, u32[]{:S(2)}, u32[]{:S(2)}) collective-permute-start(f32[288,128]{1,0:T(8,128)S(1)} %get-tuple-element.52), channel_id=1, source_target_pairs={{0,2},{2,0},{4,6},{6,4},{8,10},{10,8},{12,14},{14,12},{16,18},{18,... | collective-permute-start | bytes 442376 | tf_op jit(solution)/shard_map/ppermute | solution.py:547
  37.4 1.0 %collective-permute-done.8.other = f32[288,128]{1,0:T(8,128)S(1)} collective-permute-done((f32[288,128]{1,0:T(8,128)S(1)}, f32[288,128]{1,0:T(8,128)S(1)}, u32[]{:S(2)}, u32[]{:S(2)}) %collective-permute-start.8) | collective-permute-done | bytes 147488 | tf_op jit(solution)/shard_map/ppermute | solution.py:547
  38.4 0.8 %shard_map.70 = (f32[4,4,2048]{2,1,0:T(4,128)}, f32[5,4,2048]{2,1,0:T(4,128)}) custom-call(f32[288,128]{1,0:T(8,128)S(1)} %get-tuple-element.51.own, f32[288,128]{1,0:T(8,128)S(1)} %collective-permute-done.8.other), custom_call_target="tpu_custom_call" | custom-call | tf_op jit(solution)/shard_map/pallas_call | solution.py:533
Async XLA Ops:
  0.6 1.9 %copy-start.1 = (s32[1,2]{1,0:T(1,128)S(1)}, s32[1,2]{1,0:T(1,128)}, u32[]{:S(2)}) copy-start(s32[1,2]{1,0:T(1,128)} %edges.9) | copy-start | bytes 28
  0.6 6.3 %copy-start = (f32[4,96,2048]{2,1,0:T(8,128)S(1)}, f32[4,96,2048]{2,1,0:T(8,128)}, u32[]{:S(2)}) copy-start(f32[4,96,2048]{2,1,0:T(8,128)} %field.5) | copy-start | bytes 9437188
  3.2 4.1 %copy-start.2 = (f32[64]{0:T(128)S(1)}, f32[64]{0:T(128)}, u32[]{:S(2)}) copy-start(f32[64]{0:T(128)} %param.5) | copy-start | bytes 772
  3.2 9.8 %collective-permute-start = (f32[4,16,2048]{2,1,0:T(8,128)S(1)}, f32[4,16,2048]{2,1,0:T(8,128)S(1)}, u32[]{:S(2)}, u32[]{:S(2)}) collective-permute-start(f32[4,16,2048]{2,1,0:T(8,128)S(1)} %shard_map.59), channel_id=1, source_target_pairs={{0,2},{2,4},{4,6},{6,8},{8,10},{10,12},{12,14},{14,16},{16,18},{18... | collective-permute-start | bytes 1572872 | tf_op jit(solution)/shard_map/ppermute | solution.py:552
  7.0 20.7 %collective-permute-start.6 = (f32[4,48,1024]{2,1,0:T(8,128)S(1)}, f32[4,48,1024]{2,1,0:T(8,128)S(1)}, u32[]{:S(2)}, u32[]{:S(2)}) collective-permute-start(f32[4,48,1024]{2,1,0:T(8,128)S(1)} %shard_map.66), channel_id=1, source_target_pairs={{0,1},{1,0},{2,3},{3,2},{4,5},{5,4},{6,7},{7,6},{8,9},{9,8},{10,11... | collective-permute-start | bytes 2359304 | tf_op jit(solution)/shard_map/ppermute | solution.py:547
  13.6 1.3 %collective-permute-start.1 = (f32[168,128]{1,0:T(8,128)S(1)}, f32[168,128]{1,0:T(8,128)S(1)}, u32[]{:S(2)}, u32[]{:S(2)}) collective-permute-start(f32[168,128]{1,0:T(8,128)S(1)} %get-tuple-element.36), channel_id=1, source_target_pairs={{0,2},{2,0},{4,6},{6,4},{8,10},{10,8},{12,14},{14,12},{16,18},{18,... | collective-permute-start | bytes 258056 | tf_op jit(solution)/shard_map/ppermute | solution.py:547
  15.0 4.9 %collective-permute-start.2 = (f32[168,128]{1,0:T(8,128)S(1)}, f32[168,128]{1,0:T(8,128)S(1)}, u32[]{:S(2)}, u32[]{:S(2)}) collective-permute-start(f32[168,128]{1,0:T(8,128)S(1)} %get-tuple-element.38), channel_id=1, source_target_pairs={{0,4},{2,6},{4,0},{6,2},{8,12},{10,14},{12,8},{14,10},{16,20},{18,... | collective-permute-start | bytes 258056 | tf_op jit(solution)/shard_map/ppermute | solution.py:547
  20.1 4.4 %collective-permute-start.3 = (f32[168,128]{1,0:T(8,128)S(1)}, f32[168,128]{1,0:T(8,128)S(1)}, u32[]{:S(2)}, u32[]{:S(2)}) collective-permute-start(f32[168,128]{1,0:T(8,128)S(1)} %get-tuple-element.43), channel_id=1, source_target_pairs={{0,8},{2,10},{4,12},{6,14},{8,0},{10,2},{12,4},{14,6},{16,24},{18,... | collective-permute-start | bytes 258056 | tf_op jit(solution)/shard_map/ppermute | solution.py:547
  22.9 7.4 %collective-permute-start.7 = (f32[72,1024]{1,0:T(8,128)S(1)}, f32[72,1024]{1,0:T(8,128)S(1)}, u32[]{:S(2)}, u32[]{:S(2)}) collective-permute-start(f32[72,1024]{1,0:T(8,128)S(1)} %shard_map.67), channel_id=1, source_target_pairs={{0,1},{1,0},{2,3},{3,2},{4,5},{5,4},{6,7},{7,6},{8,9},{9,8},{10,11... | collective-permute-start | bytes 884744 | tf_op jit(solution)/shard_map/ppermute | solution.py:547
  24.5 8.2 %collective-permute-start.5 = (f32[424,128]{1,0:T(8,128)S(1)}, f32[424,128]{1,0:T(8,128)S(1)}, u32[]{:S(2)}, u32[]{:S(2)}) collective-permute-start(f32[424,128]{1,0:T(8,128)S(1)} %get-tuple-element.48.refs_0_), channel_id=1, source_target_pairs={{1,2},{2,1},{5,6},{6,5},{9,10},{10,9},{13,14},{14,13},{17,18},{18,... | collective-permute-start | bytes 651272 | tf_op jit(solution)/shard_map/ppermute | solution.py:605
  25.2 7.5 %collective-permute-start.4 = (f32[168,128]{1,0:T(8,128)S(1)}, f32[168,128]{1,0:T(8,128)S(1)}, u32[]{:S(2)}, u32[]{:S(2)}) collective-permute-start(f32[168,128]{1,0:T(8,128)S(1)} %get-tuple-element.45), channel_id=1, source_target_pairs={{0,16},{1,18},{2,17},{3,19},{4,20},{5,22},{6,21},{7,23},{8,24},{9,... | collective-permute-start | bytes 258056 | tf_op jit(solution)/shard_map/ppermute | solution.py:605
  32.8 5.6 %collective-permute-start.8 = (f32[288,128]{1,0:T(8,128)S(1)}, f32[288,128]{1,0:T(8,128)S(1)}, u32[]{:S(2)}, u32[]{:S(2)}) collective-permute-start(f32[288,128]{1,0:T(8,128)S(1)} %get-tuple-element.52), channel_id=1, source_target_pairs={{0,2},{2,0},{4,6},{6,4},{8,10},{10,8},{12,14},{14,12},{16,18},{18,... | collective-permute-start | bytes 442376 | tf_op jit(solution)/shard_map/ppermute | solution.py:547

commit v6 on v5

--- a/solution.py
+++ b/solution.py
@@ -228,12 +228,26 @@
     )(weights, coarse_width, field)
 
 
+def terms_of(value):
+    terms = []
+    for _ in range(3):
+        terms.append(value.astype(BF16))
+        value = value - terms[-1].astype(F32)
+    return terms
+
+
 def halo_kernel(weights, halo, part, own_half, other_half, turned, fresh):
     species = halo.shape[0]
     slab = lax.axis_index("slab")
-    own = weights[:, :HALO]
+    weight_terms = terms_of(weights[:, :HALO])
+    zero = jnp.zeros_like(weights[:, :HALO])
+    own = jnp.concatenate(
+        [jnp.concatenate([weight_terms[i].astype(F32)] * (3 - i) + [zero] * i, axis=1) for i in range(3)], axis=0
+    ).astype(BF16)
     for sp in range(species):
-        result = jnp.dot(own, halo[sp], precision=HIGHEST, preferred_element_type=F32)
+        stack = jnp.concatenate(terms_of(halo[sp]), axis=0)
+        result = jnp.dot(own, stack, preferred_element_type=F32)
+        result = result[:SUB] + result[SUB : 2 * SUB] + result[2 * SUB :]
         to_dense(result, turned, fresh, sp, species)
     rows = fresh.shape[0] // 2
     for ref, half in ((own_half, slab & 1), (other_half, 1 - (slab & 1))):
@@ -306,12 +320,7 @@
             last = species * SECOND
             end = pltpu.roll(second[last : last + SUB], (SUB - sp) % SUB, 0)
             pieces = [first[sp], second[sp * SECOND : (sp + 1) * SECOND], end, end]
-        left = jnp.concatenate(pieces, axis=0)
-        terms = []
-        for _ in range(3):
-            terms.append(left.astype(BF16))
-            left = left - terms[-1].astype(F32)
-        stack = jnp.concatenate(terms, axis=0)
+        stack = jnp.concatenate(terms_of(jnp.concatenate(pieces, axis=0)), axis=0)
         result = jnp.dot(weights, stack, preferred_element_type=F32)
         result = result[:TILE] + result[TILE : 2 * TILE] + result[2 * TILE :]
         for t in range(width // LANES):
@@ -591,7 +600,9 @@
     own_half, other_half = coarse_sets(weights, halo, part)
     halo, other_half = lax.optimization_barrier((halo, other_half))
     if swapped:
-        rest_in = from_partner(rest_away(brick_edges, halo, field, width), "cross", 1)
+        rest = rest_away(brick_edges, halo, field, width)
+        halo, rest = lax.optimization_barrier((halo, rest))
+        rest_in = from_partner(rest, "cross", 1)
 
     if swapped:
         near = details(True, brick_edges, factors, halo, field, width, species, lines)

time: 39.4 us -> 38.9 us (0.987)
  the two profiles are of different devices: /device:TPU:5 before, /device:TPU:0 now
where the time goes in v6:
time: 38.9 us; the launch traced here: 38.2 us
  starting transfers between devices  19.3 us (50%)
  Pallas kernels  10.6 us (27%)
  waiting for transfers between devices  5.55 us (14%)
  local copies, waits for them, and re-layouts  1.97 us (5%)
  between operations  0.76 us (2%)
    ppermute x6, starting transfers between devices, from_partner(): return lax.ppermute(block, axis, [(i, i ^ step) for i in range(count)])  13.1 us
    ppermute x6, waiting for transfers between devices, from_partner(): return lax.ppermute(block, axis, [(i, i ^ step) for i in range(count)])  5.54 us
    pallas_call x2, Pallas kernels, details(): call(functools.partial(detail_kernel, local), jax.ShapeDtypeStruct((DETAI...  4.82 us
    ppermute x1, starting transfers between devices, on_device(): lax.ppermute(send, both, partner_route)  3.1 us
    ppermute x1, starting transfers between devices, shifted(): return lax.ppermute(block, axis, [(i, i + 1) for i in range(count - 1)])  2.39 us
    slice x1, local copies, waits for them, and re-layouts, brick_tail(): field[:, LOW:LOW + TILE]  1.88 us
    pallas_call x1, Pallas kernels, brick_part(): call(brick_kernel, jax.ShapeDtypeStruct((dense, LANES), F32), grid=(speci...  1.87 us
    pallas_call x1, Pallas kernels, tile_matrix(): call(matrix_kernel, (jax.ShapeDtypeStruct((3 * TILE, 2 * LANES), BF16), j...  0.98 us
  transfers between devices with their start and end apart: 9, of which 4 were waited for; matrix products, arithmetic and copies ran while one was open for 0% of the time, Pallas kernels for 24%

profile of v6, /device:TPU:0, one launch (start us, length us, event | category | flops | bytes accessed | tf_op | source)
XLA Modules:
  0.0 38.2 jit_solution(18200377219723905114)
XLA Ops:
  0.6 0.0 copy-start.1
  0.6 0.0 copy-start
  0.6 1.9 %slice.3.rows = f32[4,64,2048]{2,1,0:T(8,128)S(1)} slice(f32[4,96,2048]{2,1,0:T(8,128)} %field.5), slice={[0:4], [32:96], [0:2048]} | slice | bytes 4194304 | tf_op jit(solution)/shard_map/slice | solution.py:56
  2.5 0.0 copy-done.1
  2.6 0.7 %shard_map.59 = f32[4,16,2048]{2,1,0:T(8,128)S(1)} custom-call(s32[1,2]{1,0:T(1,128)S(1)} %copy-done.1, f32[4,64,2048]{2,1,0:T(8,128)S(1)} %slice.3.rows), custom_call_target="tpu_custom_call" | custom-call | tf_op jit(solution)/shard_map/pallas_call | solution.py:51
  3.2 0.0 copy-start.2
  3.2 2.4 %collective-permute-start = (f32[4,16,2048]{2,1,0:T(8,128)S(1)}, f32[4,16,2048]{2,1,0:T(8,128)S(1)}, u32[]{:S(2)}, u32[]{:S(2)}) collective-permute-start(f32[4,16,2048]{2,1,0:T(8,128)S(1)} %shard_map.59), channel_id=1, source_target_pairs={{0,2},{2,4},{4,6},{6,8},{8,10},{10,12},{12,14},{14,16},{16,18},{18... | collective-permute-start | bytes 1572872 | tf_op jit(solution)/shard_map/ppermute | solution.py:561
  5.6 0.0 copy-done
  5.6 0.1 shard_map.67
  5.7 2.4 %collective-permute-start.6 = (f32[4,48,1024]{2,1,0:T(8,128)S(1)}, f32[4,48,1024]{2,1,0:T(8,128)S(1)}, u32[]{:S(2)}, u32[]{:S(2)}) collective-permute-start(f32[4,48,1024]{2,1,0:T(8,128)S(1)} %shard_map.67), channel_id=1, source_target_pairs={{0,1},{1,0},{2,3},{3,2},{4,5},{5,4},{6,7},{7,6},{8,9},{9,8},{10,11... | collective-permute-start | bytes 2359304 | tf_op jit(solution)/shard_map/ppermute | solution.py:556
  8.1 0.0 copy-done.2
  8.1 0.1 broadcast_in_dim.2.widths
  8.2 1.0 %shard_map.58 = (bf16[192,256]{1,0:T(8,128)(2,1)S(1)}, f32[8,128]{1,0:T(8,128)S(1)}, f32[8,128]{1,0:T(8,128)S(1)}) custom-call(s32[1,2]{1,0:T(1,128)S(1)} %copy-done.1, f32[64,128]{1,0:T(8,128)S(1)} %broadcast_in_dim.2.widths), custom_call_target="tpu_custom_call" | custom-call | tf_op jit(solution)/shard_map/pallas_call | solution.py:166
  9.2 1.9 %shard_map.60.part = f32[328,128]{1,0:T(8,128)S(1)} custom-call(f32[8,128]{1,0:T(8,128)S(1)} %get-tuple-element.31.weights, f32[8,128]{1,0:T(8,128)S(1)} %get-tuple-element.32.coarse_width, f32[4,96,2048]{2,1,0:T(8,128)S(1)} %copy-done), custom_call_target="tpu_custom_call" | custom-call | tf_op jit(solution)/shard_map/pallas_call | solution.py:217
  11.1 0.0 collective-permute-done.halo.first
  11.1 0.4 %shard_map.61 = (f32[168,128]{1,0:T(8,128)S(1)}, f32[168,128]{1,0:T(8,128)S(1)}) custom-call(f32[8,128]{1,0:T(8,128)S(1)} %get-tuple-element.31.weights, f32[4,16,2048]{2,1,0:T(8,128)S(1)} %collective-permute-done.halo.first, f32[328,128]{1,0:T(8,128)S(1)} %shard_map.60.part), custom_call_target="tpu_custom_call" | custom-call | tf_op jit(solution)/shard_map/pallas_call | solution.py:263
  11.5 3.3 %collective-permute-start.1 = (f32[168,128]{1,0:T(8,128)S(1)}, f32[168,128]{1,0:T(8,128)S(1)}, u32[]{:S(2)}, u32[]{:S(2)}) collective-permute-start(f32[168,128]{1,0:T(8,128)S(1)} %get-tuple-element.38), channel_id=1, source_target_pairs={{0,2},{2,0},{4,6},{6,4},{8,10},{10,8},{12,14},{14,12},{16,18},{18,... | collective-permute-start | bytes 258056 | tf_op jit(solution)/shard_map/ppermute | solution.py:556
  14.8 0.9 %collective-permute-done.1.refs_1_ = f32[168,128]{1,0:T(8,128)S(1)} collective-permute-done((f32[168,128]{1,0:T(8,128)S(1)}, f32[168,128]{1,0:T(8,128)S(1)}, u32[]{:S(2)}, u32[]{:S(2)}) %collective-permute-start.1) | collective-permute-done | bytes 86048 | tf_op jit(solution)/shard_map/ppermute | solution.py:556
  15.7 0.1 shard_map.62
  15.8 2.8 %collective-permute-start.2 = (f32[168,128]{1,0:T(8,128)S(1)}, f32[168,128]{1,0:T(8,128)S(1)}, u32[]{:S(2)}, u32[]{:S(2)}) collective-permute-start(f32[168,128]{1,0:T(8,128)S(1)} %get-tuple-element.40), channel_id=1, source_target_pairs={{0,4},{2,6},{4,0},{6,2},{8,12},{10,14},{12,8},{14,10},{16,20},{18,... | collective-permute-start | bytes 258056 | tf_op jit(solution)/shard_map/ppermute | solution.py:556
  18.6 0.7 %shard_map.64 = f32[72,1024]{1,0:T(8,128)S(1)} custom-call(s32[1,2]{1,0:T(1,128)S(1)} %copy-done.1, f32[4,16,2048]{2,1,0:T(8,128)S(1)} %collective-permute-done.halo.first, f32[4,96,2048]{2,1,0:T(8,128)S(1)} %copy-done), custom_call_target="tpu_custom_call" | custom-call | flops 20000000 | bytes 200000 | tf_op jit(solution)/shard_map/pallas_call | solution.py:300
  19.2 2.5 %shard_map.65.rest_0_ = f32[60,4,2048]{2,1,0:T(4,128)} custom-call(s32[1,2]{1,0:T(1,128)S(1)} %copy-done.1, bf16[192,256]{1,0:T(8,128)(2,1)S(1)} %get-tuple-element.43.factors, f32[4,16,2048]{2,1,0:T(8,128)S(1)} %collective-permute-done.halo.first, f32[4,96,2048]{2,1,0:T(8,128)S(1)} %copy-done), custom_call_target="tpu_custom_call" | custom-call | flops 20000000 | bytes 200000 | tf_op jit(solution)/shard_map/pallas_call | solution.py:362
  21.7 0.0 collective-permute-done.2.refs_1_
  21.7 0.1 shard_map.63
  21.8 2.5 %collective-permute-start.3 = (f32[168,128]{1,0:T(8,128)S(1)}, f32[168,128]{1,0:T(8,128)S(1)}, u32[]{:S(2)}, u32[]{:S(2)}) collective-permute-start(f32[168,128]{1,0:T(8,128)S(1)} %get-tuple-element.46), channel_id=1, source_target_pairs={{0,8},{2,10},{4,12},{6,14},{8,0},{10,2},{12,4},{14,6},{16,24},{18,... | collective-permute-start | bytes 258056 | tf_op jit(solution)/shard_map/ppermute | solution.py:556
  24.3 1.5 %collective-permute-start.7 = (f32[72,1024]{1,0:T(8,128)S(1)}, f32[72,1024]{1,0:T(8,128)S(1)}, u32[]{:S(2)}, u32[]{:S(2)}) collective-permute-start(f32[72,1024]{1,0:T(8,128)S(1)} %shard_map.64), channel_id=1, source_target_pairs={{0,1},{1,0},{2,3},{3,2},{4,5},{5,4},{6,7},{7,6},{8,9},{9,8},{10,11... | collective-permute-start | bytes 884744 | tf_op jit(solution)/shard_map/ppermute | solution.py:556
  25.8 0.9 %collective-permute-done.3.refs_1_ = f32[168,128]{1,0:T(8,128)S(1)} collective-permute-done((f32[168,128]{1,0:T(8,128)S(1)}, f32[168,128]{1,0:T(8,128)S(1)}, u32[]{:S(2)}, u32[]{:S(2)}) %collective-permute-start.3) | collective-permute-done | bytes 86048 | tf_op jit(solution)/shard_map/ppermute | solution.py:556
  26.7 0.1 shard_map.66
  26.8 0.7 %collective-permute-start.5 = (f32[424,128]{1,0:T(8,128)S(1)}, f32[424,128]{1,0:T(8,128)S(1)}, u32[]{:S(2)}, u32[]{:S(2)}) collective-permute-start(f32[424,128]{1,0:T(8,128)S(1)} %get-tuple-element.52.refs_0_), channel_id=1, source_target_pairs={{1,2},{2,1},{5,6},{6,5},{9,10},{10,9},{13,14},{14,13},{17,18},{18,... | collective-permute-start | bytes 651272 | tf_op jit(solution)/shard_map/ppermute | solution.py:616
  27.5 3.1 %collective-permute-start.4 = (f32[168,128]{1,0:T(8,128)S(1)}, f32[168,128]{1,0:T(8,128)S(1)}, u32[]{:S(2)}, u32[]{:S(2)}) collective-permute-start(f32[168,128]{1,0:T(8,128)S(1)} %get-tuple-element.48), channel_id=1, source_target_pairs={{0,16},{1,18},{2,17},{3,19},{4,20},{5,22},{6,21},{7,23},{8,24},{9,... | collective-permute-start | bytes 258056 | tf_op jit(solution)/shard_map/ppermute | solution.py:616
  30.6 0.0 collective-permute-done.6.first
  30.6 2.7 %collective-permute-done.7.second = f32[72,1024]{1,0:T(8,128)S(1)} collective-permute-done((f32[72,1024]{1,0:T(8,128)S(1)}, f32[72,1024]{1,0:T(8,128)S(1)}, u32[]{:S(2)}, u32[]{:S(2)}) %collective-permute-start.7) | collective-permute-done | bytes 294944 | tf_op jit(solution)/shard_map/ppermute | solution.py:556
  33.3 2.3 %shard_map.68 = f32[60,4,2048]{2,1,0:T(4,128)} custom-call(s32[1,2]{1,0:T(1,128)S(1)} %copy-done.1, bf16[192,256]{1,0:T(8,128)(2,1)S(1)} %get-tuple-element.43.factors, f32[4,48,1024]{2,1,0:T(8,128)S(1)} %collective-permute-done.6.first, f32[72,1024]{1,0:T(8,128)S(1)} %collective-permute-done.7.second, ...), custom_call_target="tpu_custom_call", output_to_operand_aliasing={{}: (4, {})} | custom-call | flops 20000000 | bytes 200000 | tf_op jit(solution)/shard_map/pallas_call | solution.py:362
  35.6 0.0 collective-permute-done.4.refs_1_
  35.6 0.0 collective-permute-done.5.refs_2_
  35.6 0.1 shard_map.69
  35.7 0.6 %collective-permute-start.8 = (f32[288,128]{1,0:T(8,128)S(1)}, f32[288,128]{1,0:T(8,128)S(1)}, u32[]{:S(2)}, u32[]{:S(2)}) collective-permute-start(f32[288,128]{1,0:T(8,128)S(1)} %get-tuple-element.56), channel_id=1, source_target_pairs={{0,2},{2,0},{4,6},{6,4},{8,10},{10,8},{12,14},{14,12},{16,18},{18,... | collective-permute-start | bytes 442376 | tf_op jit(solution)/shard_map/ppermute | solution.py:556
  36.3 1.0 %collective-permute-done.8.other = f32[288,128]{1,0:T(8,128)S(1)} collective-permute-done((f32[288,128]{1,0:T(8,128)S(1)}, f32[288,128]{1,0:T(8,128)S(1)}, u32[]{:S(2)}, u32[]{:S(2)}) %collective-permute-start.8) | collective-permute-done | bytes 147488 | tf_op jit(solution)/shard_map/ppermute | solution.py:556
  37.3 0.8 %shard_map.70 = (f32[4,4,2048]{2,1,0:T(4,128)}, f32[5,4,2048]{2,1,0:T(4,128)}) custom-call(f32[288,128]{1,0:T(8,128)S(1)} %get-tuple-element.55.own, f32[288,128]{1,0:T(8,128)S(1)} %collective-permute-done.8.other), custom_call_target="tpu_custom_call" | custom-call | tf_op jit(solution)/shard_map/pallas_call | solution.py:542
Async XLA Ops:
  0.6 1.9 %copy-start.1 = (s32[1,2]{1,0:T(1,128)S(1)}, s32[1,2]{1,0:T(1,128)}, u32[]{:S(2)}) copy-start(s32[1,2]{1,0:T(1,128)} %edges.9) | copy-start | bytes 28
  0.6 5.0 %copy-start = (f32[4,96,2048]{2,1,0:T(8,128)S(1)}, f32[4,96,2048]{2,1,0:T(8,128)}, u32[]{:S(2)}) copy-start(f32[4,96,2048]{2,1,0:T(8,128)} %field.5) | copy-start | bytes 9437188
  3.2 4.9 %copy-start.2 = (f32[64]{0:T(128)S(1)}, f32[64]{0:T(128)}, u32[]{:S(2)}) copy-start(f32[64]{0:T(128)} %param.5) | copy-start | bytes 772
  3.2 7.8 %collective-permute-start = (f32[4,16,2048]{2,1,0:T(8,128)S(1)}, f32[4,16,2048]{2,1,0:T(8,128)S(1)}, u32[]{:S(2)}, u32[]{:S(2)}) collective-permute-start(f32[4,16,2048]{2,1,0:T(8,128)S(1)} %shard_map.59), channel_id=1, source_target_pairs={{0,2},{2,4},{4,6},{6,8},{8,10},{10,12},{12,14},{14,16},{16,18},{18... | collective-permute-start | bytes 1572872 | tf_op jit(solution)/shard_map/ppermute | solution.py:561
  5.7 24.9 %collective-permute-start.6 = (f32[4,48,1024]{2,1,0:T(8,128)S(1)}, f32[4,48,1024]{2,1,0:T(8,128)S(1)}, u32[]{:S(2)}, u32[]{:S(2)}) collective-permute-start(f32[4,48,1024]{2,1,0:T(8,128)S(1)} %shard_map.67), channel_id=1, source_target_pairs={{0,1},{1,0},{2,3},{3,2},{4,5},{5,4},{6,7},{7,6},{8,9},{9,8},{10,11... | collective-permute-start | bytes 2359304 | tf_op jit(solution)/shard_map/ppermute | solution.py:556
  11.5 4.2 %collective-permute-start.1 = (f32[168,128]{1,0:T(8,128)S(1)}, f32[168,128]{1,0:T(8,128)S(1)}, u32[]{:S(2)}, u32[]{:S(2)}) collective-permute-start(f32[168,128]{1,0:T(8,128)S(1)} %get-tuple-element.38), channel_id=1, source_target_pairs={{0,2},{2,0},{4,6},{6,4},{8,10},{10,8},{12,14},{14,12},{16,18},{18,... | collective-permute-start | bytes 258056 | tf_op jit(solution)/shard_map/ppermute | solution.py:556
  15.8 6.0 %collective-permute-start.2 = (f32[168,128]{1,0:T(8,128)S(1)}, f32[168,128]{1,0:T(8,128)S(1)}, u32[]{:S(2)}, u32[]{:S(2)}) collective-permute-start(f32[168,128]{1,0:T(8,128)S(1)} %get-tuple-element.40), channel_id=1, source_target_pairs={{0,4},{2,6},{4,0},{6,2},{8,12},{10,14},{12,8},{14,10},{16,20},{18,... | collective-permute-start | bytes 258056 | tf_op jit(solution)/shard_map/ppermute | solution.py:556
  21.8 4.9 %collective-permute-start.3 = (f32[168,128]{1,0:T(8,128)S(1)}, f32[168,128]{1,0:T(8,128)S(1)}, u32[]{:S(2)}, u32[]{:S(2)}) collective-permute-start(f32[168,128]{1,0:T(8,128)S(1)} %get-tuple-element.46), channel_id=1, source_target_pairs={{0,8},{2,10},{4,12},{6,14},{8,0},{10,2},{12,4},{14,6},{16,24},{18,... | collective-permute-start | bytes 258056 | tf_op jit(solution)/shard_map/ppermute | solution.py:556
  24.3 9.0 %collective-permute-start.7 = (f32[72,1024]{1,0:T(8,128)S(1)}, f32[72,1024]{1,0:T(8,128)S(1)}, u32[]{:S(2)}, u32[]{:S(2)}) collective-permute-start(f32[72,1024]{1,0:T(8,128)S(1)} %shard_map.64), channel_id=1, source_target_pairs={{0,1},{1,0},{2,3},{3,2},{4,5},{5,4},{6,7},{7,6},{8,9},{9,8},{10,11... | collective-permute-start | bytes 884744 | tf_op jit(solution)/shard_map/ppermute | solution.py:556
  26.8 8.8 %collective-permute-start.5 = (f32[424,128]{1,0:T(8,128)S(1)}, f32[424,128]{1,0:T(8,128)S(1)}, u32[]{:S(2)}, u32[]{:S(2)}) collective-permute-start(f32[424,128]{1,0:T(8,128)S(1)} %get-tuple-element.52.refs_0_), channel_id=1, source_target_pairs={{1,2},{2,1},{5,6},{6,5},{9,10},{10,9},{13,14},{14,13},{17,18},{18,... | collective-permute-start | bytes 651272 | tf_op jit(solution)/shard_map/ppermute | solution.py:616
  27.5 8.1 %collective-permute-start.4 = (f32[168,128]{1,0:T(8,128)S(1)}, f32[168,128]{1,0:T(8,128)S(1)}, u32[]{:S(2)}, u32[]{:S(2)}) collective-permute-start(f32[168,128]{1,0:T(8,128)S(1)} %get-tuple-element.48), channel_id=1, source_target_pairs={{0,16},{1,18},{2,17},{3,19},{4,20},{5,22},{6,21},{7,23},{8,24},{9,... | collective-permute-start | bytes 258056 | tf_op jit(solution)/shard_map/ppermute | solution.py:616
  35.7 1.6 %collective-permute-start.8 = (f32[288,128]{1,0:T(8,128)S(1)}, f32[288,128]{1,0:T(8,128)S(1)}, u32[]{:S(2)}, u32[]{:S(2)}) collective-permute-start(f32[288,128]{1,0:T(8,128)S(1)} %get-tuple-element.56), channel_id=1, source_target_pairs={{0,2},{2,0},{4,6},{6,4},{8,10},{10,8},{12,14},{14,12},{16,18},{18,... | collective-permute-start | bytes 442376 | tf_op jit(solution)/shard_map/ppermute | solution.py:556

commit v7 on v6

--- a/solution.py
+++ b/solution.py
@@ -284,42 +284,56 @@
 def rest_kernel(edges, halo, field, out):
     species = halo.shape[0]
     shift = edges[0, 0] - lax.axis_index("slab") * TILE
-    width = out.shape[1]
+    each = species * (SECOND + 1)
+    width = out.shape[0] // each * LANES
     other = pl.ds(pl.multiple_of((1 - lax.axis_index("cross")) * width, LANES), width)
-    last = species * SECOND
-    out[last:] = jnp.zeros((out.shape[0] - last, width), F32)
     for sp in range(species):
         rows = later_nodes(shift, halo[sp, :, other], field[sp, FIRST:BRICK_END, other])
-        out[sp * SECOND : (sp + 1) * SECOND] = rows[:SECOND]
-        out[last + sp : last + sp + 1] = rows[SECOND : SECOND + 1]
+        for t in range(width // LANES):
+            tile = rows[:, t * LANES : (t + 1) * LANES]
+            out[t * each + sp * SECOND : t * each + (sp + 1) * SECOND] = tile[:SECOND]
+            last = t * each + species * SECOND + sp
+            out[last : last + 1] = tile[SECOND : SECOND + 1]
 
 
 def rest_away(edges, halo, field, width):
     species = halo.shape[0]
-    rows = species * SECOND + -(-species // SUB) * SUB
+    rows = species * (SECOND + 1) * width // LANES
     return call(
         rest_kernel,
-        jax.ShapeDtypeStruct((rows, width), F32),
+        jax.ShapeDtypeStruct((rows, LANES), F32),
         in_specs=[SMEM_SPEC, VMEM_SPEC, VMEM_SPEC],
         out_specs=VMEM_SPEC,
         cost=20_000_000,
     )(edges, halo, field)
 
 
-def detail_kernel(local, edges, factors, first, second, *rest):
+def detail_kernel(local, whole, edges, factors, first, second, *rest):
     out, wide = rest[-2:]
     species = out.shape[1]
     width = out.shape[2]
     weights = factors[:, : 3 * HELD]
+    step = pl.program_id(0)
+    if local and not whole:
+        step += lax.axis_index("cross") * pl.num_programs(0)
+    lanes = pl.ds(pl.multiple_of(step * width, LANES), width)
     shift = edges[0, 0] - lax.axis_index("slab") * TILE
     for sp in range(species):
         if local:
-            more = later_nodes(shift, first[sp], second[sp, FIRST:BRICK_END])
-            pieces = [second[sp, :FIRST], more[: SECOND + HALO]]
+            more = later_nodes(shift, first[sp, :, lanes], second[sp, FIRST:BRICK_END, lanes])
+            pieces = [second[sp, :FIRST, lanes], more[: SECOND + HALO]]
         else:
-            last = species * SECOND
-            end = pltpu.roll(second[last : last + SUB], (SUB - sp) % SUB, 0)
-            pieces = [first[sp], second[sp * SECOND : (sp + 1) * SECOND], end, end]
+            each = species * (SECOND + 1)
+            base = step * (width // LANES * each)
+
+            def rows_of(at, count):
+                return jnp.concatenate(
+                    [second[pl.ds(base + t * each + at, count)] for t in range(width // LANES)], axis=1
+                )
+
+            end = rows_of(species * SECOND + sp, 1)
+            end = jnp.concatenate([end, jnp.zeros((HALO - 1, width), F32)], axis=0)
+            pieces = [first[sp, :, lanes], rows_of(sp * SECOND, SECOND), end]
         stack = jnp.concatenate(terms_of(jnp.concatenate(pieces, axis=0)), axis=0)
         result = jnp.dot(weights, stack, preferred_element_type=F32)
         result = result[:TILE] + result[TILE : 2 * TILE] + result[2 * TILE :]
@@ -330,29 +344,17 @@
             out[k, :, t * LANES : (t + 1) * LANES] = wide[t, k * species : (k + 1) * species]
 
 
-def details(local, edges, factors, first, second, width, species, lines, onto=None, part=None):
+def details(local, edges, factors, first, second, width, species, lines, onto=None):
     chunk = min(width, 512)
     steps = width // chunk
-    begin, count = (0, steps) if part is None else (part, 1)
 
     def here(i):
-        i = i + begin
         return i if width == lines else lax.axis_index("cross") * steps + i
 
     def there(i):
-        return (1 - lax.axis_index("cross")) * steps + i + begin
-
-    if local:
-        specs = [
-            pl.BlockSpec((species, HALO, chunk), lambda i: (0, 0, here(i))),
-            pl.BlockSpec((species, HELD, chunk), lambda i: (0, 0, here(i))),
-        ]
-    else:
-        specs = [
-            pl.BlockSpec((species, FIRST, chunk), lambda i: (0, 0, i + begin)),
-            pl.BlockSpec((second.shape[0], chunk), lambda i: (0, i + begin)),
-        ]
-    specs = [SMEM_SPEC, pl.BlockSpec((3 * TILE, 2 * LANES), lambda i: (0, 0))] + specs
+        return (1 - lax.axis_index("cross")) * steps + i
+
+    specs = [SMEM_SPEC] + [VMEM_SPEC] * 3
     operands = [edges, factors, first, second]
     alias = {}
     if onto is not None:
@@ -360,9 +362,9 @@
         operands.append(onto)
         alias = {4: 0}
     return call(
-        functools.partial(detail_kernel, local),
+        functools.partial(detail_kernel, local, width == lines),
         jax.ShapeDtypeStruct((DETAILS, species, lines), F32),
-        grid=(count,),
+        grid=(steps,),
         in_specs=specs,
         out_specs=pl.BlockSpec((DETAILS, species, chunk), lambda i: (0, 0, here(i) if local else there(i))),
         scratch_shapes=[pltpu.VMEM((chunk // LANES, TILE * species, LANES), F32)],
@@ -514,41 +516,57 @@
     )(*operands)
 
 
-def finish_kernel(own, other, tree, final, turned):
+def in_outputs_order(part, tree, final, turned):
+    species, group, width = tree.shape
+    per = width // LANES
+    for k in range(COARSE):
+        for sp in range(species):
+            turned[pl.ds(sp, per, stride=species)] = part[(k * species + sp) * per : (k * species + sp + 1) * per]
+        for t in range(per):
+            final[k, :, t * LANES : (t + 1) * LANES] = turned[t * species : (t + 1) * species]
+    for sp in range(species):
+        for i in range(group):
+            at = ((COARSE + i) * species + sp) * per
+            turned[pl.ds(i, per, stride=group)] = part[at : at + per]
+        for t in range(per):
+            tree[sp, :, t * LANES : (t + 1) * LANES] = turned[t * group : (t + 1) * group]
+
+
+def finish_kernel(own_tree, own_final, other, tree, final, other_tree, other_final, turned, sems):
     core = lax.axis_index("slab") & 1
-    species, _, lines = tree.shape
-    width = lines // 2
-    per = width // LANES
-    group = COARSE - 1
-    for block, ref in ((core, own), (1 - core, other)):
-
-        def lanes(t):
-            return pl.ds(pl.multiple_of(block * width + t * LANES, LANES), LANES)
-
-        for k in range(COARSE):
-            for sp in range(species):
-                turned[pl.ds(sp, per, stride=species)] = ref[(k * species + sp) * per : (k * species + sp + 1) * per]
-            for t in range(per):
-                final[k, :, lanes(t)] = turned[t * species : (t + 1) * species]
-        for sp in range(species):
-            for i in range(group):
-                at = ((COARSE + i) * species + sp) * per
-                turned[pl.ds(i, per, stride=group)] = ref[at : at + per]
-            for t in range(per):
-                tree[sp, :, lanes(t)] = turned[t * group : (t + 1) * group]
+    width = own_tree.shape[2]
+
+    def to(ref, source, block, sem):
+        lanes = pl.ds(pl.multiple_of(block * width, LANES), width)
+        copy = pltpu.make_async_copy(source, ref.at[:, :, lanes], sem)
+        copy.start()
+        return copy
+
+    copies = [to(tree, own_tree, core, sems.at[0]), to(final, own_final, core, sems.at[1])]
+    in_outputs_order(other, other_tree, other_final, turned)
+    copies += [to(tree, other_tree, 1 - core, sems.at[2]), to(final, other_final, 1 - core, sems.at[3])]
+    for copy in copies:
+        copy.wait()
 
 
 def finish(own, other, species, lines):
+    half = lines // 2
+    shapes = ((species, COARSE - 1, half), (COARSE, species, half))
+    turned = pltpu.VMEM((half // LANES * SUB, LANES), F32)
+    placed = call(
+        in_outputs_order,
+        tuple(jax.ShapeDtypeStruct(shape, F32) for shape in shapes),
+        in_specs=[VMEM_SPEC],
+        out_specs=(VMEM_SPEC,) * 2,
+        scratch_shapes=[turned],
+    )(own)
     return call(
         finish_kernel,
-        (
-            jax.ShapeDtypeStruct((species, COARSE - 1, lines), F32),
-            jax.ShapeDtypeStruct((COARSE, species, lines), F32),
-        ),
-        in_specs=[VMEM_SPEC] * 2,
-        out_specs=(VMEM_SPEC,) * 2,
-        scratch_shapes=[pltpu.VMEM((lines // 2 // LANES * SUB, LANES), F32)],
-    )(own, other)
+        tuple(jax.ShapeDtypeStruct(shape[:2] + (lines,), F32) for shape in shapes),
+        in_specs=[VMEM_SPEC] * 3,
+        out_specs=(HBM_SPEC,) * 2,
+        scratch_shapes=[pltpu.VMEM(shape, F32) for shape in shapes] + [turned, pltpu.SemaphoreType.DMA((4,))],
+    )(*placed, other)
 
 
 def from_partner(block, axis, step):

time: 38.9 us -> 38.6 us (level)
  starting transfers between devices: 19.3 us -> 19.8 us
  waiting for transfers between devices: 5.55 us -> 5.12 us
    ppermute x6, starting transfers between devices: 13.1 us -> 13.6 us  [from_partner(): return lax.ppermute(block, axis, [(i, i ^ step) for i in range(count)])]
    ppermute x6, waiting for transfers between devices: 5.54 us -> 5.11 us  [from_partner(): return lax.ppermute(block, axis, [(i, i ^ step) for i in range(count)])]
    pallas_call x4 -> x5, Pallas kernels: 6.33 us -> 6.19 us  [the longest x2 4.68 us: details(): call(functools.partial(detail_kernel, local, width == lines), jax.ShapeDt...]
where the time goes in v7:
time: 38.6 us; the launch traced here: 38.1 us
  starting transfers between devices  19.8 us (51%)
  Pallas kernels  10.5 us (27%)
  waiting for transfers between devices  5.12 us (13%)
  local copies, waits for them, and re-layouts  1.97 us (5%)
  between operations  0.76 us (2%)
    ppermute x6, starting transfers between devices, from_partner(): return lax.ppermute(block, axis, [(i, i ^ step) for i in range(count)])  13.6 us
    ppermute x6, waiting for transfers between devices, from_partner(): return lax.ppermute(block, axis, [(i, i ^ step) for i in range(count)])  5.11 us
    pallas_call x2, Pallas kernels, details(): call(functools.partial(detail_kernel, local, width == lines), jax.ShapeDt...  4.68 us
    ppermute x1, starting transfers between devices, on_device(): lax.ppermute(send, both, partner_route)  3.1 us
    ppermute x1, starting transfers between devices, shifted(): return lax.ppermute(block, axis, [(i, i + 1) for i in range(count - 1)])  2.39 us
    slice x1, local copies, waits for them, and re-layouts, brick_tail(): field[:, LOW:LOW + TILE]  1.88 us
    pallas_call x1, Pallas kernels, brick_part(): call(brick_kernel, jax.ShapeDtypeStruct((dense, LANES), F32), grid=(speci...  1.87 us
    pallas_call x1, Pallas kernels, tile_matrix(): call(matrix_kernel, (jax.ShapeDtypeStruct((3 * TILE, 2 * LANES), BF16), j...  0.98 us
  transfers between devices with their start and end apart: 9, of which 4 were waited for; matrix products, arithmetic and copies ran while one was open for 0% of the time, Pallas kernels for 24%

profile of v7, /device:TPU:0, one launch (start us, length us, event | category | flops | bytes accessed | tf_op | source)
XLA Modules:
  0.0 38.1 jit_solution(8492202278215707189)
XLA Ops:
  0.6 0.0 copy-start.1
  0.6 0.0 copy-start
  0.6 1.9 %slice.3.rows = f32[4,64,2048]{2,1,0:T(8,128)S(1)} slice(f32[4,96,2048]{2,1,0:T(8,128)} %field.5), slice={[0:4], [32:96], [0:2048]} | slice | bytes 4194304 | tf_op jit(solution)/shard_map/slice | solution.py:56
  2.5 0.0 copy-done.1
  2.6 0.7 %shard_map.59 = f32[4,16,2048]{2,1,0:T(8,128)S(1)} custom-call(s32[1,2]{1,0:T(1,128)S(1)} %copy-done.1, f32[4,64,2048]{2,1,0:T(8,128)S(1)} %slice.3.rows), custom_call_target="tpu_custom_call" | custom-call | tf_op jit(solution)/shard_map/pallas_call | solution.py:51
  3.2 0.0 copy-start.2
  3.2 2.4 %collective-permute-start = (f32[4,16,2048]{2,1,0:T(8,128)S(1)}, f32[4,16,2048]{2,1,0:T(8,128)S(1)}, u32[]{:S(2)}, u32[]{:S(2)}) collective-permute-start(f32[4,16,2048]{2,1,0:T(8,128)S(1)} %shard_map.59), channel_id=1, source_target_pairs={{0,2},{2,4},{4,6},{6,8},{8,10},{10,12},{12,14},{14,16},{16,18},{18... | collective-permute-start | bytes 1572872 | tf_op jit(solution)/shard_map/ppermute | solution.py:579
  5.6 0.0 copy-done
  5.6 0.1 shard_map.67
  5.7 2.4 %collective-permute-start.6 = (f32[4,48,1024]{2,1,0:T(8,128)S(1)}, f32[4,48,1024]{2,1,0:T(8,128)S(1)}, u32[]{:S(2)}, u32[]{:S(2)}) collective-permute-start(f32[4,48,1024]{2,1,0:T(8,128)S(1)} %shard_map.67), channel_id=1, source_target_pairs={{0,1},{1,0},{2,3},{3,2},{4,5},{5,4},{6,7},{7,6},{8,9},{9,8},{10,11... | collective-permute-start | bytes 2359304 | tf_op jit(solution)/shard_map/ppermute | solution.py:574
  8.1 0.0 copy-done.2
  8.1 0.1 broadcast_in_dim.2.widths
  8.2 1.0 %shard_map.58 = (bf16[192,256]{1,0:T(8,128)(2,1)S(1)}, f32[8,128]{1,0:T(8,128)S(1)}, f32[8,128]{1,0:T(8,128)S(1)}) custom-call(s32[1,2]{1,0:T(1,128)S(1)} %copy-done.1, f32[64,128]{1,0:T(8,128)S(1)} %broadcast_in_dim.2.widths), custom_call_target="tpu_custom_call" | custom-call | tf_op jit(solution)/shard_map/pallas_call | solution.py:166
  9.2 1.9 %shard_map.60.part = f32[328,128]{1,0:T(8,128)S(1)} custom-call(f32[8,128]{1,0:T(8,128)S(1)} %get-tuple-element.33.weights, f32[8,128]{1,0:T(8,128)S(1)} %get-tuple-element.34.coarse_width, f32[4,96,2048]{2,1,0:T(8,128)S(1)} %copy-done), custom_call_target="tpu_custom_call" | custom-call | tf_op jit(solution)/shard_map/pallas_call | solution.py:217
  11.1 0.0 collective-permute-done.halo.first
  11.1 0.4 %shard_map.61 = (f32[168,128]{1,0:T(8,128)S(1)}, f32[168,128]{1,0:T(8,128)S(1)}) custom-call(f32[8,128]{1,0:T(8,128)S(1)} %get-tuple-element.33.weights, f32[4,16,2048]{2,1,0:T(8,128)S(1)} %collective-permute-done.halo.first, f32[328,128]{1,0:T(8,128)S(1)} %shard_map.60.part), custom_call_target="tpu_custom_call" | custom-call | tf_op jit(solution)/shard_map/pallas_call | solution.py:263
  11.5 3.3 %collective-permute-start.1 = (f32[168,128]{1,0:T(8,128)S(1)}, f32[168,128]{1,0:T(8,128)S(1)}, u32[]{:S(2)}, u32[]{:S(2)}) collective-permute-start(f32[168,128]{1,0:T(8,128)S(1)} %get-tuple-element.40), channel_id=1, source_target_pairs={{0,2},{2,0},{4,6},{6,4},{8,10},{10,8},{12,14},{14,12},{16,18},{18,... | collective-permute-start | bytes 258056 | tf_op jit(solution)/shard_map/ppermute | solution.py:574
  14.8 0.9 %collective-permute-done.1.refs_1_ = f32[168,128]{1,0:T(8,128)S(1)} collective-permute-done((f32[168,128]{1,0:T(8,128)S(1)}, f32[168,128]{1,0:T(8,128)S(1)}, u32[]{:S(2)}, u32[]{:S(2)}) %collective-permute-start.1) | collective-permute-done | bytes 86048 | tf_op jit(solution)/shard_map/ppermute | solution.py:574
  15.7 0.1 shard_map.62
  15.8 2.8 %collective-permute-start.2 = (f32[168,128]{1,0:T(8,128)S(1)}, f32[168,128]{1,0:T(8,128)S(1)}, u32[]{:S(2)}, u32[]{:S(2)}) collective-permute-start(f32[168,128]{1,0:T(8,128)S(1)} %get-tuple-element.42), channel_id=1, source_target_pairs={{0,4},{2,6},{4,0},{6,2},{8,12},{10,14},{12,8},{14,10},{16,20},{18,... | collective-permute-start | bytes 258056 | tf_op jit(solution)/shard_map/ppermute | solution.py:574
  18.6 0.7 %shard_map.64 = f32[544,128]{1,0:T(8,128)S(1)} custom-call(s32[1,2]{1,0:T(1,128)S(1)} %copy-done.1, f32[4,16,2048]{2,1,0:T(8,128)S(1)} %collective-permute-done.halo.first, f32[4,96,2048]{2,1,0:T(8,128)S(1)} %copy-done), custom_call_target="tpu_custom_call" | custom-call | flops 20000000 | bytes 200000 | tf_op jit(solution)/shard_map/pallas_call | solution.py:302
  19.2 2.4 %shard_map.65.rest_0_ = f32[60,4,2048]{2,1,0:T(4,128)} custom-call(s32[1,2]{1,0:T(1,128)S(1)} %copy-done.1, bf16[192,256]{1,0:T(8,128)(2,1)S(1)} %get-tuple-element.45.factors, f32[4,16,2048]{2,1,0:T(8,128)S(1)} %collective-permute-done.halo.first, f32[4,96,2048]{2,1,0:T(8,128)S(1)} %copy-done), custom_call_target="tpu_custom_call" | custom-call | flops 20000000 | bytes 200000 | tf_op jit(solution)/shard_map/pallas_call | solution.py:364
  21.6 0.0 collective-permute-done.2.refs_1_
  21.6 0.1 shard_map.63
  21.7 2.6 %collective-permute-start.3 = (f32[168,128]{1,0:T(8,128)S(1)}, f32[168,128]{1,0:T(8,128)S(1)}, u32[]{:S(2)}, u32[]{:S(2)}) collective-permute-start(f32[168,128]{1,0:T(8,128)S(1)} %get-tuple-element.48), channel_id=1, source_target_pairs={{0,8},{2,10},{4,12},{6,14},{8,0},{10,2},{12,4},{14,6},{16,24},{18,... | collective-permute-start | bytes 258056 | tf_op jit(solution)/shard_map/ppermute | solution.py:574
  24.3 1.5 %collective-permute-start.7 = (f32[544,128]{1,0:T(8,128)S(1)}, f32[544,128]{1,0:T(8,128)S(1)}, u32[]{:S(2)}, u32[]{:S(2)}) collective-permute-start(f32[544,128]{1,0:T(8,128)S(1)} %shard_map.64), channel_id=1, source_target_pairs={{0,1},{1,0},{2,3},{3,2},{4,5},{5,4},{6,7},{7,6},{8,9},{9,8},{10,11... | collective-permute-start | bytes 835592 | tf_op jit(solution)/shard_map/ppermute | solution.py:574
  25.8 0.9 %collective-permute-done.3.refs_1_ = f32[168,128]{1,0:T(8,128)S(1)} collective-permute-done((f32[168,128]{1,0:T(8,128)S(1)}, f32[168,128]{1,0:T(8,128)S(1)}, u32[]{:S(2)}, u32[]{:S(2)}) %collective-permute-start.3) | collective-permute-done | bytes 86048 | tf_op jit(solution)/shard_map/ppermute | solution.py:574
  26.7 0.1 shard_map.66
  26.8 0.7 %collective-permute-start.5 = (f32[424,128]{1,0:T(8,128)S(1)}, f32[424,128]{1,0:T(8,128)S(1)}, u32[]{:S(2)}, u32[]{:S(2)}) collective-permute-start(f32[424,128]{1,0:T(8,128)S(1)} %get-tuple-element.54.refs_0_), channel_id=1, source_target_pairs={{1,2},{2,1},{5,6},{6,5},{9,10},{10,9},{13,14},{14,13},{17,18},{18,... | collective-permute-start | bytes 651272 | tf_op jit(solution)/shard_map/ppermute | solution.py:634
  27.5 3.1 %collective-permute-start.4 = (f32[168,128]{1,0:T(8,128)S(1)}, f32[168,128]{1,0:T(8,128)S(1)}, u32[]{:S(2)}, u32[]{:S(2)}) collective-permute-start(f32[168,128]{1,0:T(8,128)S(1)} %get-tuple-element.50), channel_id=1, source_target_pairs={{0,16},{1,18},{2,17},{3,19},{4,20},{5,22},{6,21},{7,23},{8,24},{9,... | collective-permute-start | bytes 258056 | tf_op jit(solution)/shard_map/ppermute | solution.py:634
  30.6 0.0 collective-permute-done.6.first
  30.6 2.3 %collective-permute-done.7.second = f32[544,128]{1,0:T(8,128)S(1)} collective-permute-done((f32[544,128]{1,0:T(8,128)S(1)}, f32[544,128]{1,0:T(8,128)S(1)}, u32[]{:S(2)}, u32[]{:S(2)}) %collective-permute-start.7) | collective-permute-done | bytes 278560 | tf_op jit(solution)/shard_map/ppermute | solution.py:574
  32.9 2.3 %shard_map.68 = f32[60,4,2048]{2,1,0:T(4,128)} custom-call(s32[1,2]{1,0:T(1,128)S(1)} %copy-done.1, bf16[192,256]{1,0:T(8,128)(2,1)S(1)} %get-tuple-element.45.factors, f32[4,48,1024]{2,1,0:T(8,128)S(1)} %collective-permute-done.6.first, f32[544,128]{1,0:T(8,128)S(1)} %collective-permute-done.7.second, ...), custom_call_target="tpu_custom_call", output_to_operand_aliasing={{}: (4, {})} | custom-call | flops 20000000 | bytes 200000 | tf_op jit(solution)/shard_map/pallas_call | solution.py:364
  35.2 0.0 collective-permute-done.4.refs_1_
  35.2 0.0 collective-permute-done.5.refs_2_
  35.2 0.1 shard_map.69
  35.3 1.0 %collective-permute-start.8 = (f32[288,128]{1,0:T(8,128)S(1)}, f32[288,128]{1,0:T(8,128)S(1)}, u32[]{:S(2)}, u32[]{:S(2)}) collective-permute-start(f32[288,128]{1,0:T(8,128)S(1)} %get-tuple-element.60), channel_id=1, source_target_pairs={{0,2},{2,0},{4,6},{6,4},{8,10},{10,8},{12,14},{14,12},{16,18},{18,... | collective-permute-start | bytes 442376 | tf_op jit(solution)/shard_map/ppermute | solution.py:574
  36.3 0.1 shard_map.70
  36.4 0.9 %collective-permute-done.8.other = f32[288,128]{1,0:T(8,128)S(1)} collective-permute-done((f32[288,128]{1,0:T(8,128)S(1)}, f32[288,128]{1,0:T(8,128)S(1)}, u32[]{:S(2)}, u32[]{:S(2)}) %collective-permute-start.8) | collective-permute-done | bytes 147488 | tf_op jit(solution)/shard_map/ppermute | solution.py:574
  37.3 0.8 %shard_map.71 = (f32[4,4,2048]{2,1,0:T(4,128)}, f32[5,4,2048]{2,1,0:T(4,128)}) custom-call(f32[4,4,1024]{2,1,0:T(4,128)S(1)} %get-tuple-element.58.own_tree, f32[5,4,1024]{2,1,0:T(4,128)S(1)} %get-tuple-element.59.own_final, f32[288,128]{1,0:T(8,128)S(1)} %collective-permute-done.8.other), custom_call_target="tpu_custom_call" | custom-call | tf_op jit(solution)/shard_map/pallas_call | solution.py:563
Async XLA Ops:
  0.6 1.9 %copy-start.1 = (s32[1,2]{1,0:T(1,128)S(1)}, s32[1,2]{1,0:T(1,128)}, u32[]{:S(2)}) copy-start(s32[1,2]{1,0:T(1,128)} %edges.9) | copy-start | bytes 28
  0.6 5.0 %copy-start = (f32[4,96,2048]{2,1,0:T(8,128)S(1)}, f32[4,96,2048]{2,1,0:T(8,128)}, u32[]{:S(2)}) copy-start(f32[4,96,2048]{2,1,0:T(8,128)} %field.5) | copy-start | bytes 9437188
  3.2 4.9 %copy-start.2 = (f32[64]{0:T(128)S(1)}, f32[64]{0:T(128)}, u32[]{:S(2)}) copy-start(f32[64]{0:T(128)} %param.5) | copy-start | bytes 772
  3.2 7.8 %collective-permute-start = (f32[4,16,2048]{2,1,0:T(8,128)S(1)}, f32[4,16,2048]{2,1,0:T(8,128)S(1)}, u32[]{:S(2)}, u32[]{:S(2)}) collective-permute-start(f32[4,16,2048]{2,1,0:T(8,128)S(1)} %shard_map.59), channel_id=1, source_target_pairs={{0,2},{2,4},{4,6},{6,8},{8,10},{10,12},{12,14},{14,16},{16,18},{18... | collective-permute-start | bytes 1572872 | tf_op jit(solution)/shard_map/ppermute | solution.py:579
  5.7 24.9 %collective-permute-start.6 = (f32[4,48,1024]{2,1,0:T(8,128)S(1)}, f32[4,48,1024]{2,1,0:T(8,128)S(1)}, u32[]{:S(2)}, u32[]{:S(2)}) collective-permute-start(f32[4,48,1024]{2,1,0:T(8,128)S(1)} %shard_map.67), channel_id=1, source_target_pairs={{0,1},{1,0},{2,3},{3,2},{4,5},{5,4},{6,7},{7,6},{8,9},{9,8},{10,11... | collective-permute-start | bytes 2359304 | tf_op jit(solution)/shard_map/ppermute | solution.py:574
  11.5 4.2 %collective-permute-start.1 = (f32[168,128]{1,0:T(8,128)S(1)}, f32[168,128]{1,0:T(8,128)S(1)}, u32[]{:S(2)}, u32[]{:S(2)}) collective-permute-start(f32[168,128]{1,0:T(8,128)S(1)} %get-tuple-element.40), channel_id=1, source_target_pairs={{0,2},{2,0},{4,6},{6,4},{8,10},{10,8},{12,14},{14,12},{16,18},{18,... | collective-permute-start | bytes 258056 | tf_op jit(solution)/shard_map/ppermute | solution.py:574
  15.8 5.9 %collective-permute-start.2 = (f32[168,128]{1,0:T(8,128)S(1)}, f32[168,128]{1,0:T(8,128)S(1)}, u32[]{:S(2)}, u32[]{:S(2)}) collective-permute-start(f32[168,128]{1,0:T(8,128)S(1)} %get-tuple-element.42), channel_id=1, source_target_pairs={{0,4},{2,6},{4,0},{6,2},{8,12},{10,14},{12,8},{14,10},{16,20},{18,... | collective-permute-start | bytes 258056 | tf_op jit(solution)/shard_map/ppermute | solution.py:574
  21.7 5.0 %collective-permute-start.3 = (f32[168,128]{1,0:T(8,128)S(1)}, f32[168,128]{1,0:T(8,128)S(1)}, u32[]{:S(2)}, u32[]{:S(2)}) collective-permute-start(f32[168,128]{1,0:T(8,128)S(1)} %get-tuple-element.48), channel_id=1, source_target_pairs={{0,8},{2,10},{4,12},{6,14},{8,0},{10,2},{12,4},{14,6},{16,24},{18,... | collective-permute-start | bytes 258056 | tf_op jit(solution)/shard_map/ppermute | solution.py:574
  24.3 8.6 %collective-permute-start.7 = (f32[544,128]{1,0:T(8,128)S(1)}, f32[544,128]{1,0:T(8,128)S(1)}, u32[]{:S(2)}, u32[]{:S(2)}) collective-permute-start(f32[544,128]{1,0:T(8,128)S(1)} %shard_map.64), channel_id=1, source_target_pairs={{0,1},{1,0},{2,3},{3,2},{4,5},{5,4},{6,7},{7,6},{8,9},{9,8},{10,11... | collective-permute-start | bytes 835592 | tf_op jit(solution)/shard_map/ppermute | solution.py:574
  26.8 8.4 %collective-permute-start.5 = (f32[424,128]{1,0:T(8,128)S(1)}, f32[424,128]{1,0:T(8,128)S(1)}, u32[]{:S(2)}, u32[]{:S(2)}) collective-permute-start(f32[424,128]{1,0:T(8,128)S(1)} %get-tuple-element.54.refs_0_), channel_id=1, source_target_pairs={{1,2},{2,1},{5,6},{6,5},{9,10},{10,9},{13,14},{14,13},{17,18},{18,... | collective-permute-start | bytes 651272 | tf_op jit(solution)/shard_map/ppermute | solution.py:634
  27.5 7.7 %collective-permute-start.4 = (f32[168,128]{1,0:T(8,128)S(1)}, f32[168,128]{1,0:T(8,128)S(1)}, u32[]{:S(2)}, u32[]{:S(2)}) collective-permute-start(f32[168,128]{1,0:T(8,128)S(1)} %get-tuple-element.50), channel_id=1, source_target_pairs={{0,16},{1,18},{2,17},{3,19},{4,20},{5,22},{6,21},{7,23},{8,24},{9,... | collective-permute-start | bytes 258056 | tf_op jit(solution)/shard_map/ppermute | solution.py:634
  35.3 2.0 %collective-permute-start.8 = (f32[288,128]{1,0:T(8,128)S(1)}, f32[288,128]{1,0:T(8,128)S(1)}, u32[]{:S(2)}, u32[]{:S(2)}) collective-permute-start(f32[288,128]{1,0:T(8,128)S(1)} %get-tuple-element.60), channel_id=1, source_target_pairs={{0,2},{2,0},{4,6},{6,4},{8,10},{10,8},{12,14},{14,12},{16,18},{18,... | collective-permute-start | bytes 442376 | tf_op jit(solution)/shard_map/ppermute | solution.py:574

commit v8 on v7

--- a/solution.py
+++ b/solution.py
@@ -53,7 +53,7 @@
         jax.ShapeDtypeStruct((species, HALO, lines), F32),
         in_specs=[SMEM_SPEC, VMEM_SPEC],
         out_specs=VMEM_SPEC,
-    )(edges, field[:, LOW : LOW + TILE])
+    )(edges, field[:, LOW : LOW + TILE - SUB])
 
 
 def first_kernel(field, away):

time: 38.6 us -> 38.5 us (level)
  no operation moved by 1% of the time
where the time goes in v8:
time: 38.5 us; the launch traced here: 38 us
  starting transfers between devices  19.8 us (51%)
  Pallas kernels  10.5 us (27%)
  waiting for transfers between devices  5.12 us (13%)
  local copies, waits for them, and re-layouts  1.91 us (5%)
  between operations  0.76 us (2%)
    ppermute x6, starting transfers between devices, from_partner(): return lax.ppermute(block, axis, [(i, i ^ step) for i in range(count)])  13.6 us
    ppermute x6, waiting for transfers between devices, from_partner(): return lax.ppermute(block, axis, [(i, i ^ step) for i in range(count)])  5.11 us
    pallas_call x2, Pallas kernels, details(): call(functools.partial(detail_kernel, local, width == lines), jax.ShapeDt...  4.67 us
    ppermute x1, starting transfers between devices, on_device(): lax.ppermute(send, both, partner_route)  3.09 us
    ppermute x1, starting transfers between devices, shifted(): return lax.ppermute(block, axis, [(i, i + 1) for i in range(count - 1)])  2.39 us
    pallas_call x1, Pallas kernels, brick_part(): call(brick_kernel, jax.ShapeDtypeStruct((dense, LANES), F32), grid=(speci...  1.87 us
    slice x1, local copies, waits for them, and re-layouts, brick_tail(): field[:, LOW:LOW + TILE - SUB]  1.83 us
    pallas_call x1, Pallas kernels, tile_matrix(): call(matrix_kernel, (jax.ShapeDtypeStruct((3 * TILE, 2 * LANES), BF16), j...  0.98 us
  transfers between devices with their start and end apart: 9, of which 4 were waited for; matrix products, arithmetic and copies ran while one was open for 0% of the time, Pallas kernels for 24%

profile of v8, /device:TPU:0, one launch (start us, length us, event | category | flops | bytes accessed | tf_op | source)
XLA Modules:
  0.0 38.0 jit_solution(12608923611483237629)
XLA Ops:
  0.6 0.0 copy-start.1
  0.6 0.0 copy-start
  0.6 1.8 %slice.3.rows = f32[4,56,2048]{2,1,0:T(8,128)S(1)} slice(f32[4,96,2048]{2,1,0:T(8,128)} %field.5), slice={[0:4], [32:88], [0:2048]} | slice | bytes 3670016 | tf_op jit(solution)/shard_map/slice | solution.py:56
  2.5 0.0 copy-done.1
  2.5 0.7 %shard_map.59 = f32[4,16,2048]{2,1,0:T(8,128)S(1)} custom-call(s32[1,2]{1,0:T(1,128)S(1)} %copy-done.1, f32[4,56,2048]{2,1,0:T(8,128)S(1)} %slice.3.rows), custom_call_target="tpu_custom_call" | custom-call | tf_op jit(solution)/shard_map/pallas_call | solution.py:51
  3.2 0.0 copy-start.2
  3.2 2.4 %collective-permute-start = (f32[4,16,2048]{2,1,0:T(8,128)S(1)}, f32[4,16,2048]{2,1,0:T(8,128)S(1)}, u32[]{:S(2)}, u32[]{:S(2)}) collective-permute-start(f32[4,16,2048]{2,1,0:T(8,128)S(1)} %shard_map.59), channel_id=1, source_target_pairs={{0,2},{2,4},{4,6},{6,8},{8,10},{10,12},{12,14},{14,16},{16,18},{18... | collective-permute-start | bytes 1572872 | tf_op jit(solution)/shard_map/ppermute | solution.py:579
  5.6 0.0 copy-done
  5.6 0.1 shard_map.67
  5.7 2.4 %collective-permute-start.6 = (f32[4,48,1024]{2,1,0:T(8,128)S(1)}, f32[4,48,1024]{2,1,0:T(8,128)S(1)}, u32[]{:S(2)}, u32[]{:S(2)}) collective-permute-start(f32[4,48,1024]{2,1,0:T(8,128)S(1)} %shard_map.67), channel_id=1, source_target_pairs={{0,1},{1,0},{2,3},{3,2},{4,5},{5,4},{6,7},{7,6},{8,9},{9,8},{10,11... | collective-permute-start | bytes 2359304 | tf_op jit(solution)/shard_map/ppermute | solution.py:574
  8.1 0.0 copy-done.2
  8.1 0.1 broadcast_in_dim.2.widths
  8.1 1.0 %shard_map.58 = (bf16[192,256]{1,0:T(8,128)(2,1)S(1)}, f32[8,128]{1,0:T(8,128)S(1)}, f32[8,128]{1,0:T(8,128)S(1)}) custom-call(s32[1,2]{1,0:T(1,128)S(1)} %copy-done.1, f32[64,128]{1,0:T(8,128)S(1)} %broadcast_in_dim.2.widths), custom_call_target="tpu_custom_call" | custom-call | tf_op jit(solution)/shard_map/pallas_call | solution.py:166
  9.1 1.9 %shard_map.60.part = f32[328,128]{1,0:T(8,128)S(1)} custom-call(f32[8,128]{1,0:T(8,128)S(1)} %get-tuple-element.33.weights, f32[8,128]{1,0:T(8,128)S(1)} %get-tuple-element.34.coarse_width, f32[4,96,2048]{2,1,0:T(8,128)S(1)} %copy-done), custom_call_target="tpu_custom_call" | custom-call | tf_op jit(solution)/shard_map/pallas_call | solution.py:217
  11.0 0.0 collective-permute-done.halo.first
  11.0 0.4 %shard_map.61 = (f32[168,128]{1,0:T(8,128)S(1)}, f32[168,128]{1,0:T(8,128)S(1)}) custom-call(f32[8,128]{1,0:T(8,128)S(1)} %get-tuple-element.33.weights, f32[4,16,2048]{2,1,0:T(8,128)S(1)} %collective-permute-done.halo.first, f32[328,128]{1,0:T(8,128)S(1)} %shard_map.60.part), custom_call_target="tpu_custom_call" | custom-call | tf_op jit(solution)/shard_map/pallas_call | solution.py:263
  11.4 3.3 %collective-permute-start.1 = (f32[168,128]{1,0:T(8,128)S(1)}, f32[168,128]{1,0:T(8,128)S(1)}, u32[]{:S(2)}, u32[]{:S(2)}) collective-permute-start(f32[168,128]{1,0:T(8,128)S(1)} %get-tuple-element.40), channel_id=1, source_target_pairs={{0,2},{2,0},{4,6},{6,4},{8,10},{10,8},{12,14},{14,12},{16,18},{18,... | collective-permute-start | bytes 258056 | tf_op jit(solution)/shard_map/ppermute | solution.py:574
  14.7 0.9 %collective-permute-done.1.refs_1_ = f32[168,128]{1,0:T(8,128)S(1)} collective-permute-done((f32[168,128]{1,0:T(8,128)S(1)}, f32[168,128]{1,0:T(8,128)S(1)}, u32[]{:S(2)}, u32[]{:S(2)}) %collective-permute-start.1) | collective-permute-done | bytes 86048 | tf_op jit(solution)/shard_map/ppermute | solution.py:574
  15.6 0.1 shard_map.62
  15.7 2.8 %collective-permute-start.2 = (f32[168,128]{1,0:T(8,128)S(1)}, f32[168,128]{1,0:T(8,128)S(1)}, u32[]{:S(2)}, u32[]{:S(2)}) collective-permute-start(f32[168,128]{1,0:T(8,128)S(1)} %get-tuple-element.42), channel_id=1, source_target_pairs={{0,4},{2,6},{4,0},{6,2},{8,12},{10,14},{12,8},{14,10},{16,20},{18,... | collective-permute-start | bytes 258056 | tf_op jit(solution)/shard_map/ppermute | solution.py:574
  18.5 0.7 %shard_map.64 = f32[544,128]{1,0:T(8,128)S(1)} custom-call(s32[1,2]{1,0:T(1,128)S(1)} %copy-done.1, f32[4,16,2048]{2,1,0:T(8,128)S(1)} %collective-permute-done.halo.first, f32[4,96,2048]{2,1,0:T(8,128)S(1)} %copy-done), custom_call_target="tpu_custom_call" | custom-call | flops 20000000 | bytes 200000 | tf_op jit(solution)/shard_map/pallas_call | solution.py:302
  19.2 2.4 %shard_map.65.rest_0_ = f32[60,4,2048]{2,1,0:T(4,128)} custom-call(s32[1,2]{1,0:T(1,128)S(1)} %copy-done.1, bf16[192,256]{1,0:T(8,128)(2,1)S(1)} %get-tuple-element.45.factors, f32[4,16,2048]{2,1,0:T(8,128)S(1)} %collective-permute-done.halo.first, f32[4,96,2048]{2,1,0:T(8,128)S(1)} %copy-done), custom_call_target="tpu_custom_call" | custom-call | flops 20000000 | bytes 200000 | tf_op jit(solution)/shard_map/pallas_call | solution.py:364
  21.6 0.0 collective-permute-done.2.refs_1_
  21.6 0.1 shard_map.63
  21.7 2.6 %collective-permute-start.3 = (f32[168,128]{1,0:T(8,128)S(1)}, f32[168,128]{1,0:T(8,128)S(1)}, u32[]{:S(2)}, u32[]{:S(2)}) collective-permute-start(f32[168,128]{1,0:T(8,128)S(1)} %get-tuple-element.48), channel_id=1, source_target_pairs={{0,8},{2,10},{4,12},{6,14},{8,0},{10,2},{12,4},{14,6},{16,24},{18,... | collective-permute-start | bytes 258056 | tf_op jit(solution)/shard_map/ppermute | solution.py:574
  24.2 1.5 %collective-permute-start.7 = (f32[544,128]{1,0:T(8,128)S(1)}, f32[544,128]{1,0:T(8,128)S(1)}, u32[]{:S(2)}, u32[]{:S(2)}) collective-permute-start(f32[544,128]{1,0:T(8,128)S(1)} %shard_map.64), channel_id=1, source_target_pairs={{0,1},{1,0},{2,3},{3,2},{4,5},{5,4},{6,7},{7,6},{8,9},{9,8},{10,11... | collective-permute-start | bytes 835592 | tf_op jit(solution)/shard_map/ppermute | solution.py:574
  25.7 0.9 %collective-permute-done.3.refs_1_ = f32[168,128]{1,0:T(8,128)S(1)} collective-permute-done((f32[168,128]{1,0:T(8,128)S(1)}, f32[168,128]{1,0:T(8,128)S(1)}, u32[]{:S(2)}, u32[]{:S(2)}) %collective-permute-start.3) | collective-permute-done | bytes 86048 | tf_op jit(solution)/shard_map/ppermute | solution.py:574
  26.7 0.1 shard_map.66
  26.8 0.7 %collective-permute-start.5 = (f32[424,128]{1,0:T(8,128)S(1)}, f32[424,128]{1,0:T(8,128)S(1)}, u32[]{:S(2)}, u32[]{:S(2)}) collective-permute-start(f32[424,128]{1,0:T(8,128)S(1)} %get-tuple-element.54.refs_0_), channel_id=1, source_target_pairs={{1,2},{2,1},{5,6},{6,5},{9,10},{10,9},{13,14},{14,13},{17,18},{18,... | collective-permute-start | bytes 651272 | tf_op jit(solution)/shard_map/ppermute | solution.py:634
  27.5 3.1 %collective-permute-start.4 = (f32[168,128]{1,0:T(8,128)S(1)}, f32[168,128]{1,0:T(8,128)S(1)}, u32[]{:S(2)}, u32[]{:S(2)}) collective-permute-start(f32[168,128]{1,0:T(8,128)S(1)} %get-tuple-element.50), channel_id=1, source_target_pairs={{0,16},{1,18},{2,17},{3,19},{4,20},{5,22},{6,21},{7,23},{8,24},{9,... | collective-permute-start | bytes 258056 | tf_op jit(solution)/shard_map/ppermute | solution.py:634
  30.6 0.0 collective-permute-done.6.first
  30.6 2.3 %collective-permute-done.7.second = f32[544,128]{1,0:T(8,128)S(1)} collective-permute-done((f32[544,128]{1,0:T(8,128)S(1)}, f32[544,128]{1,0:T(8,128)S(1)}, u32[]{:S(2)}, u32[]{:S(2)}) %collective-permute-start.7) | collective-permute-done | bytes 278560 | tf_op jit(solution)/shard_map/ppermute | solution.py:574
  32.9 2.3 %shard_map.68 = f32[60,4,2048]{2,1,0:T(4,128)} custom-call(s32[1,2]{1,0:T(1,128)S(1)} %copy-done.1, bf16[192,256]{1,0:T(8,128)(2,1)S(1)} %get-tuple-element.45.factors, f32[4,48,1024]{2,1,0:T(8,128)S(1)} %collective-permute-done.6.first, f32[544,128]{1,0:T(8,128)S(1)} %collective-permute-done.7.second, ...), custom_call_target="tpu_custom_call", output_to_operand_aliasing={{}: (4, {})} | custom-call | flops 20000000 | bytes 200000 | tf_op jit(solution)/shard_map/pallas_call | solution.py:364
  35.1 0.0 collective-permute-done.4.refs_1_
  35.1 0.0 collective-permute-done.5.refs_2_
  35.1 0.1 shard_map.69
  35.2 1.0 %collective-permute-start.8 = (f32[288,128]{1,0:T(8,128)S(1)}, f32[288,128]{1,0:T(8,128)S(1)}, u32[]{:S(2)}, u32[]{:S(2)}) collective-permute-start(f32[288,128]{1,0:T(8,128)S(1)} %get-tuple-element.60), channel_id=1, source_target_pairs={{0,2},{2,0},{4,6},{6,4},{8,10},{10,8},{12,14},{14,12},{16,18},{18,... | collective-permute-start | bytes 442376 | tf_op jit(solution)/shard_map/ppermute | solution.py:574
  36.3 0.1 shard_map.70
  36.3 0.9 %collective-permute-done.8.other = f32[288,128]{1,0:T(8,128)S(1)} collective-permute-done((f32[288,128]{1,0:T(8,128)S(1)}, f32[288,128]{1,0:T(8,128)S(1)}, u32[]{:S(2)}, u32[]{:S(2)}) %collective-permute-start.8) | collective-permute-done | bytes 147488 | tf_op jit(solution)/shard_map/ppermute | solution.py:574
  37.3 0.8 %shard_map.71 = (f32[4,4,2048]{2,1,0:T(4,128)}, f32[5,4,2048]{2,1,0:T(4,128)}) custom-call(f32[4,4,1024]{2,1,0:T(4,128)S(1)} %get-tuple-element.58.own_tree, f32[5,4,1024]{2,1,0:T(4,128)S(1)} %get-tuple-element.59.own_final, f32[288,128]{1,0:T(8,128)S(1)} %collective-permute-done.8.other), custom_call_target="tpu_custom_call" | custom-call | tf_op jit(solution)/shard_map/pallas_call | solution.py:563
Async XLA Ops:
  0.6 1.9 %copy-start.1 = (s32[1,2]{1,0:T(1,128)S(1)}, s32[1,2]{1,0:T(1,128)}, u32[]{:S(2)}) copy-start(s32[1,2]{1,0:T(1,128)} %edges.9) | copy-start | bytes 28
  0.6 4.9 %copy-start = (f32[4,96,2048]{2,1,0:T(8,128)S(1)}, f32[4,96,2048]{2,1,0:T(8,128)}, u32[]{:S(2)}) copy-start(f32[4,96,2048]{2,1,0:T(8,128)} %field.5) | copy-start | bytes 9437188
  3.2 4.9 %copy-start.2 = (f32[64]{0:T(128)S(1)}, f32[64]{0:T(128)}, u32[]{:S(2)}) copy-start(f32[64]{0:T(128)} %param.5) | copy-start | bytes 772
  3.2 7.8 %collective-permute-start = (f32[4,16,2048]{2,1,0:T(8,128)S(1)}, f32[4,16,2048]{2,1,0:T(8,128)S(1)}, u32[]{:S(2)}, u32[]{:S(2)}) collective-permute-start(f32[4,16,2048]{2,1,0:T(8,128)S(1)} %shard_map.59), channel_id=1, source_target_pairs={{0,2},{2,4},{4,6},{6,8},{8,10},{10,12},{12,14},{14,16},{16,18},{18... | collective-permute-start | bytes 1572872 | tf_op jit(solution)/shard_map/ppermute | solution.py:579
  5.7 24.9 %collective-permute-start.6 = (f32[4,48,1024]{2,1,0:T(8,128)S(1)}, f32[4,48,1024]{2,1,0:T(8,128)S(1)}, u32[]{:S(2)}, u32[]{:S(2)}) collective-permute-start(f32[4,48,1024]{2,1,0:T(8,128)S(1)} %shard_map.67), channel_id=1, source_target_pairs={{0,1},{1,0},{2,3},{3,2},{4,5},{5,4},{6,7},{7,6},{8,9},{9,8},{10,11... | collective-permute-start | bytes 2359304 | tf_op jit(solution)/shard_map/ppermute | solution.py:574
  11.4 4.2 %collective-permute-start.1 = (f32[168,128]{1,0:T(8,128)S(1)}, f32[168,128]{1,0:T(8,128)S(1)}, u32[]{:S(2)}, u32[]{:S(2)}) collective-permute-start(f32[168,128]{1,0:T(8,128)S(1)} %get-tuple-element.40), channel_id=1, source_target_pairs={{0,2},{2,0},{4,6},{6,4},{8,10},{10,8},{12,14},{14,12},{16,18},{18,... | collective-permute-start | bytes 258056 | tf_op jit(solution)/shard_map/ppermute | solution.py:574
  15.7 5.9 %collective-permute-start.2 = (f32[168,128]{1,0:T(8,128)S(1)}, f32[168,128]{1,0:T(8,128)S(1)}, u32[]{:S(2)}, u32[]{:S(2)}) collective-permute-start(f32[168,128]{1,0:T(8,128)S(1)} %get-tuple-element.42), channel_id=1, source_target_pairs={{0,4},{2,6},{4,0},{6,2},{8,12},{10,14},{12,8},{14,10},{16,20},{18,... | collective-permute-start | bytes 258056 | tf_op jit(solution)/shard_map/ppermute | solution.py:574
  21.7 5.0 %collective-permute-start.3 = (f32[168,128]{1,0:T(8,128)S(1)}, f32[168,128]{1,0:T(8,128)S(1)}, u32[]{:S(2)}, u32[]{:S(2)}) collective-permute-start(f32[168,128]{1,0:T(8,128)S(1)} %get-tuple-element.48), channel_id=1, source_target_pairs={{0,8},{2,10},{4,12},{6,14},{8,0},{10,2},{12,4},{14,6},{16,24},{18,... | collective-permute-start | bytes 258056 | tf_op jit(solution)/shard_map/ppermute | solution.py:574
  24.2 8.6 %collective-permute-start.7 = (f32[544,128]{1,0:T(8,128)S(1)}, f32[544,128]{1,0:T(8,128)S(1)}, u32[]{:S(2)}, u32[]{:S(2)}) collective-permute-start(f32[544,128]{1,0:T(8,128)S(1)} %shard_map.64), channel_id=1, source_target_pairs={{0,1},{1,0},{2,3},{3,2},{4,5},{5,4},{6,7},{7,6},{8,9},{9,8},{10,11... | collective-permute-start | bytes 835592 | tf_op jit(solution)/shard_map/ppermute | solution.py:574
  26.8 8.4 %collective-permute-start.5 = (f32[424,128]{1,0:T(8,128)S(1)}, f32[424,128]{1,0:T(8,128)S(1)}, u32[]{:S(2)}, u32[]{:S(2)}) collective-permute-start(f32[424,128]{1,0:T(8,128)S(1)} %get-tuple-element.54.refs_0_), channel_id=1, source_target_pairs={{1,2},{2,1},{5,6},{6,5},{9,10},{10,9},{13,14},{14,13},{17,18},{18,... | collective-permute-start | bytes 651272 | tf_op jit(solution)/shard_map/ppermute | solution.py:634
  27.5 7.7 %collective-permute-start.4 = (f32[168,128]{1,0:T(8,128)S(1)}, f32[168,128]{1,0:T(8,128)S(1)}, u32[]{:S(2)}, u32[]{:S(2)}) collective-permute-start(f32[168,128]{1,0:T(8,128)S(1)} %get-tuple-element.50), channel_id=1, source_target_pairs={{0,16},{1,18},{2,17},{3,19},{4,20},{5,22},{6,21},{7,23},{8,24},{9,... | collective-permute-start | bytes 258056 | tf_op jit(solution)/shard_map/ppermute | solution.py:634
  35.2 2.0 %collective-permute-start.8 = (f32[288,128]{1,0:T(8,128)S(1)}, f32[288,128]{1,0:T(8,128)S(1)}, u32[]{:S(2)}, u32[]{:S(2)}) collective-permute-start(f32[288,128]{1,0:T(8,128)S(1)} %get-tuple-element.60), channel_id=1, source_target_pairs={{0,2},{2,0},{4,6},{6,4},{8,10},{10,8},{12,14},{14,12},{16,18},{18,... | collective-permute-start | bytes 442376 | tf_op jit(solution)/shard_map/ppermute | solution.py:574

commit v9 on v8

--- a/solution.py
+++ b/solution.py
@@ -619,7 +619,8 @@
     halo, other_half = lax.optimization_barrier((halo, other_half))
     if swapped:
         rest = rest_away(brick_edges, halo, field, width)
-        halo, rest = lax.optimization_barrier((halo, rest))
+        first_other = from_partner(other_half, "slab", 1)
+        first_other, halo, rest = lax.optimization_barrier((first_other, halo, rest))
         rest_in = from_partner(rest, "cross", 1)
 
     if swapped:
@@ -635,7 +636,8 @@
             tile_detail = details(False, brick_edges, factors, first_in, rest_in, width, species, lines, near)
             operands, tile_detail = lax.optimization_barrier((operands, tile_detail))
         else:
-            operands = (carried, from_partner(send, "slab", 1 << level))
+            other = first_other if swapped and level == 0 else from_partner(send, "slab", 1 << level)
+            operands = (carried, other)
         send, carried = merge(level, depth, rows, swapped, *operands)
     here_set, away_set = send, carried
     partner_set = from_partner(away_set, "slab", 1)

time: 38.5 us -> 38.5 us (level)
  transfers between devices with their start and end apart: 9 -> 9, of which waited for: 4 -> 5; matrix products, arithmetic and copies ran while one was open for 0% -> 0% of each run, Pallas kernels for 24% -> 23%
where the time goes in v9:
time: 38.5 us; the launch traced here: 38 us
  starting transfers between devices  20 us (52%)
  Pallas kernels  10.4 us (27%)
  waiting for transfers between devices  4.92 us (13%)
  local copies, waits for them, and re-layouts  1.91 us (5%)
  between operations  0.76 us (2%)
    ppermute x6, starting transfers between devices, from_partner(): return lax.ppermute(block, axis, [(i, i ^ step) for i in range(count)])  13.8 us
    ppermute x6, waiting for transfers between devices, from_partner(): return lax.ppermute(block, axis, [(i, i ^ step) for i in range(count)])  4.91 us
    pallas_call x2, Pallas kernels, details(): call(functools.partial(detail_kernel, local, width == lines), jax.ShapeDt...  4.64 us
    ppermute x1, starting transfers between devices, on_device(): lax.ppermute(send, both, partner_route)  3.09 us
    ppermute x1, starting transfers between devices, shifted(): return lax.ppermute(block, axis, [(i, i + 1) for i in range(count - 1)])  2.39 us
    pallas_call x1, Pallas kernels, brick_part(): call(brick_kernel, jax.ShapeDtypeStruct((dense, LANES), F32), grid=(speci...  1.87 us
    slice x1, local copies, waits for them, and re-layouts, brick_tail(): field[:, LOW:LOW + TILE - SUB]  1.83 us
    pallas_call x1, Pallas kernels, tile_matrix(): call(matrix_kernel, (jax.ShapeDtypeStruct((3 * TILE, 2 * LANES), BF16), j...  0.98 us
  transfers between devices with their start and end apart: 9, of which 5 were waited for; matrix products, arithmetic and copies ran while one was open for 0% of the time, Pallas kernels for 23%

profile of v9, /device:TPU:0, one launch (start us, length us, event | category | flops | bytes accessed | tf_op | source)
XLA Modules:
  0.0 38.0 jit_solution(14947459850269008690)
XLA Ops:
  0.6 0.0 copy-start.1
  0.6 0.0 copy-start
  0.6 1.8 %slice.3.rows = f32[4,56,2048]{2,1,0:T(8,128)S(1)} slice(f32[4,96,2048]{2,1,0:T(8,128)} %field.5), slice={[0:4], [32:88], [0:2048]} | slice | bytes 3670016 | tf_op jit(solution)/shard_map/slice | solution.py:56
  2.5 0.0 copy-done.1
  2.5 0.7 %shard_map.59 = f32[4,16,2048]{2,1,0:T(8,128)S(1)} custom-call(s32[1,2]{1,0:T(1,128)S(1)} %copy-done.1, f32[4,56,2048]{2,1,0:T(8,128)S(1)} %slice.3.rows), custom_call_target="tpu_custom_call" | custom-call | tf_op jit(solution)/shard_map/pallas_call | solution.py:51
  3.2 0.0 copy-start.2
  3.2 2.4 %collective-permute-start = (f32[4,16,2048]{2,1,0:T(8,128)S(1)}, f32[4,16,2048]{2,1,0:T(8,128)S(1)}, u32[]{:S(2)}, u32[]{:S(2)}) collective-permute-start(f32[4,16,2048]{2,1,0:T(8,128)S(1)} %shard_map.59), channel_id=1, source_target_pairs={{0,2},{2,4},{4,6},{6,8},{8,10},{10,12},{12,14},{14,16},{16,18},{18... | collective-permute-start | bytes 1572872 | tf_op jit(solution)/shard_map/ppermute | solution.py:579
  5.6 0.0 copy-done
  5.6 0.1 shard_map.67
  5.7 2.4 %collective-permute-start.6 = (f32[4,48,1024]{2,1,0:T(8,128)S(1)}, f32[4,48,1024]{2,1,0:T(8,128)S(1)}, u32[]{:S(2)}, u32[]{:S(2)}) collective-permute-start(f32[4,48,1024]{2,1,0:T(8,128)S(1)} %shard_map.67), channel_id=1, source_target_pairs={{0,1},{1,0},{2,3},{3,2},{4,5},{5,4},{6,7},{7,6},{8,9},{9,8},{10,11... | collective-permute-start | bytes 2359304 | tf_op jit(solution)/shard_map/ppermute | solution.py:574
  8.1 0.0 copy-done.2
  8.1 0.1 broadcast_in_dim.2.widths
  8.1 1.0 %shard_map.58 = (bf16[192,256]{1,0:T(8,128)(2,1)S(1)}, f32[8,128]{1,0:T(8,128)S(1)}, f32[8,128]{1,0:T(8,128)S(1)}) custom-call(s32[1,2]{1,0:T(1,128)S(1)} %copy-done.1, f32[64,128]{1,0:T(8,128)S(1)} %broadcast_in_dim.2.widths), custom_call_target="tpu_custom_call" | custom-call | tf_op jit(solution)/shard_map/pallas_call | solution.py:166
  9.1 1.9 %shard_map.60.part = f32[328,128]{1,0:T(8,128)S(1)} custom-call(f32[8,128]{1,0:T(8,128)S(1)} %get-tuple-element.34.weights, f32[8,128]{1,0:T(8,128)S(1)} %get-tuple-element.35.coarse_width, f32[4,96,2048]{2,1,0:T(8,128)S(1)} %copy-done), custom_call_target="tpu_custom_call" | custom-call | tf_op jit(solution)/shard_map/pallas_call | solution.py:217
  11.0 0.0 collective-permute-done.halo.first
  11.0 0.4 %shard_map.61 = (f32[168,128]{1,0:T(8,128)S(1)}, f32[168,128]{1,0:T(8,128)S(1)}) custom-call(f32[8,128]{1,0:T(8,128)S(1)} %get-tuple-element.34.weights, f32[4,16,2048]{2,1,0:T(8,128)S(1)} %collective-permute-done.halo.first, f32[328,128]{1,0:T(8,128)S(1)} %shard_map.60.part), custom_call_target="tpu_custom_call" | custom-call | tf_op jit(solution)/shard_map/pallas_call | solution.py:263
  11.4 3.3 %collective-permute-start.1 = (f32[168,128]{1,0:T(8,128)S(1)}, f32[168,128]{1,0:T(8,128)S(1)}, u32[]{:S(2)}, u32[]{:S(2)}) collective-permute-start(f32[168,128]{1,0:T(8,128)S(1)} %get-tuple-element.41), channel_id=1, source_target_pairs={{0,2},{2,0},{4,6},{6,4},{8,10},{10,8},{12,14},{14,12},{16,18},{18,... | collective-permute-start | bytes 258056 | tf_op jit(solution)/shard_map/ppermute | solution.py:574
  14.7 0.7 %shard_map.62 = f32[544,128]{1,0:T(8,128)S(1)} custom-call(s32[1,2]{1,0:T(1,128)S(1)} %copy-done.1, f32[4,16,2048]{2,1,0:T(8,128)S(1)} %collective-permute-done.halo.first, f32[4,96,2048]{2,1,0:T(8,128)S(1)} %copy-done), custom_call_target="tpu_custom_call" | custom-call | flops 20000000 | bytes 200000 | tf_op jit(solution)/shard_map/pallas_call | solution.py:302
  15.4 0.3 collective-permute-done.1.refs_1_
  15.6 0.1 shard_map.63
  15.7 2.8 %collective-permute-start.2 = (f32[168,128]{1,0:T(8,128)S(1)}, f32[168,128]{1,0:T(8,128)S(1)}, u32[]{:S(2)}, u32[]{:S(2)}) collective-permute-start(f32[168,128]{1,0:T(8,128)S(1)} %get-tuple-element.45), channel_id=1, source_target_pairs={{0,4},{2,6},{4,0},{6,2},{8,12},{10,14},{12,8},{14,10},{16,20},{18,... | collective-permute-start | bytes 258056 | tf_op jit(solution)/shard_map/ppermute | solution.py:574
  18.5 2.4 %shard_map.65.rest_0_ = f32[60,4,2048]{2,1,0:T(4,128)} custom-call(s32[1,2]{1,0:T(1,128)S(1)} %copy-done.1, bf16[192,256]{1,0:T(8,128)(2,1)S(1)} %get-tuple-element.48.factors, f32[4,16,2048]{2,1,0:T(8,128)S(1)} %collective-permute-done.halo.first, f32[4,96,2048]{2,1,0:T(8,128)S(1)} %copy-done), custom_call_target="tpu_custom_call" | custom-call | flops 20000000 | bytes 200000 | tf_op jit(solution)/shard_map/pallas_call | solution.py:364
  20.9 0.5 %collective-permute-done.2.refs_1_ = f32[168,128]{1,0:T(8,128)S(1)} collective-permute-done((f32[168,128]{1,0:T(8,128)S(1)}, f32[168,128]{1,0:T(8,128)S(1)}, u32[]{:S(2)}, u32[]{:S(2)}) %collective-permute-start.2) | collective-permute-done | bytes 86048 | tf_op jit(solution)/shard_map/ppermute | solution.py:574
  21.4 0.1 shard_map.64
  21.4 2.8 %collective-permute-start.3 = (f32[168,128]{1,0:T(8,128)S(1)}, f32[168,128]{1,0:T(8,128)S(1)}, u32[]{:S(2)}, u32[]{:S(2)}) collective-permute-start(f32[168,128]{1,0:T(8,128)S(1)} %get-tuple-element.50), channel_id=1, source_target_pairs={{0,8},{2,10},{4,12},{6,14},{8,0},{10,2},{12,4},{14,6},{16,24},{18,... | collective-permute-start | bytes 258056 | tf_op jit(solution)/shard_map/ppermute | solution.py:574
  24.2 1.5 %collective-permute-start.7 = (f32[544,128]{1,0:T(8,128)S(1)}, f32[544,128]{1,0:T(8,128)S(1)}, u32[]{:S(2)}, u32[]{:S(2)}) collective-permute-start(f32[544,128]{1,0:T(8,128)S(1)} %shard_map.62), channel_id=1, source_target_pairs={{0,1},{1,0},{2,3},{3,2},{4,5},{5,4},{6,7},{7,6},{8,9},{9,8},{10,11... | collective-permute-start | bytes 835592 | tf_op jit(solution)/shard_map/ppermute | solution.py:574
  25.7 0.9 %collective-permute-done.3.refs_1_ = f32[168,128]{1,0:T(8,128)S(1)} collective-permute-done((f32[168,128]{1,0:T(8,128)S(1)}, f32[168,128]{1,0:T(8,128)S(1)}, u32[]{:S(2)}, u32[]{:S(2)}) %collective-permute-start.3) | collective-permute-done | bytes 86048 | tf_op jit(solution)/shard_map/ppermute | solution.py:574
  26.7 0.1 shard_map.66
  26.8 0.7 %collective-permute-start.5 = (f32[424,128]{1,0:T(8,128)S(1)}, f32[424,128]{1,0:T(8,128)S(1)}, u32[]{:S(2)}, u32[]{:S(2)}) collective-permute-start(f32[424,128]{1,0:T(8,128)S(1)} %get-tuple-element.56.refs_0_), channel_id=1, source_target_pairs={{1,2},{2,1},{5,6},{6,5},{9,10},{10,9},{13,14},{14,13},{17,18},{18,... | collective-permute-start | bytes 651272 | tf_op jit(solution)/shard_map/ppermute | solution.py:635
  27.5 3.1 %collective-permute-start.4 = (f32[168,128]{1,0:T(8,128)S(1)}, f32[168,128]{1,0:T(8,128)S(1)}, u32[]{:S(2)}, u32[]{:S(2)}) collective-permute-start(f32[168,128]{1,0:T(8,128)S(1)} %get-tuple-element.52), channel_id=1, source_target_pairs={{0,16},{1,18},{2,17},{3,19},{4,20},{5,22},{6,21},{7,23},{8,24},{9,... | collective-permute-start | bytes 258056 | tf_op jit(solution)/shard_map/ppermute | solution.py:635
  30.6 0.0 collective-permute-done.6.first
  30.6 2.3 %collective-permute-done.7.second = f32[544,128]{1,0:T(8,128)S(1)} collective-permute-done((f32[544,128]{1,0:T(8,128)S(1)}, f32[544,128]{1,0:T(8,128)S(1)}, u32[]{:S(2)}, u32[]{:S(2)}) %collective-permute-start.7) | collective-permute-done | bytes 278560 | tf_op jit(solution)/shard_map/ppermute | solution.py:574
  32.9 2.3 %shard_map.68 = f32[60,4,2048]{2,1,0:T(4,128)} custom-call(s32[1,2]{1,0:T(1,128)S(1)} %copy-done.1, bf16[192,256]{1,0:T(8,128)(2,1)S(1)} %get-tuple-element.48.factors, f32[4,48,1024]{2,1,0:T(8,128)S(1)} %collective-permute-done.6.first, f32[544,128]{1,0:T(8,128)S(1)} %collective-permute-done.7.second, ...), custom_call_target="tpu_custom_call", output_to_operand_aliasing={{}: (4, {})} | custom-call | flops 20000000 | bytes 200000 | tf_op jit(solution)/shard_map/pallas_call | solution.py:364
  35.1 0.0 collective-permute-done.4.refs_1_
  35.1 0.0 collective-permute-done.5.refs_2_
  35.1 0.1 shard_map.69
  35.2 1.0 %collective-permute-start.8 = (f32[288,128]{1,0:T(8,128)S(1)}, f32[288,128]{1,0:T(8,128)S(1)}, u32[]{:S(2)}, u32[]{:S(2)}) collective-permute-start(f32[288,128]{1,0:T(8,128)S(1)} %get-tuple-element.62), channel_id=1, source_target_pairs={{0,2},{2,0},{4,6},{6,4},{8,10},{10,8},{12,14},{14,12},{16,18},{18,... | collective-permute-start | bytes 442376 | tf_op jit(solution)/shard_map/ppermute | solution.py:574
  36.3 0.1 shard_map.70
  36.3 0.9 %collective-permute-done.8.other = f32[288,128]{1,0:T(8,128)S(1)} collective-permute-done((f32[288,128]{1,0:T(8,128)S(1)}, f32[288,128]{1,0:T(8,128)S(1)}, u32[]{:S(2)}, u32[]{:S(2)}) %collective-permute-start.8) | collective-permute-done | bytes 147488 | tf_op jit(solution)/shard_map/ppermute | solution.py:574
  37.3 0.8 %shard_map.71 = (f32[4,4,2048]{2,1,0:T(4,128)}, f32[5,4,2048]{2,1,0:T(4,128)}) custom-call(f32[4,4,1024]{2,1,0:T(4,128)S(1)} %get-tuple-element.60.own_tree, f32[5,4,1024]{2,1,0:T(4,128)S(1)} %get-tuple-element.61.own_final, f32[288,128]{1,0:T(8,128)S(1)} %collective-permute-done.8.other), custom_call_target="tpu_custom_call" | custom-call | tf_op jit(solution)/shard_map/pallas_call | solution.py:563
Async XLA Ops:
  0.6 1.9 %copy-start.1 = (s32[1,2]{1,0:T(1,128)S(1)}, s32[1,2]{1,0:T(1,128)}, u32[]{:S(2)}) copy-start(s32[1,2]{1,0:T(1,128)} %edges.9) | copy-start | bytes 28
  0.6 4.9 %copy-start = (f32[4,96,2048]{2,1,0:T(8,128)S(1)}, f32[4,96,2048]{2,1,0:T(8,128)}, u32[]{:S(2)}) copy-start(f32[4,96,2048]{2,1,0:T(8,128)} %field.5) | copy-start | bytes 9437188
  3.2 4.9 %copy-start.2 = (f32[64]{0:T(128)S(1)}, f32[64]{0:T(128)}, u32[]{:S(2)}) copy-start(f32[64]{0:T(128)} %param.5) | copy-start | bytes 772
  3.2 7.8 %collective-permute-start = (f32[4,16,2048]{2,1,0:T(8,128)S(1)}, f32[4,16,2048]{2,1,0:T(8,128)S(1)}, u32[]{:S(2)}, u32[]{:S(2)}) collective-permute-start(f32[4,16,2048]{2,1,0:T(8,128)S(1)} %shard_map.59), channel_id=1, source_target_pairs={{0,2},{2,4},{4,6},{6,8},{8,10},{10,12},{12,14},{14,16},{16,18},{18... | collective-permute-start | bytes 1572872 | tf_op jit(solution)/shard_map/ppermute | solution.py:579
  5.7 24.9 %collective-permute-start.6 = (f32[4,48,1024]{2,1,0:T(8,128)S(1)}, f32[4,48,1024]{2,1,0:T(8,128)S(1)}, u32[]{:S(2)}, u32[]{:S(2)}) collective-permute-start(f32[4,48,1024]{2,1,0:T(8,128)S(1)} %shard_map.67), channel_id=1, source_target_pairs={{0,1},{1,0},{2,3},{3,2},{4,5},{5,4},{6,7},{7,6},{8,9},{9,8},{10,11... | collective-permute-start | bytes 2359304 | tf_op jit(solution)/shard_map/ppermute | solution.py:574
  11.4 4.2 %collective-permute-start.1 = (f32[168,128]{1,0:T(8,128)S(1)}, f32[168,128]{1,0:T(8,128)S(1)}, u32[]{:S(2)}, u32[]{:S(2)}) collective-permute-start(f32[168,128]{1,0:T(8,128)S(1)} %get-tuple-element.41), channel_id=1, source_target_pairs={{0,2},{2,0},{4,6},{6,4},{8,10},{10,8},{12,14},{14,12},{16,18},{18,... | collective-permute-start | bytes 258056 | tf_op jit(solution)/shard_map/ppermute | solution.py:574
  15.7 5.6 %collective-permute-start.2 = (f32[168,128]{1,0:T(8,128)S(1)}, f32[168,128]{1,0:T(8,128)S(1)}, u32[]{:S(2)}, u32[]{:S(2)}) collective-permute-start(f32[168,128]{1,0:T(8,128)S(1)} %get-tuple-element.45), channel_id=1, source_target_pairs={{0,4},{2,6},{4,0},{6,2},{8,12},{10,14},{12,8},{14,10},{16,20},{18,... | collective-permute-start | bytes 258056 | tf_op jit(solution)/shard_map/ppermute | solution.py:574
  21.4 5.3 %collective-permute-start.3 = (f32[168,128]{1,0:T(8,128)S(1)}, f32[168,128]{1,0:T(8,128)S(1)}, u32[]{:S(2)}, u32[]{:S(2)}) collective-permute-start(f32[168,128]{1,0:T(8,128)S(1)} %get-tuple-element.50), channel_id=1, source_target_pairs={{0,8},{2,10},{4,12},{6,14},{8,0},{10,2},{12,4},{14,6},{16,24},{18,... | collective-permute-start | bytes 258056 | tf_op jit(solution)/shard_map/ppermute | solution.py:574
  24.2 8.6 %collective-permute-start.7 = (f32[544,128]{1,0:T(8,128)S(1)}, f32[544,128]{1,0:T(8,128)S(1)}, u32[]{:S(2)}, u32[]{:S(2)}) collective-permute-start(f32[544,128]{1,0:T(8,128)S(1)} %shard_map.62), channel_id=1, source_target_pairs={{0,1},{1,0},{2,3},{3,2},{4,5},{5,4},{6,7},{7,6},{8,9},{9,8},{10,11... | collective-permute-start | bytes 835592 | tf_op jit(solution)/shard_map/ppermute | solution.py:574
  26.8 8.4 %collective-permute-start.5 = (f32[424,128]{1,0:T(8,128)S(1)}, f32[424,128]{1,0:T(8,128)S(1)}, u32[]{:S(2)}, u32[]{:S(2)}) collective-permute-start(f32[424,128]{1,0:T(8,128)S(1)} %get-tuple-element.56.refs_0_), channel_id=1, source_target_pairs={{1,2},{2,1},{5,6},{6,5},{9,10},{10,9},{13,14},{14,13},{17,18},{18,... | collective-permute-start | bytes 651272 | tf_op jit(solution)/shard_map/ppermute | solution.py:635
  27.5 7.7 %collective-permute-start.4 = (f32[168,128]{1,0:T(8,128)S(1)}, f32[168,128]{1,0:T(8,128)S(1)}, u32[]{:S(2)}, u32[]{:S(2)}) collective-permute-start(f32[168,128]{1,0:T(8,128)S(1)} %get-tuple-element.52), channel_id=1, source_target_pairs={{0,16},{1,18},{2,17},{3,19},{4,20},{5,22},{6,21},{7,23},{8,24},{9,... | collective-permute-start | bytes 258056 | tf_op jit(solution)/shard_map/ppermute | solution.py:635
  35.2 2.0 %collective-permute-start.8 = (f32[288,128]{1,0:T(8,128)S(1)}, f32[288,128]{1,0:T(8,128)S(1)}, u32[]{:S(2)}, u32[]{:S(2)}) collective-permute-start(f32[288,128]{1,0:T(8,128)S(1)} %get-tuple-element.62), channel_id=1, source_target_pairs={{0,2},{2,0},{4,6},{6,4},{8,10},{10,8},{12,14},{14,12},{16,18},{18,... | collective-permute-start | bytes 442376 | tf_op jit(solution)/shard_map/ppermute | solution.py:574
